TPU v7x, 32 devices: a whole 2x2x4 slice. The times are simulated.
32 devices in a mesh: replica: 16 (over z, x, core), shard: 2 (over y).
Axes of the slice: x: 2, y: 2, z: 4, core: 2. Of those that a mesh axis runs over, the one named last changes fastest.
Arguments:
- inputs: bfloat16 [32768, 768], P(('replica', 'shard')), may hold values from -6 to 6
- segments: int32 [32, 1024], P(('replica', 'shard')), may hold values from 0 to 15, never falling along the last dimension, each value on 1 to 512 neighbouring positions
- w_qkv: bfloat16 [768, 2304], P('shard'), may hold values from -0.21875 to 0.21875
- b_qv: bfloat16 [1536], P('shard'), may hold values from -3 to 3
- w_out: bfloat16 [768, 768], P('shard'), may hold values from -0.875 to 0.875
- b_out: bfloat16 [768], P('shard'), may hold values from -3 to 3
- attn_gain: bfloat16 [768], P('shard'), may hold values from 0.5 to 1.5
- attn_shift: bfloat16 [768], P('shard'), may hold values from -3 to 3
- w_up: bfloat16 [768, 3072], P('shard'), may hold values from -0.21875 to 0.21875
- b_up: bfloat16 [3072], P('shard'), may hold values from -3 to 3
- w_down: bfloat16 [3072, 768], P('shard'), may hold values from -0.109375 to 0.109375
- b_down: bfloat16 [768], P('shard'), may hold values from -3 to 3
- ffn_gain: bfloat16 [768], P('shard'), may hold values from 0.5 to 1.5
- ffn_shift: bfloat16 [768], P('shard'), may hold values from -3 to 3
- cotangent: bfloat16 [32768, 768], P(('replica', 'shard')), may hold values from -6 to 6
Outputs:
- layer_output: bfloat16 [32768, 768], P(('replica', 'shard'))
- input_grad: bfloat16 [32768, 768], P(('replica', 'shard'))
- w_qkv_grad: float32 [768, 2304], P('shard')
- b_qv_grad: float32 [1536], P('shard')
- w_out_grad: float32 [768, 768], P('shard')
- b_out_grad: float32 [768], P('shard')
- attn_gain_grad: float32 [768], P('shard')
- attn_shift_grad: float32 [768], P('shard')
- w_up_grad: float32 [768, 3072], P('shard')
- b_up_grad: float32 [3072], P('shard')
- w_down_grad: float32 [3072, 768], P('shard')
- b_down_grad: float32 [768], P('shard')
- ffn_gain_grad: float32 [768], P('shard')
- ffn_shift_grad: float32 [768], P('shard')
Inputs may be any that keep to these rules, and one draw needn't show every extreme that they name: `segments`: within each sequence the document numbers never fall; each document has 1 to 512 tokens and one document of each sequence has exactly 512.
All inputs are finite; a program needn't handle non-finite values.
Results may differ from a plain program's by a relative error of at most 0.019.
Values may be sent and summed in bfloat16 or wider, within the bound.
No kernel may reach another device: no remote copies, remote signals or barrier semaphores. Data moves between devices by JAX's collectives and lax.ppermute only.
A program may use at most 192 MiB of HBM per device.

v0:
```python
import jax
import jax.numpy as jnp
from jax import lax
from jax.sharding import PartitionSpec as P

D = 768
HEADS = 12
HEAD_DIM = 64
LEN = 1024


EPSILON = 1e-12
MASKED_SCORE = -1000000000.0


def layer_norm(hidden, gain, shift):
    average = jnp.mean(hidden, axis=-1, keepdims=True)
    centered = hidden - average
    variance = jnp.mean(centered * centered, axis=-1, keepdims=True)
    return centered * lax.rsqrt(variance + EPSILON) * gain + shift


def gelu_exact(value):
    return jax.nn.gelu(value, approximate=False)


def matmul(left, right):
    return jnp.dot(left, right, preferred_element_type=jnp.float32)


def matmul_right_t(left, right):
    return lax.dot_general(
        left, right, (((1,), (1,)), ((), ())), preferred_element_type=jnp.float32
    )


def matmul_left_t(left, right):
    return lax.dot_general(
        left, right, (((0,), (0,)), ((), ())), preferred_element_type=jnp.float32
    )


def split_heads(matrix, seq_count):
    return matrix.reshape(seq_count, LEN, HEADS, HEAD_DIM).transpose(2, 0, 1, 3)


def join_heads(stacked, seq_count):
    return stacked.transpose(1, 2, 0, 3).reshape(seq_count * LEN, D)


def as_float(value):
    return value.astype(jnp.float32)


def local(
    inputs,
    segments,
    w_qkv,
    b_qv,
    w_out,
    b_out,
    attn_gain,
    attn_shift,
    w_up,
    b_up,
    w_down,
    b_down,
    ffn_gain,
    ffn_shift,
    cotangent,
):
    seq_count = segments.shape[0]
    scale = HEAD_DIM ** (-0.5)
    same_doc = segments[:, :, None] == segments[:, None, :]

    def head_scores(query_head, key_head):
        scores = (
            jnp.einsum("sqd,skd->sqk", query_head, key_head, preferred_element_type=jnp.float32)
            * scale
        )
        return jnp.where(same_doc, scores, MASKED_SCORE)

    def head_forward(operands):
        query_head, key_head, value_head = operands
        masked = head_scores(query_head, key_head)
        row_max = jnp.max(masked, axis=-1, keepdims=True)
        exp_terms = jnp.exp(masked - row_max)
        row_total = jnp.sum(exp_terms, axis=-1, keepdims=True)
        attn_probs = (exp_terms / row_total).astype(jnp.bfloat16)
        context_head = jnp.einsum(
            "sqk,skd->sqd", attn_probs, value_head, preferred_element_type=jnp.float32
        )
        return (context_head, (row_max + jnp.log(row_total))[..., 0])

    def head_backward(operands):
        query_head, key_head, value_head, grad_head, log_total = operands
        masked = head_scores(query_head, key_head)
        attn_float = jnp.exp(masked - log_total[..., None])
        attn_probs = attn_float.astype(jnp.bfloat16)
        grad_value = jnp.einsum(
            "sqk,sqd->skd", attn_probs, grad_head, preferred_element_type=jnp.float32
        )
        grad_probs = jnp.einsum(
            "sqd,skd->sqk", grad_head, value_head, preferred_element_type=jnp.float32
        )
        row_dot = jnp.sum(attn_float * grad_probs, axis=-1, keepdims=True)
        grad_scores = (attn_float * (grad_probs - row_dot)).astype(jnp.bfloat16)
        grad_query = (
            jnp.einsum("sqk,skd->sqd", grad_scores, key_head, preferred_element_type=jnp.float32)
            * scale
        )
        grad_key = (
            jnp.einsum("sqk,sqd->skd", grad_scores, query_head, preferred_element_type=jnp.float32)
            * scale
        )
        return (grad_query, grad_key, grad_value)

    full_qkv, full_bqv, full_wout, full_bout, full_again, full_ashift = (
        lax.all_gather(w_qkv, "shard", axis=0, tiled=True),
        lax.all_gather(b_qv, "shard", axis=0, tiled=True),
        lax.all_gather(w_out, "shard", axis=0, tiled=True),
        lax.all_gather(b_out, "shard", axis=0, tiled=True),
        lax.all_gather(attn_gain, "shard", axis=0, tiled=True),
        lax.all_gather(attn_shift, "shard", axis=0, tiled=True),
    )
    qkv_bias = as_float(
        jnp.concatenate([full_bqv[:D], jnp.zeros((D,), jnp.bfloat16), full_bqv[D:]])
    )
    projected = (matmul(inputs, full_qkv) + qkv_bias).astype(jnp.bfloat16)
    query_heads = split_heads(projected[:, :D], seq_count)
    key_heads = split_heads(projected[:, D : 2 * D], seq_count)
    value_heads = split_heads(projected[:, 2 * D :], seq_count)
    context_heads, log_totals = lax.map(head_forward, (query_heads, key_heads, value_heads))
    context = join_heads(context_heads, seq_count).astype(jnp.bfloat16)
    attended = matmul(context, full_wout) + as_float(full_bout)
    residual_one = as_float(inputs) + attended
    normed_one, norm_one_pull = jax.vjp(
        layer_norm, residual_one, as_float(full_again), as_float(full_ashift)
    )
    full_wup, full_bup, full_wdown, full_bdown, full_fgain, full_fshift = (
        lax.all_gather(w_up, "shard", axis=0, tiled=True),
        lax.all_gather(b_up, "shard", axis=0, tiled=True),
        lax.all_gather(w_down, "shard", axis=0, tiled=True),
        lax.all_gather(b_down, "shard", axis=0, tiled=True),
        lax.all_gather(ffn_gain, "shard", axis=0, tiled=True),
        lax.all_gather(ffn_shift, "shard", axis=0, tiled=True),
    )
    normed_low = normed_one.astype(jnp.bfloat16)
    up_proj = matmul(normed_low, full_wup) + as_float(full_bup)
    activated_float, gelu_pull = jax.vjp(gelu_exact, up_proj)
    activated = activated_float.astype(jnp.bfloat16)
    down_proj = matmul(activated, full_wdown) + as_float(full_bdown)
    residual_two = normed_one + down_proj
    output_float, norm_two_pull = jax.vjp(
        layer_norm, residual_two, as_float(full_fgain), as_float(full_fshift)
    )
    layer_output = output_float.astype(jnp.bfloat16)
    back_wup, back_bup, back_wdown, back_bdown, back_fgain, back_fshift = (
        lax.all_gather(w_up, "shard", axis=0, tiled=True),
        lax.all_gather(b_up, "shard", axis=0, tiled=True),
        lax.all_gather(w_down, "shard", axis=0, tiled=True),
        lax.all_gather(b_down, "shard", axis=0, tiled=True),
        lax.all_gather(ffn_gain, "shard", axis=0, tiled=True),
        lax.all_gather(ffn_shift, "shard", axis=0, tiled=True),
    )
    d_sum_two, grad_ffn_gain, grad_ffn_shift = norm_two_pull(as_float(cotangent))
    d_down = d_sum_two.astype(jnp.bfloat16)
    grad_w_down = matmul_left_t(activated, d_down)
    grad_b_down = jnp.sum(d_down, axis=0, dtype=jnp.float32)
    d_activated = matmul_right_t(d_down, back_wdown)
    d_up = gelu_pull(d_activated)[0].astype(jnp.bfloat16)
    grad_w_up = matmul_left_t(normed_low, d_up)
    grad_b_up = jnp.sum(d_up, axis=0, dtype=jnp.float32)
    d_normed_one = d_sum_two + matmul_right_t(d_up, back_wup)
    back_qkv, back_bqv, back_wout, back_bout, back_again, back_ashift = (
        lax.all_gather(w_qkv, "shard", axis=0, tiled=True),
        lax.all_gather(b_qv, "shard", axis=0, tiled=True),
        lax.all_gather(w_out, "shard", axis=0, tiled=True),
        lax.all_gather(b_out, "shard", axis=0, tiled=True),
        lax.all_gather(attn_gain, "shard", axis=0, tiled=True),
        lax.all_gather(attn_shift, "shard", axis=0, tiled=True),
    )
    d_sum_one, grad_attn_gain, grad_attn_shift = norm_one_pull(d_normed_one)
    d_attended = d_sum_one.astype(jnp.bfloat16)
    grad_w_out = matmul_left_t(context, d_attended)
    grad_b_out = jnp.sum(d_attended, axis=0, dtype=jnp.float32)
    d_context = matmul_right_t(d_attended, back_wout).astype(jnp.bfloat16)
    d_context_heads = split_heads(d_context, seq_count)
    d_queries, d_keys, d_values = lax.map(
        head_backward, (query_heads, key_heads, value_heads, d_context_heads, log_totals)
    )
    d_projected = jnp.concatenate(
        [
            join_heads(d_queries, seq_count),
            join_heads(d_keys, seq_count),
            join_heads(d_values, seq_count),
        ],
        axis=1,
    ).astype(jnp.bfloat16)
    grad_w_qkv = matmul_left_t(inputs, d_projected)
    column_sums = jnp.sum(d_projected, axis=0, dtype=jnp.float32)
    grad_b_qv = jnp.concatenate([column_sums[:D], column_sums[2 * D :]])
    input_grad = (d_sum_one + matmul_right_t(d_projected, back_qkv)).astype(jnp.bfloat16)
    (
        owned_qkv,
        owned_bqv,
        owned_wout,
        owned_bout,
        owned_again,
        owned_ashift,
        owned_wup,
        owned_bup,
        owned_wdown,
        owned_bdown,
        owned_fgain,
        owned_fshift,
    ) = (
        lax.psum_scatter(
            grad_w_qkv.astype(jnp.bfloat16), "shard", scatter_dimension=0, tiled=True
        ).astype(jnp.float32),
        lax.psum_scatter(
            grad_b_qv.astype(jnp.bfloat16), "shard", scatter_dimension=0, tiled=True
        ).astype(jnp.float32),
        lax.psum_scatter(
            grad_w_out.astype(jnp.bfloat16), "shard", scatter_dimension=0, tiled=True
        ).astype(jnp.float32),
        lax.psum_scatter(
            grad_b_out.astype(jnp.bfloat16), "shard", scatter_dimension=0, tiled=True
        ).astype(jnp.float32),
        lax.psum_scatter(
            grad_attn_gain.astype(jnp.bfloat16), "shard", scatter_dimension=0, tiled=True
        ).astype(jnp.float32),
        lax.psum_scatter(
            grad_attn_shift.astype(jnp.bfloat16), "shard", scatter_dimension=0, tiled=True
        ).astype(jnp.float32),
        lax.psum_scatter(
            grad_w_up.astype(jnp.bfloat16), "shard", scatter_dimension=0, tiled=True
        ).astype(jnp.float32),
        lax.psum_scatter(
            grad_b_up.astype(jnp.bfloat16), "shard", scatter_dimension=0, tiled=True
        ).astype(jnp.float32),
        lax.psum_scatter(
            grad_w_down.astype(jnp.bfloat16), "shard", scatter_dimension=0, tiled=True
        ).astype(jnp.float32),
        lax.psum_scatter(
            grad_b_down.astype(jnp.bfloat16), "shard", scatter_dimension=0, tiled=True
        ).astype(jnp.float32),
        lax.psum_scatter(
            grad_ffn_gain.astype(jnp.bfloat16), "shard", scatter_dimension=0, tiled=True
        ).astype(jnp.float32),
        lax.psum_scatter(
            grad_ffn_shift.astype(jnp.bfloat16), "shard", scatter_dimension=0, tiled=True
        ).astype(jnp.float32),
    )
    finals = (
        lax.psum(owned_qkv.astype(jnp.bfloat16), "replica").astype(jnp.float32),
        lax.psum(owned_bqv.astype(jnp.bfloat16), "replica").astype(jnp.float32),
        lax.psum(owned_wout.astype(jnp.bfloat16), "replica").astype(jnp.float32),
        lax.psum(owned_bout.astype(jnp.bfloat16), "replica").astype(jnp.float32),
        lax.psum(owned_again.astype(jnp.bfloat16), "replica").astype(jnp.float32),
        lax.psum(owned_ashift.astype(jnp.bfloat16), "replica").astype(jnp.float32),
        lax.psum(owned_wup.astype(jnp.bfloat16), "replica").astype(jnp.float32),
        lax.psum(owned_bup.astype(jnp.bfloat16), "replica").astype(jnp.float32),
        lax.psum(owned_wdown.astype(jnp.bfloat16), "replica").astype(jnp.float32),
        lax.psum(owned_bdown.astype(jnp.bfloat16), "replica").astype(jnp.float32),
        lax.psum(owned_fgain.astype(jnp.bfloat16), "replica").astype(jnp.float32),
        lax.psum(owned_fshift.astype(jnp.bfloat16), "replica").astype(jnp.float32),
    )
    return (layer_output, input_grad) + tuple(finals)


def solution(mesh):
    in_specs = (
        P(("replica", "shard"), None),
        P(("replica", "shard"), None),
        P("shard", None),
        P("shard"),
        P("shard", None),
        P("shard"),
        P("shard"),
        P("shard"),
        P("shard", None),
        P("shard"),
        P("shard", None),
        P("shard"),
        P("shard"),
        P("shard"),
        P(("replica", "shard"), None),
    )
    out_specs = (
        P(("replica", "shard"), None),
        P(("replica", "shard"), None),
        P("shard", None),
        P("shard"),
        P("shard", None),
        P("shard"),
        P("shard"),
        P("shard"),
        P("shard", None),
        P("shard"),
        P("shard", None),
        P("shard"),
        P("shard"),
        P("shard"),
    )
    return jax.shard_map(local, mesh=mesh, in_specs=in_specs, out_specs=out_specs, check_vma=False)
```

profile of v0, /device:TPU:0, one launch (start us, length us, event | category | flops | bytes accessed | tf_op | source)
XLA Modules:
  0.0 815.6 jit_solution(408371401616509706)
XLA Ops:
  10.1 5.3 all-gather
  17.1 4.3 all-gather.1
  21.5 4.3 all-gather.2
  25.9 4.3 all-gather.3
  30.3 4.5 all-gather.4
  34.8 4.3 all-gather.5
  41.4 4.3 all-gather.6
  46.4 4.3 all-gather.7
  51.3 10.6 %all-gather.13.cloned.1.call-done = bf16[768,2304]{1,0:T(8,128)(2,1)} async-done(((bf16[384,2304]{1,0:T(8,128)(2,1)}), bf16[768,2304]{1,0:T(8,128)(2,1)}) %all-gather.13.cloned.1.call-update) | async-done | bytes 3538960 | tf_op jit(solution)/shard_map/all_gather | solution.py:119
  62.0 6.0 add_convert_fusion.1
  71.6 3.1 copy.61
  74.7 2.6 copy.59
  77.3 4.1 copy.62
  81.4 2.6 copy.60
  83.9 4.1 copy.63
  89.4 75.4 %while.28 = (s32[]{:T(128)}, bf16[12,1,1024,64]{2,3,1,0:T(8,128)(2,1)}, f32[12,1,1024]{2,1,0:T(1,128)}, bf16[12,1,1024,64]{3,2,1,0:T(8,128)(2,1)S(1)}, bf16[12,1...) while((s32[]{:T(128)}, ...), condition=%wide.region_3.4_spmd.clone, body=%wide.region_0.3_spmd.clone.sunk | while | flops 284163072 | bytes 13695573 | solution.py:133
  92.7 3.0 fusion.121
  99.1 3.0 fusion.121
  105.4 2.9 fusion.121
  111.7 2.9 fusion.121
  117.9 2.9 fusion.121
  124.2 2.9 fusion.121
  130.5 2.9 fusion.121
  136.7 2.9 fusion.121
  143.0 2.9 fusion.121
  149.3 2.9 fusion.121
  155.6 2.9 fusion.121
  161.9 3.0 fusion.121
  166.5 3.8 fusion.77
  170.8 38.2 %multiply_convert_fusion.1 = (bf16[1024,3072]{1,0:T(8,128)(2,1)}, f32[1024,3072]{1,0:T(8,128)}, f32[1024,3072]{1,0:T(8,128)}) fusion(f32[3072]{0:T(1024)S(1)} %bitcast.176, bf16[768,3072]{1,0:T(8,128)(2,1)} %all-gather.17.cloned.1.call-done, f32[1024,768]{0,1:T(8,128)S(1)} %get-tuple-element.311, f32[768]{0:T(1024)S(1)} %reshape.343, ...), kind=kOutput, calls=%fused_computation.60 | convolution fusion | flops 5043388416 | bytes 39348224 | tf_op jit(solution)/shard_map/dot_general | solution.py:28
  209.0 5.6 all-gather.19.cloned.1.call-done
  214.7 9.9 %fusion.78 = (f32[1024]{0:T(1024)S(1)}, f32[1024,768]{0,1:T(8,128)S(1)}) fusion(f32[768]{0:T(1024)S(1)} %copy-done.16, bf16[1024,3072]{1,0:T(8,128)(2,1)} %get-tuple-element.296, bf16[3072,768]{1,0:T(8,128)(2,1)} %all-gather.19.cloned.1.call-done, f32[768]{0:T(1024)S(1)} %reshape.343, f32[768]{0:T(1024)S(1)} %reshape.342, f32[1024]{0:T(1024)S(1)} %fusion.64, ...), kind=kOutput, calls=%fused_computation.132 | convolution fusion | flops 4837342208 | bytes 17323008 | tf_op jit(solution)/shard_map/dot_general | solution.py:28
  225.4 2.9 fusion.62
  229.5 17.6 %fusion.79 = (bf16[3072]{0:T(1024)(128)(2,1)S(1)}, bf16[1024,3072]{1,0:T(8,128)(2,1)}) fusion(f32[1024,3072]{1,0:T(8,128)} %get-tuple-element.297, bf16[1024,768]{0,1:T(8,128)(2,1)S(1)} %get-tuple-element.291, bf16[3072,768]{1,0:T(8,128)(2,1)} %all-gather.19.cloned.1.call-done, f32[1024,3072]{1,0:T(8,128)} %get-tuple-element.312, f32[3072]{0:T(1024)S(1)} %bitcast.177), kind=kOutput, calls=%fused_computation.133 | convolution fusion | flops 4882166784 | bytes 37767168 | tf_op jit(solution)/shard_map/dot_general | solution.py:32
  247.2 11.0 %multiply_reduce_fusion.1 = (bf16[768]{0:T(1024)(128)(2,1)S(1)}, f32[1024]{0:T(1024)S(1)}, bf16[768]{0:T(1024)(128)(2,1)S(1)}, f32[1024,768]{0,1:T(8,128)S(1)}) fusion(f32[1024,768]{0,1:T(8,128)} %copy-done.1, f32[1024]{0:T(1024)S(1)} %fusion.64, f32[1024]{0:T(1024)S(1)} %broadcast_multiply_fusion.1, f32[768]{0:T(1024)S(1)} %reshape.342, ...), kind=kOutput, calls=%fused_computation.88 | convolution fusion | flops 4845204480 | bytes 22057984 | tf_op jit(solution)/shard_map/dot_general | solution.py:32
  262.8 4.1 copy.66
  271.1 157.0 %while.29 = (s32[]{:T(128)}, bf16[12,1,1024,64]{2,3,1,0:T(8,128)(2,1)}, bf16[12,1,1024,64]{2,3,1,0:T(8,128)(2,1)}, bf16[12,1,1024,64]{2,3,1,0:T(8,128)(2,1)}, bf...) while((s32[]{:T(128)}, ...), condition=%wide.region_14.15_spmd.clone, body=%wide.region_12.14_spmd.clone.sunk | while | flops 681704448 | bytes 34112624 | solution.py:189
  286.5 2.6 multiply_reduce_fusion.6
  299.6 2.6 multiply_reduce_fusion.6
  312.7 2.6 multiply_reduce_fusion.6
  325.8 2.6 multiply_reduce_fusion.6
  338.9 2.6 multiply_reduce_fusion.6
  351.9 2.6 multiply_reduce_fusion.6
  365.0 2.6 multiply_reduce_fusion.6
  378.1 2.6 multiply_reduce_fusion.6
  417.2 2.6 multiply_reduce_fusion.6
  428.0 8.5 %fusion.58 = bf16[768,2304]{0,1:T(8,128)(2,1)} fusion(bf16[1024,768]{1,0:T(8,128)(2,1)} %param.19, bf16[1024,768]{0,1:T(8,128)(2,1)} %bitcast.20, bf16[1024,768]{0,1:T(8,128)(2,1)} %bitcast.165, bf16[1024,768]{0,1:T(8,128)(2,1)} %bitcast.162), kind=kOutput, calls=%fused_computation.81 | convolution fusion | flops 3639803904 | bytes 9830400 | tf_op jit(solution)/shard_map/dot_general | solution.py:38
  436.5 5.8 copy.76
  442.4 4.3 convolution_convert_fusion.4
  446.8 9.9 %convolution_convert_fusion = bf16[3072,768]{1,0:T(8,128)(2,1)} fusion(bf16[1024,3072]{1,0:T(8,128)(2,1)} %get-tuple-element.296, bf16[1024,768]{0,1:T(8,128)(2,1)} %copy-done.12), kind=kOutput, calls=%fused_computation.75 | convolution fusion | flops 4834197504 | bytes 12582912 | tf_op jit(solution)/shard_map/dot_general | solution.py:38
  456.8 9.7 %convolution_convert_fusion.1 = bf16[768,3072]{1,0:T(8,128)(2,1)} fusion(bf16[1024,3072]{1,0:T(8,128)(2,1)} %get-tuple-element.317, f32[1024,768]{0,1:T(8,128)} %copy-done.1, f32[768]{0:T(1024)S(1)} %reshape.343, f32[768]{0:T(1024)S(1)} %reshape.342, f32[1024]{0:T(1024)S(1)} %fusion.64, f32[1024]{0:T(1024)S(1)} %broadcast_multiply_fusion.1), kind=kOutput, calls=%fused_computation.76 | convolution fusion | flops 4838129664 | bytes 14170112 | tf_op jit(solution)/shard_map/dot_general | solution.py:38
  466.6 23.6 %reduce-scatter.13.cloned.1.call-done = bf16[384,2304]{1,0:T(8,128)(2,1)} async-done(((bf16[768,2304]{1,0:T(8,128)(2,1)}), bf16[384,2304]{1,0:T(8,128)(2,1)}) %reduce-scatter.13.cloned.1.call-update) | async-done | bytes 1769488
  490.2 3.9 copy.77
  494.0 20.7 %reduce-scatter.7.cloned.1.call-done = bf16[384,768]{1,0:T(8,128)(2,1)} async-done(((bf16[768,768]{1,0:T(8,128)(2,1)}), bf16[384,768]{1,0:T(8,128)(2,1)}) %reduce-scatter.7.cloned.1.call-update) | async-done | bytes 589840 | tf_op jit(solution)/shard_map/reduce_scatter | solution.py:224
  514.7 62.9 %reduce-scatter.11.cloned.1.call-done = bf16[1536,768]{1,0:T(8,128)(2,1)} async-done(((bf16[3072,768]{1,0:T(8,128)(2,1)}), bf16[1536,768]{1,0:T(8,128)(2,1)}) %reduce-scatter.11.cloned.1.call-update) | async-done | bytes 2359312 | tf_op jit(solution)/shard_map/reduce_scatter | solution.py:242
  577.6 63.0 %reduce-scatter.9.cloned.1.call-done = bf16[384,3072]{1,0:T(8,128)(2,1)} async-done(((bf16[768,3072]{1,0:T(8,128)(2,1)}), bf16[384,3072]{1,0:T(8,128)(2,1)}) %reduce-scatter.9.cloned.1.call-update) | async-done | bytes 2359312 | tf_op jit(solution)/shard_map/reduce_scatter | solution.py:236
  644.9 2.7 fusion.66
  647.6 7.1 all-reduce.10
  655.4 62.9 %all-reduce.8 = (bf16[768]{0:T(1024)(128)(2,1)S(1)}, bf16[384]{0:T(512)(128)(2,1)S(1)}, bf16[384]{0:T(512)(128)(2,1)S(1)}, bf16[384]{0:T(512)(128)(2,1)S(1)}, bf...) all-reduce(bf16[768]{0:T(1024)(128)(2,1)S(1)} %dynamic-slice.1, ...), channel_id=1, replica_groups=mesh['replica'=16,'shard'=2] {'replica'}, use_global_device_ids=true, to_apply=%region_19.20 | all-reduce | flops 4608 | bytes 18432 | tf_op jit(solution)/shard_map/psum | solution.py:257
  722.9 8.4 %add_convert_fusion.2 = bf16[1024,768]{0,1:T(8,128)(2,1)} fusion(f32[1024,768]{0,1:T(8,128)S(1)} %get-tuple-element.295, bf16[768,2304]{1,0:T(8,128)(2,1)} %all-gather.13.cloned.1.call-done, f32[1024]{0:T(1024)S(1)} %negate_multiply_fusion.1, bf16[1024,768]{0,1:T(8,128)(2,1)} %bitcast.20, bf16[1024,768]{0,1:T(8,128)(2,1)} %bitcast.167, ...), kind=kOutput, calls=%fused_computation.89 | convolution fusion | flops 3640393728 | bytes 12980224 | tf_op jit(solution)/shard_map/dot_general | solution.py:32
  731.3 2.7 copy.72
  735.6 62.1 %all-reduce.13.cloned.1.call-done = (bf16[384,2304]{0,1:T(8,128)(2,1)}, bf16[384,768]{1,0:T(8,128)(2,1)}, bf16[384,3072]{1,0:T(8,128)(2,1)}, bf16[1536,768]{1,0:T(8,128)(2,1)}) async-done(((bf16[384,2304]{0,1:T(8,128)(2,1)}, bf16[384,768]{1,0:T(8,128)(2,1)}, bf16[384,3072]{1,0:T(8,128)(2,1)}, bf16[1536,768]{1,0:T(8,128)(2,1)}), (bf16[384,2304]{0,1:T(8,128)(2,1)}, bf16[384,768]{1,0:T(8,128)(2,1)}, ...) | async-done | bytes 7077904 | tf_op jit(solution)/shard_map/psum | solution.py:256
  797.7 4.6 convert_element_type.213
  804.8 2.7 copy.73
  (266 shorter events, 211.9 us)
Async XLA Ops:
  7.2 2.9 copy-start.18
  7.2 8.2 %copy-start.11 = (bf16[1024,768]{1,0:T(8,128)(2,1)S(1)}, bf16[1024,768]{1,0:T(8,128)(2,1)}, u32[]{:S(2)}) copy-start(bf16[1024,768]{1,0:T(8,128)(2,1)} %param.19) | copy-start | bytes 4718596
  7.2 54.8 %all-gather.13.cloned.1.call-start = ((), (), s32[]{:S(2)}) async-start(), calls=%async_computation.4 | async-start | bytes 5308416 | tf_op jit(solution)/shard_map/all_gather | solution.py:119
  7.9 156.9 %all-gather.15.cloned.1.call-start = ((), (), s32[]{:S(2)}) async-start(), calls=%async_computation.5 | async-start | bytes 1769472 | tf_op jit(solution)/shard_map/all_gather | solution.py:121
  8.7 162.1 %all-gather.17.cloned.1.call-start = ((), (), s32[]{:S(2)}) async-start(), calls=%async_computation.6 | async-start | bytes 7077888 | tf_op jit(solution)/shard_map/all_gather | solution.py:141
  9.4 7.7 copy-start.19
  9.4 12.0 %copy-start.20 = (bf16[384]{0:T(512)(128)(2,1)S(1)}, bf16[384]{0:T(512)(128)(2,1)}, u32[]{:S(2)}) copy-start(bf16[384]{0:T(512)(128)(2,1)} %param.25) | copy-start | bytes 2308
  9.4 16.4 %copy-start.21 = (bf16[384]{0:T(512)(128)(2,1)S(1)}, bf16[384]{0:T(512)(128)(2,1)}, u32[]{:S(2)}) copy-start(bf16[384]{0:T(512)(128)(2,1)} %param.26) | copy-start | bytes 2308
  9.5 20.8 %copy-start.17 = (bf16[1536]{0:T(1024)(128)(2,1)S(1)}, bf16[1536]{0:T(1024)(128)(2,1)}, u32[]{:S(2)}) copy-start(bf16[1536]{0:T(1024)(128)(2,1)} %param.28) | copy-start | bytes 9220
  9.5 25.3 %copy-start.22 = (bf16[384]{0:T(512)(128)(2,1)S(1)}, bf16[384]{0:T(512)(128)(2,1)}, u32[]{:S(2)}) copy-start(bf16[384]{0:T(512)(128)(2,1)} %param.30) | copy-start | bytes 2308
  9.5 30.3 %copy-start.4 = (bf16[1024,768]{1,0:T(8,128)(2,1)S(1)}, bf16[1024,768]{1,0:T(8,128)(2,1)}, u32[]{:S(2)}) copy-start(bf16[1024,768]{1,0:T(8,128)(2,1)} %param.33) | copy-start | bytes 4718596
  9.5 205.2 %all-gather.19.cloned.1.call-start = ((), (), s32[]{:S(2)}) async-start(), calls=%async_computation.7 | async-start | bytes 7077888 | tf_op jit(solution)/shard_map/all_gather | solution.py:143
  10.1 480.1 %reduce-scatter.13.cloned.1.call-start = ((), (), s32[]{:S(2)}) async-start(), calls=%async_computation.11 | async-start | bytes 5308416
  15.4 26.0 %copy-start.23 = (bf16[384]{0:T(512)(128)(2,1)S(1)}, bf16[384]{0:T(512)(128)(2,1)}, u32[]{:S(2)}) copy-start(bf16[384]{0:T(512)(128)(2,1)} %param.31) | copy-start | bytes 2308
  15.4 30.9 %copy-start.24 = (bf16[384]{0:T(512)(128)(2,1)S(1)}, bf16[384]{0:T(512)(128)(2,1)}, u32[]{:S(2)}) copy-start(bf16[384]{0:T(512)(128)(2,1)} %param.32) | copy-start | bytes 2308
  83.9 5.5 copy-start.8
  164.8 1.7 copy-start.3
  170.3 38.7 %copy-start.1 = (f32[1024,768]{0,1:T(8,128)}, f32[1024,768]{0,1:T(8,128)S(1)}, u32[]{:S(2)}) copy-start(f32[1024,768]{0,1:T(8,128)S(1)} %get-tuple-element.311) | copy-start | bytes 9437188
  170.8 43.9 %copy-start.16 = (f32[768]{0:T(1024)S(1)}, f32[768]{0:T(1024)}, u32[]{:S(2)}) copy-start(f32[768]{0:T(1024)} %reshape.345) | copy-start | bytes 9220
  214.6 9.9 %copy-start = (bf16[1024,768]{0,1:T(8,128)(2,1)S(1)}, bf16[1024,768]{0,1:T(8,128)(2,1)}, u32[]{:S(2)}) copy-start(bf16[1024,768]{0,1:T(8,128)(2,1)} %copy.64) | copy-start | bytes 4718596
  214.6 9.9 %copy-start.14 = (f32[768]{0:T(1024)S(1)}, f32[768]{0:T(1024)}, u32[]{:S(2)}) copy-start(f32[768]{0:T(1024)} %reshape.346) | copy-start | bytes 9220
  224.5 0.8 copy-start.15
  229.5 17.6 %copy-start.12 = (bf16[1024,768]{0,1:T(8,128)(2,1)}, bf16[1024,768]{0,1:T(8,128)(2,1)S(1)}, u32[]{:S(2)}) copy-start(bf16[1024,768]{0,1:T(8,128)(2,1)S(1)} %get-tuple-element.291) | copy-start | bytes 4718596
  247.2 11.1 %copy-start.2 = (f32[1024,768]{0,1:T(8,128)S(1)}, f32[1024,768]{0,1:T(8,128)}, u32[]{:S(2)}) copy-start(f32[1024,768]{0,1:T(8,128)} %copy-done.1) | copy-start | bytes 9437188
  259.0 1.3 copy-start.25
  259.4 3.4 copy-start.10
  266.9 4.1 copy-start.9
  442.3 72.4 %reduce-scatter.7.cloned.1.call-start = ((), (), s32[]{:S(2)}) async-start(), calls=%async_computation.8 | async-start | bytes 1769472 | tf_op jit(solution)/shard_map/reduce_scatter | solution.py:224
  446.7 130.9 %reduce-scatter.11.cloned.1.call-start = ((), (), s32[]{:S(2)}) async-start(), calls=%async_computation.10 | async-start | bytes 7077888 | tf_op jit(solution)/shard_map/reduce_scatter | solution.py:242
  456.7 183.9 %reduce-scatter.9.cloned.1.call-start = ((), (), s32[]{:S(2)}) async-start(), calls=%async_computation.9 | async-start | bytes 7077888 | tf_op jit(solution)/shard_map/reduce_scatter | solution.py:236
  466.5 331.1 %all-reduce.13.cloned.1.call-start = ((), (), s32[]{:S(2)}) async-start(), calls=%async_computation.12 | async-start | bytes 14155776 | tf_op jit(solution)/shard_map/psum | solution.py:256
  640.6 1.7 copy-start.26
  731.3 2.7 copy-start.5
  797.7 4.6 copy-start.6
  802.3 2.6 copy-start.7
  804.8 2.7 copy-start.13
Sparse Core Ops, SparseCore 0:
  9.6 52.3 all-gather.12
  63.5 22.7 all-gather.14
  87.9 62.6 all-gather.16
  152.0 62.6 all-gather.18
  442.4 47.6 reduce-scatter.12
  492.9 21.7 reduce-scatter.6
  517.6 59.9 reduce-scatter.10
  580.6 59.9 reduce-scatter.8
  645.2 152.3 all-reduce.12
where the time goes:
time: 827 us; the launch traced here: 816 us
  matrix products  320 us (39%)
  waiting for transfers between devices  251 us (30%)
  blocking collectives  106 us (13%)
  local copies, waits for them, and re-layouts  70.8 us (9%)
  other arithmetic  50 us (6%)
  between operations  16.7 us (2%)
    reduce_scatter x1, waiting for transfers between devices, local(): lax.psum_scatter(grad_w_up.astype(jnp.bfloat16), 'shard', scatter_dimensi...  63 us
    reduce_scatter x1, waiting for transfers between devices, local(): lax.psum_scatter(grad_w_down.astype(jnp.bfloat16), 'shard', scatter_dimen...  62.9 us
    psum x1, blocking collectives, local(): lax.psum(owned_bqv.astype(jnp.bfloat16), 'replica').astype(jnp.float32)  62.9 us
    psum x1, waiting for transfers between devices, local(): lax.psum(owned_qkv.astype(jnp.bfloat16), 'replica').astype(jnp.float32)  62.1 us
    dot_general x4, matrix products, matmul(): return jnp.dot(left, right, preferred_element_type=jnp.float32)  58 us
    dot_general x24, matrix products, head_scores(): jnp.einsum('sqd,skd->sqk', query_head, key_head, preferred_element_type=j...  51.2 us
    dot_general x4, matrix products, matmul_right_t(): lax.dot_general(left, right, (((1,), (1,)), ((), ())), preferred_element_...  39.5 us
    dot_general x12, matrix products, head_forward(): jnp.einsum('sqk,skd->sqd', attn_probs, value_head, preferred_element_type...  35.4 us
  transfers between devices with their start and end apart: 9, of which 7 were waited for; matrix products, arithmetic and copies ran while one was open for 25% of the time, Pallas kernels for 0%

commit v1 on v0

v1 whole, which is shorter than its diff:
```python
import functools

import jax
import jax.numpy as jnp
from jax import lax
from jax.experimental import pallas as pl
from jax.experimental.pallas import tpu as pltpu
from jax.sharding import PartitionSpec as P

D = 768
HEADS = 12
HEAD_DIM = 64
LEN = 1024
PAIRS = HEADS // 2
WIDE = 2 * HEAD_DIM
KEY_TILE = 128
FORWARD_ROWS = 512
BACKWARD_ROWS = 256
BIG = float(2**30)
EPSILON = 1e-12
F32 = jnp.float32
LOW = jnp.bfloat16


def layer_norm(hidden, gain, shift):
    average = jnp.mean(hidden, axis=-1, keepdims=True)
    centered = hidden - average
    variance = jnp.mean(centered * centered, axis=-1, keepdims=True)
    return centered * lax.rsqrt(variance + EPSILON) * gain + shift


def gelu_exact(value):
    return jax.nn.gelu(value, approximate=False)


def matmul(left, right):
    return jnp.dot(left, right, preferred_element_type=F32)


def matmul_right_t(left, right):
    return lax.dot_general(left, right, (((1,), (1,)), ((), ())), preferred_element_type=F32)


def matmul_left_t(left, right):
    return lax.dot_general(left, right, (((0,), (0,)), ((), ())), preferred_element_type=F32)


def as_float(value):
    return value.astype(F32)


def key_ranges(segments, rows):
    tiles = segments.reshape(LEN // rows, rows)
    below = jnp.sum(segments[None, :] < tiles[:, :1], axis=1, dtype=jnp.int32)
    upto = jnp.sum(segments[None, :] <= tiles[:, -1:], axis=1, dtype=jnp.int32)
    start = below // KEY_TILE
    count = (upto + KEY_TILE - 1) // KEY_TILE - start
    return jnp.concatenate([start, count])


def document_features(segments):
    lane = jnp.arange(WIDE, dtype=jnp.int32) % HEAD_DIM
    hot = segments[:, None] == lane[None, :]
    query_side = jnp.where((lane < 16) & hot, 1.0, 0.0).astype(LOW)
    key_side = jnp.where(
        lane < 16, jnp.where(hot, 0.0, -BIG), jnp.where(lane < 19, 1.0, 0.0)
    ).astype(LOW)
    return query_side, key_side


def attention_forward_body(
    ranges, packed, feature_q, feature_k, context, log_total, key_a, key_b, value_a, value_b
):
    rows = FORWARD_ROWS
    tiles = LEN // rows
    left = lax.broadcasted_iota(jnp.int32, (LEN, WIDE), 1) < HEAD_DIM
    keys, values = packed[:, WIDE : 2 * WIDE], packed[:, 2 * WIDE :]
    side = feature_k[...]
    ones = jnp.ones_like(values)
    key_a[...] = jnp.where(left, keys, side)
    key_b[...] = jnp.where(left, side, keys)
    value_a[...] = jnp.where(left, values, ones)
    value_b[...] = jnp.where(left, ones, values)
    left_q = lax.broadcasted_iota(jnp.int32, (rows, WIDE), 1) < HEAD_DIM

    def tile(index, carry):
        here = pl.ds(pl.multiple_of(index * rows, rows), rows)
        queries = packed[here, :WIDE] * jnp.asarray(HEAD_DIM**-0.5, LOW)
        side_q = feature_q[here, :]
        query_a = jnp.where(left_q, queries, side_q)
        query_b = jnp.where(left_q, side_q, queries)
        start = pl.multiple_of(ranges[index] * KEY_TILE, KEY_TILE)

        def over(width):
            def run():
                span = pl.ds(start, width)

                def head(query, key, value):
                    scores = matmul_right_t(query, key[span, :])
                    row_max = jnp.max(scores, axis=1, keepdims=True)
                    terms = jnp.exp(scores - row_max).astype(LOW)
                    return matmul(terms, value[span, :]), row_max

                out_a, max_a = head(query_a, key_a, value_a)
                out_b, max_b = head(query_b, key_b, value_b)
                totals = jnp.where(left_q, out_b, out_a)
                log_total[here, :] = jnp.where(left_q, max_b, max_a) + jnp.log(totals)
                inverse = pltpu.roll(1.0 / totals, HEAD_DIM, 1)
                context[here, :] = (jnp.where(left_q, out_a, out_b) * inverse).astype(LOW)

            return run

        lax.switch(
            ranges[tiles + index] - 1, [over(KEY_TILE * (n + 1)) for n in range(LEN // KEY_TILE)]
        )
        return carry

    lax.fori_loop(0, tiles, tile, 0)


def attention_forward(ranges, packed, feature_q, feature_k):
    whole = pl.BlockSpec((LEN, WIDE), lambda h, r: (0, 0))
    out = pl.BlockSpec((LEN, WIDE), lambda h, r: (0, h))
    return pl.pallas_call(
        attention_forward_body,
        out_shape=(jax.ShapeDtypeStruct((LEN, D), LOW), jax.ShapeDtypeStruct((LEN, D), F32)),
        grid_spec=pltpu.PrefetchScalarGridSpec(
            num_scalar_prefetch=1,
            grid=(PAIRS,),
            in_specs=[pl.BlockSpec((LEN, 3 * WIDE), lambda h, r: (0, h)), whole, whole],
            out_specs=[out, out],
            scratch_shapes=[pltpu.VMEM((LEN, WIDE), LOW)] * 4,
        ),
        name="attention_forward",
    )(ranges, packed, feature_q, feature_k)


def attention_backward_body(
    ranges,
    packed,
    context,
    d_context,
    log_total,
    feature_q,
    feature_k,
    d_packed,
    bias_sums,
    key_a,
    key_b,
    value_a,
    value_b,
    key_t,
    d_key,
    d_value,
):
    rows = BACKWARD_ROWS
    tiles = LEN // rows
    lane = lax.broadcasted_iota(jnp.int32, (LEN, WIDE), 1)
    left = lane < HEAD_DIM
    keys, values = packed[:, WIDE : 2 * WIDE], packed[:, 2 * WIDE :]
    side = feature_k[...]
    ones = jnp.where(lane % HEAD_DIM < 3, 1.0, 0.0).astype(LOW)
    key_a[...] = jnp.where(left, keys, side)
    key_b[...] = jnp.where(left, side, keys)
    value_a[...] = jnp.where(left, values, ones)
    value_b[...] = jnp.where(left, ones, values)
    key_t[...] = keys.T
    d_key[...] = jnp.zeros_like(d_key)
    d_value[...] = jnp.zeros_like(d_value)
    lane_q = lax.broadcasted_iota(jnp.int32, (rows, WIDE), 1)
    left_q = lane_q < HEAD_DIM
    inner = lane_q % HEAD_DIM
    zero = jnp.zeros((rows, WIDE), LOW)

    def spread(value, base):
        high = as_float(value.astype(LOW))
        rest = value - high
        middle = as_float(rest.astype(LOW))
        tail = rest - middle
        return jnp.where(
            inner == base,
            high,
            jnp.where(inner == base + 1, middle, jnp.where(inner == base + 2, tail, 0.0)),
        ).astype(LOW)

    def tile(index, sums):
        here = pl.ds(pl.multiple_of(index * rows, rows), rows)
        queries = packed[here, :WIDE] * jnp.asarray(HEAD_DIM**-0.5, LOW)
        side_q = feature_q[here, :] + spread(-log_total[here, :], 16)
        query_a = jnp.where(left_q, queries, side_q)
        query_b = jnp.where(left_q, side_q, queries)
        grad = d_context[here, :]
        product = as_float(grad) * as_float(context[here, :])
        dot_a = jnp.sum(jnp.where(left_q, product, 0.0), axis=1, keepdims=True)
        dot_b = jnp.sum(jnp.where(left_q, 0.0, product), axis=1, keepdims=True)
        side_g = spread(-jnp.where(left_q, dot_b, dot_a), 0)
        grad_a = jnp.where(left_q, grad, side_g)
        grad_b = jnp.where(left_q, side_g, grad)
        grad_both = jnp.concatenate(
            [jnp.where(left_q, grad, zero), jnp.where(left_q, zero, grad)], axis=0
        )
        query_both = jnp.concatenate(
            [jnp.where(left_q, queries, zero), jnp.where(left_q, zero, queries)], axis=0
        )
        start = pl.multiple_of(ranges[index] * KEY_TILE, KEY_TILE)

        def over(width):
            def run():
                span = pl.ds(start, width)

                def head(query, g, key, value):
                    probs = jnp.exp(matmul_right_t(key[span, :], query))
                    d_probs = matmul_right_t(value[span, :], g)
                    return probs.astype(LOW), (probs * d_probs).astype(LOW)

                probs_a, d_scores_a = head(query_a, grad_a, key_a, value_a)
                probs_b, d_scores_b = head(query_b, grad_b, key_b, value_b)
                d_value[span, :] += matmul(
                    jnp.concatenate([probs_a, probs_b], axis=1), grad_both
                )
                d_key[span, :] += matmul(
                    jnp.concatenate([d_scores_a, d_scores_b], axis=1), query_both
                )
                d_query_t = jnp.concatenate(
                    [
                        matmul(key_t[:HEAD_DIM, span], d_scores_a),
                        matmul(key_t[HEAD_DIM:, span], d_scores_b),
                    ],
                    axis=0,
                )
                d_packed[here, :WIDE] = (d_query_t.T * HEAD_DIM**-0.5).astype(LOW)

            return run

        lax.switch(
            ranges[tiles + index] - 1, [over(KEY_TILE * (n + 1)) for n in range(LEN // KEY_TILE)]
        )
        return sums + jnp.sum(as_float(d_packed[here, :WIDE]), axis=0, keepdims=True)

    sums = lax.fori_loop(0, tiles, tile, jnp.zeros((1, WIDE), F32))
    d_value_low = d_value[...].astype(LOW)
    d_packed[:, WIDE : 2 * WIDE] = d_key[...].astype(LOW)
    d_packed[:, 2 * WIDE :] = d_value_low
    bias_sums[0:1, :] = sums
    bias_sums[1:2, :] = jnp.sum(as_float(d_value_low), axis=0, keepdims=True)


def attention_backward(ranges, packed, context, d_context, log_total, feature_q, feature_k, pairs):
    whole = pl.BlockSpec((LEN, WIDE), lambda h, r: (0, 0))
    last = ranges.shape[0] - 1

    def column(width):
        return pl.BlockSpec((LEN, width), lambda h, r: (0, r[last] + h))

    return pl.pallas_call(
        attention_backward_body,
        out_shape=(
            jax.ShapeDtypeStruct((LEN, pairs * 3 * WIDE), LOW),
            jax.ShapeDtypeStruct((2, pairs * WIDE), F32),
        ),
        grid_spec=pltpu.PrefetchScalarGridSpec(
            num_scalar_prefetch=1,
            grid=(pairs,),
            in_specs=[column(3 * WIDE), column(WIDE), column(WIDE), column(WIDE), whole, whole],
            out_specs=[
                pl.BlockSpec((LEN, 3 * WIDE), lambda h, r: (0, h)),
                pl.BlockSpec((2, WIDE), lambda h, r: (0, h)),
            ],
            scratch_shapes=[pltpu.VMEM((LEN, WIDE), LOW)] * 4
            + [pltpu.VMEM((WIDE, LEN), LOW)]
            + [pltpu.VMEM((LEN, WIDE), F32)] * 2,
        ),
        name="attention_backward",
    )(ranges, packed, context, d_context, log_total, feature_q, feature_k)


class Place:
    def __init__(self, replicas, shards):
        self.replicas, self.shards = replicas, shards
        replica = lax.axis_index("replica")
        self.core = replica % 2
        self.x = replica // 2 % 2
        self.z = replica // 4
        self.depth = replicas // 4
        self.y = lax.axis_index("shard")


def swap(value, axis, size, mask):
    return lax.ppermute(value, axis, [(i, i ^ mask) for i in range(size)])


def pick(options, index):
    chosen = options[-1]
    for at in range(len(options) - 2, -1, -1):
        chosen = jnp.where(index == at, options[at], chosen)
    return chosen


def rows_of(value, block, size):
    return lax.dynamic_slice_in_dim(value, block * size, size, 0)


def gather_shards(pieces, at):
    found = {0: pieces}
    mask = 1
    while mask < at.shards:
        for d in range(mask):
            found[d | mask] = swap(found[d], "shard", at.shards, mask)
        mask *= 2
    return [found[d] for d in range(at.shards)]


def gather_weight(weight, at):
    half = weight.shape[0] // 2
    found = gather_shards(rows_of(weight, at.core, half), at)
    whole = [weight]
    for d in range(1, at.shards):
        other = swap(found[d], "replica", at.replicas, 1)
        whole.append(
            jnp.concatenate([pick([found[d], other], at.core), pick([other, found[d]], at.core)])
        )
    return jnp.concatenate([pick(whole, at.y ^ j) for j in range(at.shards)])


def reduce_shards(parts, at):
    mask = at.shards // 2
    while mask:
        parts = [
            (as_float(parts[d]) + as_float(swap(parts[d | mask], "shard", at.shards, mask))).astype(
                parts[d].dtype
            )
            for d in range(mask)
        ]
        mask //= 2
    return parts[0]


def reduce_gradient(send, keep, at):
    m = keep.shape[0] // at.shards
    got = swap(send, "replica", at.replicas, 1)
    parts = []
    for d in range(at.shards):
        block = at.y ^ d
        parts.append((as_float(rows_of(keep, block, m)) + as_float(rows_of(got, block, m))).astype(LOW))
    mine = reduce_shards(parts, at)
    half = m // 2
    got = swap(rows_of(mine, 1 - at.x, half), "replica", at.replicas, 2)
    mine = (as_float(rows_of(mine, at.x, half)) + as_float(got)).astype(LOW)
    piece = half // at.depth
    total = as_float(rows_of(mine, at.z, piece))
    for d in range(1, at.depth):
        total += as_float(
            swap(rows_of(mine, at.z ^ d, piece), "replica", at.replicas, 4 * d)
        )
    total = total.astype(LOW)
    found = [total] + [swap(total, "replica", at.replicas, 4 * d) for d in range(1, at.depth)]
    mine = jnp.concatenate([pick(found, at.z ^ j) for j in range(at.depth)])
    other = swap(mine, "replica", at.replicas, 2)
    mine_core = swap(mine, "replica", at.replicas, 1)
    other_core = swap(other, "replica", at.replicas, 1)
    own = jnp.concatenate([pick([mine, other], at.x), pick([other, mine], at.x)])
    partner = jnp.concatenate(
        [pick([mine_core, other_core], at.x), pick([other_core, mine_core], at.x)]
    )
    return as_float(pick([own, partner], at.core)), as_float(pick([partner, own], at.core))


def reduce_small(values, at):
    mine = reduce_shards([lax.dynamic_index_in_dim(values, at.y ^ d, 0, False) for d in range(at.shards)], at)
    mask = 1
    while mask < at.replicas:
        mine = mine + swap(mine, "replica", at.replicas, mask)
        mask *= 2
    return mine


def halves(left, right, at, columns):
    half = columns // 2
    return tuple(
        matmul_left_t(left, lax.dynamic_slice_in_dim(right, block * half, half, 1))
        for block in (1 - at.core, at.core)
    )


def pair_major(matrix):
    lead = matrix.shape[:-1]
    parts = matrix.reshape(lead + (3, PAIRS, WIDE))
    return jnp.swapaxes(parts, -3, -2).reshape(lead + (3 * D,))


def local(
    replicas,
    shards,
    inputs,
    segments,
    w_qkv,
    b_qv,
    w_out,
    b_out,
    attn_gain,
    attn_shift,
    w_up,
    b_up,
    w_down,
    b_down,
    ffn_gain,
    ffn_shift,
    cotangent,
):
    at = Place(replicas, shards)
    segments = segments.reshape(LEN)
    feature_q, feature_k = document_features(segments)

    vectors = (b_qv, b_out, attn_gain, attn_shift, b_up, b_down, ffn_gain, ffn_shift)
    sizes = [v.shape[0] for v in vectors]
    small = gather_shards(jnp.concatenate(vectors), at)
    small = as_float(jnp.stack([pick(small, at.y ^ j) for j in range(shards)]))
    full, offset = [], 0
    for size in sizes:
        full.append(small[:, offset : offset + size].reshape(-1))
        offset += size
    full_bqv, full_bout, full_again, full_ashift, full_bup, full_bdown, full_fgain, full_fshift = full

    full_qkv = pair_major(gather_weight(w_qkv, at))
    qkv_bias = pair_major(jnp.concatenate([full_bqv[:D], jnp.zeros((D,), F32), full_bqv[D:]]))
    full_wout = gather_weight(w_out, at)
    full_wup = gather_weight(w_up, at)
    full_wdown = gather_weight(w_down, at)

    projected = (matmul(inputs, full_qkv) + qkv_bias).astype(LOW)
    context, log_total = attention_forward(
        key_ranges(segments, FORWARD_ROWS), projected, feature_q, feature_k
    )
    attended = matmul(context, full_wout) + full_bout
    residual_one = as_float(inputs) + attended
    normed_one, norm_one_pull = jax.vjp(layer_norm, residual_one, full_again, full_ashift)
    normed_low = normed_one.astype(LOW)
    up_proj = matmul(normed_low, full_wup) + full_bup
    activated_float, gelu_pull = jax.vjp(gelu_exact, up_proj)
    activated = activated_float.astype(LOW)
    down_proj = matmul(activated, full_wdown) + full_bdown
    residual_two = normed_one + down_proj
    output_float, norm_two_pull = jax.vjp(layer_norm, residual_two, full_fgain, full_fshift)
    layer_output = output_float.astype(LOW)

    d_sum_two, grad_ffn_gain, grad_ffn_shift = norm_two_pull(as_float(cotangent))
    d_down = d_sum_two.astype(LOW)
    down_send, down_keep = halves(activated, d_down, at, D)
    grad_w_down = reduce_gradient(down_send.astype(LOW), down_keep, at)
    grad_b_down = jnp.sum(d_down, axis=0, dtype=F32)
    d_activated = matmul_right_t(d_down, full_wdown)
    d_up = gelu_pull(d_activated)[0].astype(LOW)
    up_send, up_keep = halves(normed_low, d_up, at, 4 * D)
    grad_w_up = reduce_gradient(up_send.astype(LOW), up_keep, at)
    grad_b_up = jnp.sum(d_up, axis=0, dtype=F32)
    d_normed_one = d_sum_two + matmul_right_t(d_up, full_wup)
    d_sum_one, grad_attn_gain, grad_attn_shift = norm_one_pull(d_normed_one)
    d_attended = d_sum_one.astype(LOW)
    out_send, out_keep = halves(context, d_attended, at, D)
    grad_w_out = reduce_gradient(out_send.astype(LOW), out_keep, at)
    grad_b_out = jnp.sum(d_attended, axis=0, dtype=F32)
    d_context = matmul_right_t(d_attended, full_wout).astype(LOW)

    ranges = key_ranges(segments, BACKWARD_ROWS)
    pairs = PAIRS // 2
    input_grad = d_sum_one
    shares, sums = [], []
    for block in (1 - at.core, at.core):
        d_packed, bias_sums = attention_backward(
            jnp.concatenate([ranges, (block * pairs).reshape(1)]),
            projected,
            context,
            d_context,
            log_total,
            feature_q,
            feature_k,
            pairs,
        )
        shares.append(matmul_left_t(inputs, d_packed))
        sums.append(bias_sums)
        half = lax.dynamic_slice_in_dim(full_qkv, block * pairs * 3 * WIDE, pairs * 3 * WIDE, 1)
        input_grad = input_grad + matmul_right_t(d_packed, half)
    input_grad = input_grad.astype(LOW)
    grad_qkv = reduce_gradient(shares[0].astype(LOW), shares[1], at)
    grad_qkv = jnp.concatenate(grad_qkv, axis=1)
    grad_qkv = jnp.swapaxes(grad_qkv.reshape(-1, PAIRS, 3, WIDE), 1, 2).reshape(-1, 3 * D)
    sums = pick(
        [jnp.concatenate(sums[::-1], axis=1), jnp.concatenate(sums, axis=1)], at.core
    )

    grads = (
        sums.reshape(-1),
        grad_b_out,
        grad_attn_gain,
        grad_attn_shift,
        grad_b_up,
        grad_b_down,
        grad_ffn_gain,
        grad_ffn_shift,
    )
    packed = jnp.concatenate([g.reshape(shards, -1) for g in grads], axis=1)
    packed = reduce_small(packed.reshape(shards, -1, 128), at).reshape(-1)
    owned, offset = [], 0
    for size in sizes:
        owned.append(packed[offset : offset + size])
        offset += size
    return (
        layer_output,
        input_grad,
        grad_qkv,
        owned[0],
        jnp.concatenate(grad_w_out, axis=1),
        owned[1],
        owned[2],
        owned[3],
        jnp.concatenate(grad_w_up, axis=1),
        owned[4],
        jnp.concatenate(grad_w_down, axis=1),
        owned[5],
        owned[6],
        owned[7],
    )


def solution(mesh):
    tokens, matrix, vector = P(("replica", "shard"), None), P("shard", None), P("shard")
    weights = (matrix, vector, matrix, vector, vector, vector)
    weights += (matrix, vector, matrix, vector, vector, vector)
    return jax.shard_map(
        functools.partial(local, mesh.shape["replica"], mesh.shape["shard"]),
        mesh=mesh,
        in_specs=(tokens, tokens) + weights + (tokens,),
        out_specs=(tokens, tokens) + weights,
        check_vma=False,
    )
```

time: 827 us -> 547 us (0.66)
  the two profiles are of different devices: /device:TPU:0 before, /device:TPU:11 now
where the time goes in v1:
time: 547 us; the launch traced here: 538 us
  waiting for transfers between devices  130 us (24%)
  matrix products  121 us (22%)
  starting transfers between devices  81.8 us (15%)
  local copies, waits for them, and re-layouts  73 us (13%)
  Pallas kernels  69.3 us (13%)
  other arithmetic  59.9 us (11%)
    ppermute x62, waiting for transfers between devices, swap(): return lax.ppermute(value, axis, [(i, i ^ mask) for i in range(size)])  130 us
    ppermute x62, starting transfers between devices, swap(): return lax.ppermute(value, axis, [(i, i ^ mask) for i in range(size)])  81.8 us
    dot_general x4, matrix products, matmul(): return jnp.dot(left, right, preferred_element_type=F32)  49.1 us
    pallas_call x2, Pallas kernels, attention_backward(): pl.pallas_call(attention_backward_body, out_shape=(jax.ShapeDtypeStruct((...  42.6 us
    dot_general x5, matrix products, matmul_right_t(): lax.dot_general(left, right, (((1,), (1,)), ((), ())), preferred_element_...  41.3 us
    unnamed x154, local copies, waits for them, and re-layouts  35 us
    dot_general x8, matrix products, matmul_left_t(): lax.dot_general(left, right, (((0,), (0,)), ((), ())), preferred_element_...  31.1 us
    pallas_call x1, Pallas kernels, attention_forward(): pl.pallas_call(attention_forward_body, out_shape=(jax.ShapeDtypeStruct((L...  26.7 us
  transfers between devices with their start and end apart: 62, of which 22 were waited for; matrix products, arithmetic and copies ran while one was open for 26% of the time, Pallas kernels for 5%

profile of v1, /device:TPU:11, one launch (start us, length us, event | category | flops | bytes accessed | tf_op | source)
XLA Modules:
  0.0 538.4 jit_solution(5850759895404147434)
XLA Ops:
  9.0 2.1 constant_dynamic-slice_fusion.19
  15.6 2.5 constant_dynamic-slice_fusion.16
  24.5 2.8 copy.93
  29.1 2.7 copy.86
  32.0 3.0 collective-permute-start.1
  35.0 2.9 collective-permute-done.3
  37.9 3.3 collective-permute-start.4
  47.1 16.1 %collective-permute-done.5 = bf16[192,3072]{1,0:T(8,128)(2,1)} collective-permute-done((bf16[192,3072]{1,0:T(8,128)(2,1)}, bf16[192,3072]{1,0:T(8,128)(2,1)}, u32[]{:S(2)}, u32[]{:S(2)}) %collective-permute-start.5) | collective-permute-done | bytes 1179680 | tf_op jit(solution)/shard_map/ppermute | solution.py:289
  63.2 3.3 collective-permute-start.6
  66.5 21.9 %collective-permute-done.7 = bf16[768,768]{1,0:T(8,128)(2,1)} collective-permute-done((bf16[768,768]{1,0:T(8,128)(2,1)}, bf16[768,768]{1,0:T(8,128)(2,1)}, u32[]{:S(2)}, u32[]{:S(2)}) %collective-permute-start.7) | collective-permute-done | bytes 1179680 | tf_op jit(solution)/shard_map/ppermute | solution.py:289
  88.5 1.9 collective-permute-start.8
  90.4 2.3 copy.90
  97.4 5.5 %fusion.6.packed = bf16[1024,2304]{1,0:T(8,128)(2,1)} fusion(bf16[768,2304]{0,1:T(8,128)(2,1)S(1)} %bitcast.80, bf16[1024,768]{1,0:T(8,128)(2,1)S(1)} %copy-done.19, f32[2304]{0:T(1024)S(1)} %add.344), kind=kOutput, calls=%fused_computation.19 | convolution fusion | flops 3628597248 | bytes 9839616 | tf_op jit(solution)/shard_map/dot_general | solution.py:37
  102.8 26.7 %attention_forward.1 = (bf16[1024,768]{1,0:T(8,128)(2,1)}, f32[1024,768]{1,0:T(8,128)}) custom-call(s32[4]{0:T(128)} %get-tuple-element.207.ranges, bf16[1024,2304]{1,0:T(8,128)(2,1)} %fusion.6.packed, bf16[1024,128]{1,0:T(8,128)(2,1)} %select_convert_fusion.feature_q, bf16[1024,128]{1,0:T(8,128)(2,1)} %fusion.34.feature_k), custom_call_target="tpu_custom_call" | custom-call | tf_op jit(solution)/shard_map/attention_forward/pallas_call | solution.py:124
  129.6 3.8 fusion.60
  134.3 2.4 broadcast_select_fusion.15
  138.5 3.5 broadcast_select_fusion.13
  143.6 33.9 %multiply_convert_fusion = (bf16[1024,3072]{1,0:T(8,128)(2,1)S(1)}, f32[1024,3072]{1,0:T(8,128)}, f32[1024,3072]{1,0:T(8,128)}) fusion(f32[3072]{0:T(1024)S(1)} %add.356, bf16[1024,768]{0,1:T(8,128)(2,1)S(1)} %fusion.18, bf16[384,3072]{1,0:T(8,128)(2,1)S(1)} %get-tuple-element.111, bf16[384,3072]{1,0:T(8,128)(2,1)S(1)} %get-tuple-element.110), kind=kOutput, calls=%fused_computation.4 | convolution fusion | flops 5048893440 | bytes 37761024 | tf_op jit(solution)/shard_map/dot_general | solution.py:37
  177.6 5.9 %fusion.61 = (f32[1024]{0:T(1024)S(1)}, f32[1024,768]{0,1:T(8,128)S(1)}) fusion(f32[768]{0:T(1024)S(1)} %copy-done.48, bf16[1024,3072]{1,0:T(8,128)(2,1)S(1)} %get-tuple-element.104, bf16[1536,768]{1,0:T(8,128)(2,1)S(1)} %get-tuple-element.109, bf16[1536,768]{1,0:T(8,128)(2,1)S(1)} %get-tuple-element.108, f32[768]{0:T(1024)S(1)} %add.353, ...), kind=kOutput, calls=%fused_computation.286 | convolution fusion | flops 4846779392 | bytes 17323008 | tf_op jit(solution)/shard_map/dot_general | solution.py:37
  186.8 3.6 convert_reduce_fusion.2
  190.4 18.2 %convert_reduce_fusion = (f32[3072]{0:T(1024)}, bf16[1024,3072]{1,0:T(8,128)(2,1)}) fusion(f32[1024,3072]{1,0:T(8,128)} %get-tuple-element.105, bf16[1024,768]{0,1:T(8,128)(2,1)} %get-tuple-element.97, bf16[1536,768]{1,0:T(8,128)(2,1)} %copy-done.16, bf16[1536,768]{1,0:T(8,128)(2,1)} %copy-done.15, f32[1024,3072]{1,0:T(8,128)} %get-tuple-element.201, ...), kind=kOutput, calls=%fused_computation.2 | convolution fusion | flops 4894749696 | bytes 37773312 | tf_op jit(solution)/shard_map/dot_general | solution.py:41
  208.6 12.6 %multiply_reduce_fusion = (f32[768]{0:T(1024)}, f32[1024]{0:T(1024)S(1)}, f32[768]{0:T(1024)S(1)}, f32[1024,768]{0,1:T(8,128)S(1)}) fusion(f32[1024,768]{0,1:T(8,128)S(1)} %get-tuple-element.200, f32[1024]{0:T(1024)S(1)} %fusion.45, f32[1024]{0:T(1024)S(1)} %broadcast_multiply_fusion.1, f32[768]{0:T(1024)S(1)} %mul.254, ...), kind=kOutput, calls=%fused_computation.40 | convolution fusion | flops 4854641664 | bytes 22061056 | tf_op jit(solution)/shard_map/dot_general | solution.py:41
  224.2 2.6 convolution_convert_fusion.3.d_context
  228.7 4.8 convolution_convert_fusion
  233.5 21.4 %attention_backward.3 = (bf16[1024,1152]{1,0:T(8,128)(2,1)}, f32[2,384]{1,0:T(2,128)}) custom-call(s32[9]{0:T(128)} %get-tuple-element.198.ranges, bf16[1024,2304]{1,0:T(8,128)(2,1)} %fusion.6.packed, bf16[1024,768]{1,0:T(8,128)(2,1)} %get-tuple-element.20.context, bf16[1024,768]{1,0:T(8,128)(2,1)} %convolution_convert_fusion.3.d_context, ...), custom_call_target="tpu_custom_call" | custom-call | tf_op jit(solution)/shard_map/attention_backward/pallas_call | solution.py:255
  254.9 21.1 %attention_backward.2 = (bf16[1024,1152]{1,0:T(8,128)(2,1)}, f32[2,384]{1,0:T(2,128)}) custom-call(s32[9]{0:T(128)} %get-tuple-element.197.ranges, bf16[1024,2304]{1,0:T(8,128)(2,1)} %fusion.6.packed, bf16[1024,768]{1,0:T(8,128)(2,1)} %get-tuple-element.20.context, bf16[1024,768]{1,0:T(8,128)(2,1)} %convolution_convert_fusion.3.d_context, ...), custom_call_target="tpu_custom_call" | custom-call | tf_op jit(solution)/shard_map/attention_backward/pallas_call | solution.py:255
  276.1 5.7 %fusion.17 = bf16[768,1152]{1,0:T(8,128)(2,1)} fusion(bf16[1024,1152]{1,0:T(8,128)(2,1)} %get-tuple-element.22, bf16[1024,768]{1,0:T(8,128)(2,1)} %param.15), kind=kOutput, calls=%fused_computation.53 | convolution fusion | flops 1812824064 | bytes 5701632 | tf_op jit(solution)/shard_map/dot_general | solution.py:45
  298.4 4.1 fusion.21
  302.5 3.8 add_convert_fusion.2
  306.4 5.2 fusion.28
  311.7 4.3 fusion.12
  321.0 4.1 convolution_convert_fusion.1
  328.8 4.1 fusion.62
  334.5 2.7 copy.107
  337.2 2.5 collective-permute-start.38
  343.1 2.2 collective-permute-start.30
  353.6 2.7 collective-permute-start.50
  358.5 3.4 collective-permute-done.35
  362.8 8.7 %collective-permute-done.10 = bf16[384,1152]{1,0:T(8,128)(2,1)S(1)} collective-permute-done((bf16[384,1152]{1,0:T(8,128)(2,1)S(1)}, bf16[384,1152]{1,0:T(8,128)(2,1)S(1)}, u32[]{:S(2)}, u32[]{:S(2)}) %collective-permute-start.10) | collective-permute-done | bytes 884768 | tf_op jit(solution)/shard_map/ppermute | solution.py:289
  375.4 6.1 %collective-permute-done.11 = bf16[192,1152]{1,0:T(8,128)(2,1)S(1)} collective-permute-done((bf16[192,1152]{1,0:T(8,128)(2,1)S(1)}, bf16[192,1152]{1,0:T(8,128)(2,1)S(1)}, u32[]{:S(2)}, u32[]{:S(2)}) %collective-permute-start.11) | collective-permute-done | bytes 442400 | tf_op jit(solution)/shard_map/ppermute | solution.py:289
  382.8 4.6 collective-permute-start.13
  388.9 4.6 collective-permute-done.13
  393.6 3.0 collective-permute-start.15
  399.7 2.3 collective-permute-done.16
  402.1 4.7 collective-permute-done.17
  409.3 2.4 collective-permute-start.19
  414.3 22.2 %collective-permute-done.51 = bf16[1536,384]{1,0:T(8,128)(2,1)S(1)} collective-permute-done((bf16[1536,384]{1,0:T(8,128)(2,1)S(1)}, bf16[1536,384]{1,0:T(8,128)(2,1)S(1)}, u32[]{:S(2)}, u32[]{:S(2)}) %collective-permute-start.51) | collective-permute-done | bytes 1179680 | tf_op jit(solution)/shard_map/ppermute | solution.py:289
  442.3 5.0 collective-permute-start.20
  452.2 3.3 collective-permute-start.42
  457.8 3.3 collective-permute-start.54
  461.1 1.9 broadcast_select_fusion.28
  465.3 6.2 %collective-permute-done.42 = bf16[48,1536]{1,0:T(8,128)(2,1)} collective-permute-done((bf16[48,1536]{1,0:T(8,128)(2,1)}, bf16[48,1536]{1,0:T(8,128)(2,1)}, u32[]{:S(2)}, u32[]{:S(2)}) %collective-permute-start.42) | collective-permute-done | bytes 147488 | tf_op jit(solution)/shard_map/ppermute | solution.py:289
  472.7 3.3 collective-permute-start.44
  479.1 3.4 collective-permute-start.56
  484.5 2.6 collective-permute-done.45
  487.1 11.7 %collective-permute-done.46 = bf16[48,1536]{1,0:T(8,128)(2,1)S(1)} collective-permute-done((bf16[48,1536]{1,0:T(8,128)(2,1)S(1)}, bf16[48,1536]{1,0:T(8,128)(2,1)S(1)}, u32[]{:S(2)}, u32[]{:S(2)}) %collective-permute-start.46) | collective-permute-done | bytes 147488 | tf_op jit(solution)/shard_map/ppermute | solution.py:289
  500.0 5.2 collective-permute-done.58
  507.4 3.6 convert_bitcast_fusion
  511.1 4.5 copy.105
  515.5 2.9 copy.108
  519.9 6.7 %collective-permute-done.59 = bf16[768,384]{1,0:T(8,128)(2,1)} collective-permute-done((bf16[768,384]{1,0:T(8,128)(2,1)}, bf16[768,384]{1,0:T(8,128)(2,1)}, u32[]{:S(2)}, u32[]{:S(2)}) %collective-permute-start.59) | collective-permute-done | bytes 589856 | tf_op jit(solution)/shard_map/ppermute | solution.py:289
  526.5 2.1 collective-permute-start.61
  532.1 2.8 maximum_convert_fusion
  535.4 2.5 maximum_convert_fusion.1
  (378 shorter events, 130.5 us)
Async XLA Ops:
  7.7 24.2 %collective-permute-start.2 = (bf16[4608]{0:T(1024)(128)(2,1)S(1)}, bf16[4608]{0:T(1024)(128)(2,1)S(1)}, u32[]{:S(2)}, u32[]{:S(2)}) collective-permute-start(bf16[4608]{0:T(1024)(128)(2,1)S(1)} %dynamic-update-slice.19), channel_id=1, source_target_pairs={{0,1},{1,0},{2,3},{3,2},{4,5},{5,4},{6,7},{7,6},{8,9},{9,8},{10,11... | collective-permute-start | bytes 27656 | tf_op jit(solution)/shard_map/ppermute | solution.py:289
  11.1 20.8 %collective-permute-start = (bf16[192,2304]{1,0:T(8,128)(2,1)}, bf16[192,2304]{1,0:T(8,128)(2,1)}, u32[]{:S(2)}, u32[]{:S(2)}) collective-permute-start(bf16[192,2304]{1,0:T(8,128)(2,1)} %constant_dynamic-slice_fusion.19), channel_id=1, source_target_pairs={{0,1},{1,0},{2,3},{3,2},{4,5},{5,4},{6,7},{7,6},{8,9},{9,8},{10,11... | collective-permute-start | bytes 2654216 | tf_op jit(solution)/shard_map/ppermute | solution.py:289
  13.0 24.9 %collective-permute-start.3 = (bf16[192,768]{1,0:T(8,128)(2,1)}, bf16[192,768]{1,0:T(8,128)(2,1)}, u32[]{:S(2)}, u32[]{:S(2)}) collective-permute-start(bf16[192,768]{1,0:T(8,128)(2,1)} %constant_dynamic-slice_fusion.18), channel_id=1, source_target_pairs={{0,1},{1,0},{2,3},{3,2},{4,5},{5,4},{6,7},{7,6},{8,9},{9,8},{10,11... | collective-permute-start | bytes 884744 | tf_op jit(solution)/shard_map/ppermute | solution.py:289
  15.4 47.9 %collective-permute-start.5 = (bf16[192,3072]{1,0:T(8,128)(2,1)}, bf16[192,3072]{1,0:T(8,128)(2,1)}, u32[]{:S(2)}, u32[]{:S(2)}) collective-permute-start(bf16[192,3072]{1,0:T(8,128)(2,1)} %constant_dynamic-slice_fusion.17), channel_id=1, source_target_pairs={{0,1},{1,0},{2,3},{3,2},{4,5},{5,4},{6,7},{7,6},{8,9},{9,8},{10,11... | collective-permute-start | bytes 3538952 | tf_op jit(solution)/shard_map/ppermute | solution.py:289
  18.1 70.4 %collective-permute-start.7 = (bf16[768,768]{1,0:T(8,128)(2,1)}, bf16[768,768]{1,0:T(8,128)(2,1)}, u32[]{:S(2)}, u32[]{:S(2)}) collective-permute-start(bf16[768,768]{1,0:T(8,128)(2,1)} %constant_dynamic-slice_fusion.16), channel_id=1, source_target_pairs={{0,1},{1,0},{2,3},{3,2},{4,5},{5,4},{6,7},{7,6},{8,9},{9,8},{10,11... | collective-permute-start | bytes 3538952 | tf_op jit(solution)/shard_map/ppermute | solution.py:289
  32.0 58.4 %collective-permute-start.1 = (bf16[192,2304]{1,0:T(8,128)(2,1)}, bf16[192,2304]{1,0:T(8,128)(2,1)}, u32[]{:S(2)}, u32[]{:S(2)}) collective-permute-start(bf16[192,2304]{1,0:T(8,128)(2,1)} %collective-permute-done), channel_id=1, source_target_pairs={{0,2},{2,0},{4,6},{6,4},{8,10},{10,8},{12,14},{14,12},{16,18},{18,... | collective-permute-start | bytes 2654216 | tf_op jit(solution)/shard_map/ppermute | solution.py:289
  37.9 5.3 collective-permute-start.4
  63.2 71.1 %collective-permute-start.6 = (bf16[192,3072]{1,0:T(8,128)(2,1)}, bf16[192,3072]{1,0:T(8,128)(2,1)}, u32[]{:S(2)}, u32[]{:S(2)}) collective-permute-start(bf16[192,3072]{1,0:T(8,128)(2,1)} %collective-permute-done.5), channel_id=1, source_target_pairs={{0,2},{2,0},{4,6},{6,4},{8,10},{10,8},{12,14},{14,12},{16,18},{18,... | collective-permute-start | bytes 3538952 | tf_op jit(solution)/shard_map/ppermute | solution.py:289
  88.5 50.0 %collective-permute-start.8 = (bf16[768,768]{1,0:T(8,128)(2,1)}, bf16[768,768]{1,0:T(8,128)(2,1)}, u32[]{:S(2)}, u32[]{:S(2)}) collective-permute-start(bf16[768,768]{1,0:T(8,128)(2,1)} %collective-permute-done.7), channel_id=1, source_target_pairs={{0,2},{2,0},{4,6},{6,4},{8,10},{10,8},{12,14},{14,12},{16,18},{18,... | collective-permute-start | bytes 3538952 | tf_op jit(solution)/shard_map/ppermute | solution.py:289
  143.5 34.0 %copy-start.15 = (bf16[1536,768]{1,0:T(8,128)(2,1)}, bf16[1536,768]{1,0:T(8,128)(2,1)S(1)}, u32[]{:S(2)}) copy-start(bf16[1536,768]{1,0:T(8,128)(2,1)S(1)} %get-tuple-element.108) | copy-start | bytes 7077892
  281.8 69.4 %collective-permute-start.9 = (bf16[768,1152]{1,0:T(8,128)(2,1)}, bf16[768,1152]{1,0:T(8,128)(2,1)}, u32[]{:S(2)}, u32[]{:S(2)}) collective-permute-start(bf16[768,1152]{1,0:T(8,128)(2,1)} %fusion.17), channel_id=1, source_target_pairs={{0,2},{2,0},{4,6},{6,4},{8,10},{10,8},{12,14},{14,12},{16,18},{18,... | collective-permute-start | bytes 5308424 | tf_op jit(solution)/shard_map/ppermute | solution.py:289
  297.8 13.8 %collective-permute-start.21 = (f32[36,128]{1,0:T(8,128)S(1)}, f32[36,128]{1,0:T(8,128)S(1)}, u32[]{:S(2)}, u32[]{:S(2)}) collective-permute-start(f32[36,128]{1,0:T(8,128)S(1)} %dynamic-slice_bitcast_fusion), channel_id=1, source_target_pairs={{0,1},{1,0},{2,3},{3,2},{4,5},{5,4},{6,7},{7,6},{8,9},{9,8},{10,11... | collective-permute-start | bytes 55304 | tf_op jit(solution)/shard_map/ppermute | solution.py:289
  297.8 21.3 %collective-permute-start.26 = (bf16[768,384]{1,0:T(8,128)(2,1)}, bf16[768,384]{1,0:T(8,128)(2,1)S(1)}, u32[]{:S(2)}, u32[]{:S(2)}) collective-permute-start(bf16[768,384]{1,0:T(8,128)(2,1)} %convolution_convert_fusion.4), channel_id=1, source_target_pairs={{0,2},{2,0},{4,6},{6,4},{8,10},{10,8},{12,14},{14,12},{16,18},{18,... | collective-permute-start | bytes 1769480 | tf_op jit(solution)/shard_map/ppermute | solution.py:289
  311.6 4.4 collective-permute-start.22
  316.0 2.9 collective-permute-start.23
  318.9 6.2 %collective-permute-start.24 = (f32[36,128]{1,0:T(8,128)S(1)}, f32[36,128]{1,0:T(8,128)S(1)}, u32[]{:S(2)}, u32[]{:S(2)}) collective-permute-start(f32[36,128]{1,0:T(8,128)S(1)} %add.393), channel_id=1, source_target_pairs={{0,8},{2,10},{4,12},{6,14},{8,0},{10,2},{12,4},{14,6},{16,24},{18,... | collective-permute-start | bytes 55304 | tf_op jit(solution)/shard_map/ppermute | solution.py:289
  319.2 8.3 %collective-permute-start.27 = (bf16[384,384]{1,0:T(8,128)(2,1)S(1)}, bf16[384,384]{1,0:T(8,128)(2,1)S(1)}, u32[]{:S(2)}, u32[]{:S(2)}) collective-permute-start(bf16[384,384]{1,0:T(8,128)(2,1)S(1)} %add_convert_fusion.17), channel_id=1, source_target_pairs={{0,1},{1,0},{2,3},{3,2},{4,5},{5,4},{6,7},{7,6},{8,9},{9,8},{10,11... | collective-permute-start | bytes 884744 | tf_op jit(solution)/shard_map/ppermute | solution.py:289
  325.7 14.0 %collective-permute-start.25 = (f32[36,128]{1,0:T(8,128)}, f32[36,128]{1,0:T(8,128)}, u32[]{:S(2)}, u32[]{:S(2)}) collective-permute-start(f32[36,128]{1,0:T(8,128)} %add.394), channel_id=1, source_target_pairs={{0,16},{2,18},{4,20},{6,22},{8,24},{10,26},{12,28},{14,30},{16,0},... | collective-permute-start | bytes 55304 | tf_op jit(solution)/shard_map/ppermute | solution.py:289
  328.4 12.1 %collective-permute-start.28 = (bf16[192,384]{1,0:T(8,128)(2,1)}, bf16[192,384]{1,0:T(8,128)(2,1)}, u32[]{:S(2)}, u32[]{:S(2)}) collective-permute-start(bf16[192,384]{1,0:T(8,128)(2,1)} %constant_dynamic-slice_fusion.10), channel_id=1, source_target_pairs={{0,4},{2,6},{4,0},{6,2},{8,12},{10,14},{12,8},{14,10},{16,20},{18,... | collective-permute-start | bytes 442376 | tf_op jit(solution)/shard_map/ppermute | solution.py:289
  337.2 50.1 %collective-permute-start.38 = (bf16[768,1536]{1,0:T(8,128)(2,1)}, bf16[768,1536]{1,0:T(8,128)(2,1)S(1)}, u32[]{:S(2)}, u32[]{:S(2)}) collective-permute-start(bf16[768,1536]{1,0:T(8,128)(2,1)} %convolution_convert_fusion.1), channel_id=1, source_target_pairs={{0,2},{2,0},{4,6},{6,4},{8,10},{10,8},{12,14},{14,12},{16,18},{18,... | collective-permute-start | bytes 7077896 | tf_op jit(solution)/shard_map/ppermute | solution.py:289
  341.5 4.5 collective-permute-start.31
  343.1 4.3 collective-permute-start.30
  345.4 3.1 collective-permute-start.29
  348.5 5.1 collective-permute-start.32
  349.7 6.6 %collective-permute-start.33 = (bf16[48,384]{1,0:T(8,128)(2,1)S(1)}, bf16[48,384]{1,0:T(8,128)(2,1)S(1)}, u32[]{:S(2)}, u32[]{:S(2)}) collective-permute-start(bf16[48,384]{1,0:T(8,128)(2,1)S(1)} %add_convert_fusion.23), channel_id=1, source_target_pairs={{0,16},{2,18},{4,20},{6,22},{8,24},{10,26},{12,28},{14,30},{16,0},... | collective-permute-start | bytes 110600 | tf_op jit(solution)/shard_map/ppermute | solution.py:289
  350.0 6.3 %collective-permute-start.34 = (bf16[48,384]{1,0:T(8,128)(2,1)S(1)}, bf16[48,384]{1,0:T(8,128)(2,1)S(1)}, u32[]{:S(2)}, u32[]{:S(2)}) collective-permute-start(bf16[48,384]{1,0:T(8,128)(2,1)S(1)} %add_convert_fusion.23), channel_id=1, source_target_pairs={{0,24},{2,26},{4,28},{6,30},{8,16},{10,18},{12,20},{14,22},{16,8},... | collective-permute-start | bytes 110600 | tf_op jit(solution)/shard_map/ppermute | solution.py:289
  351.2 36.2 %slice-start.2 = ((s8[4718592]{0:T(1024)(128)(4,1)}), s8[4194304]{0:T(1024)(128)(4,1)S(1)}, s32[]{:S(2)}) async-start(s8[4718592]{0:T(1024)(128)(4,1)} %bitcast.78), calls=%async_computation.2 | async-start | bytes 8388608
  352.7 18.8 %collective-permute-start.10 = (bf16[384,1152]{1,0:T(8,128)(2,1)S(1)}, bf16[384,1152]{1,0:T(8,128)(2,1)S(1)}, u32[]{:S(2)}, u32[]{:S(2)}) collective-permute-start(bf16[384,1152]{1,0:T(8,128)(2,1)S(1)} %fusion.19), channel_id=1, source_target_pairs={{0,1},{1,0},{2,3},{3,2},{4,5},{5,4},{6,7},{7,6},{8,9},{9,8},{10,11... | collective-permute-start | bytes 2654216 | tf_op jit(solution)/shard_map/ppermute | solution.py:289
  353.6 44.1 %collective-permute-start.50 = (bf16[3072,384]{1,0:T(8,128)(2,1)S(1)}, bf16[3072,384]{1,0:T(8,128)(2,1)S(1)}, u32[]{:S(2)}, u32[]{:S(2)}) collective-permute-start(bf16[3072,384]{1,0:T(8,128)(2,1)S(1)} %copy-done.50), channel_id=1, source_target_pairs={{0,2},{2,0},{4,6},{6,4},{8,10},{10,8},{12,14},{14,12},{16,18},{18,... | collective-permute-start | bytes 7077896 | tf_op jit(solution)/shard_map/ppermute | solution.py:289
  356.4 5.5 %collective-permute-start.35 = (bf16[192,384]{1,0:T(8,128)(2,1)S(1)}, bf16[192,384]{1,0:T(8,128)(2,1)S(1)}, u32[]{:S(2)}, u32[]{:S(2)}) collective-permute-start(bf16[192,384]{1,0:T(8,128)(2,1)S(1)} %pad_maximum_fusion.27), channel_id=1, source_target_pairs={{0,4},{2,6},{4,0},{6,2},{8,12},{10,14},{12,8},{14,10},{16,20},{18,... | collective-permute-start | bytes 442376 | tf_op jit(solution)/shard_map/ppermute | solution.py:289
  358.2 16.0 %collective-permute-start.36 = (bf16[192,384]{1,0:T(8,128)(2,1)S(1)}, bf16[192,384]{1,0:T(8,128)(2,1)S(1)}, u32[]{:S(2)}, u32[]{:S(2)}) collective-permute-start(bf16[192,384]{1,0:T(8,128)(2,1)S(1)} %pad_maximum_fusion.27), channel_id=1, source_target_pairs={{0,2},{2,0},{4,6},{6,4},{8,10},{10,8},{12,14},{14,12},{16,18},{18,... | collective-permute-start | bytes 442376 | tf_op jit(solution)/shard_map/ppermute | solution.py:289
  361.9 12.3 %collective-permute-start.37 = (bf16[192,384]{1,0:T(8,128)(2,1)S(1)}, bf16[192,384]{1,0:T(8,128)(2,1)S(1)}, u32[]{:S(2)}, u32[]{:S(2)}) collective-permute-start(bf16[192,384]{1,0:T(8,128)(2,1)S(1)} %collective-permute-done.35), channel_id=1, source_target_pairs={{0,2},{2,0},{4,6},{6,4},{8,10},{10,8},{12,14},{14,12},{16,18},{18,... | collective-permute-start | bytes 442376 | tf_op jit(solution)/shard_map/ppermute | solution.py:289
  373.2 8.4 %collective-permute-start.11 = (bf16[192,1152]{1,0:T(8,128)(2,1)S(1)}, bf16[192,1152]{1,0:T(8,128)(2,1)S(1)}, u32[]{:S(2)}, u32[]{:S(2)}) collective-permute-start(bf16[192,1152]{1,0:T(8,128)(2,1)S(1)} %constant_dynamic-slice_fusion.15), channel_id=1, source_target_pairs={{0,4},{2,6},{4,0},{6,2},{8,12},{10,14},{12,8},{14,10},{16,20},{18,... | collective-permute-start | bytes 1327112 | tf_op jit(solution)/shard_map/ppermute | solution.py:289
  381.8 7.1 %collective-permute-start.14 = (bf16[48,1152]{1,0:T(8,128)(2,1)S(1)}, bf16[48,1152]{1,0:T(8,128)(2,1)S(1)}, u32[]{:S(2)}, u32[]{:S(2)}) collective-permute-start(bf16[48,1152]{1,0:T(8,128)(2,1)S(1)} %get-tuple-element.164), channel_id=1, source_target_pairs={{0,24},{2,26},{4,28},{6,30},{8,16},{10,18},{12,20},{14,22},{16,8},... | collective-permute-start | bytes 331784 | tf_op jit(solution)/shard_map/ppermute | solution.py:289
  382.8 10.7 %collective-permute-start.13 = (bf16[48,1152]{1,0:T(8,128)(2,1)S(1)}, bf16[48,1152]{1,0:T(8,128)(2,1)S(1)}, u32[]{:S(2)}, u32[]{:S(2)}) collective-permute-start(bf16[48,1152]{1,0:T(8,128)(2,1)S(1)} %get-tuple-element.165), channel_id=1, source_target_pairs={{0,16},{2,18},{4,20},{6,22},{8,24},{10,26},{12,28},{14,30},{16,0},... | collective-permute-start | bytes 331784 | tf_op jit(solution)/shard_map/ppermute | solution.py:289
  387.4 6.1 %collective-permute-start.12 = (bf16[48,1152]{1,0:T(8,128)(2,1)S(1)}, bf16[48,1152]{1,0:T(8,128)(2,1)S(1)}, u32[]{:S(2)}, u32[]{:S(2)}) collective-permute-start(bf16[48,1152]{1,0:T(8,128)(2,1)S(1)} %get-tuple-element.163), channel_id=1, source_target_pairs={{0,8},{2,10},{4,12},{6,14},{8,0},{10,2},{12,4},{14,6},{16,24},{18,... | collective-permute-start | bytes 331784 | tf_op jit(solution)/shard_map/ppermute | solution.py:289
  387.8 24.0 %collective-permute-start.39 = (bf16[384,1536]{1,0:T(8,128)(2,1)S(1)}, bf16[384,1536]{1,0:T(8,128)(2,1)S(1)}, u32[]{:S(2)}, u32[]{:S(2)}) collective-permute-start(bf16[384,1536]{1,0:T(8,128)(2,1)S(1)} %add_convert_fusion.10), channel_id=1, source_target_pairs={{0,1},{1,0},{2,3},{3,2},{4,5},{5,4},{6,7},{7,6},{8,9},{9,8},{10,11... | collective-permute-start | bytes 3538952 | tf_op jit(solution)/shard_map/ppermute | solution.py:289
  393.6 6.2 %collective-permute-start.15 = (bf16[48,1152]{1,0:T(8,128)(2,1)S(1)}, bf16[48,1152]{1,0:T(8,128)(2,1)S(1)}, u32[]{:S(2)}, u32[]{:S(2)}) collective-permute-start(bf16[48,1152]{1,0:T(8,128)(2,1)S(1)} %add_convert_fusion.22), channel_id=1, source_target_pairs={{0,8},{2,10},{4,12},{6,14},{8,0},{10,2},{12,4},{14,6},{16,24},{18,... | collective-permute-start | bytes 331784 | tf_op jit(solution)/shard_map/ppermute | solution.py:289
  396.5 5.5 %collective-permute-start.16 = (bf16[48,1152]{1,0:T(8,128)(2,1)S(1)}, bf16[48,1152]{1,0:T(8,128)(2,1)S(1)}, u32[]{:S(2)}, u32[]{:S(2)}) collective-permute-start(bf16[48,1152]{1,0:T(8,128)(2,1)S(1)} %add_convert_fusion.22), channel_id=1, source_target_pairs={{0,16},{2,18},{4,20},{6,22},{8,24},{10,26},{12,28},{14,30},{16,0},... | collective-permute-start | bytes 331784 | tf_op jit(solution)/shard_map/ppermute | solution.py:289
  396.8 9.9 %collective-permute-start.17 = (bf16[48,1152]{1,0:T(8,128)(2,1)S(1)}, bf16[48,1152]{1,0:T(8,128)(2,1)S(1)}, u32[]{:S(2)}, u32[]{:S(2)}) collective-permute-start(bf16[48,1152]{1,0:T(8,128)(2,1)S(1)} %add_convert_fusion.22), channel_id=1, source_target_pairs={{0,24},{2,26},{4,28},{6,30},{8,16},{10,18},{12,20},{14,22},{16,8},... | collective-permute-start | bytes 331784 | tf_op jit(solution)/shard_map/ppermute | solution.py:289
  398.1 38.4 %collective-permute-start.51 = (bf16[1536,384]{1,0:T(8,128)(2,1)S(1)}, bf16[1536,384]{1,0:T(8,128)(2,1)S(1)}, u32[]{:S(2)}, u32[]{:S(2)}) collective-permute-start(bf16[1536,384]{1,0:T(8,128)(2,1)S(1)} %add_convert_fusion.7), channel_id=1, source_target_pairs={{0,1},{1,0},{2,3},{3,2},{4,5},{5,4},{6,7},{7,6},{8,9},{9,8},{10,11... | collective-permute-start | bytes 3538952 | tf_op jit(solution)/shard_map/ppermute | solution.py:289
  407.6 32.0 %collective-permute-start.18 = (bf16[192,1152]{1,0:T(8,128)(2,1)}, bf16[192,1152]{1,0:T(8,128)(2,1)S(1)}, u32[]{:S(2)}, u32[]{:S(2)}) collective-permute-start(bf16[192,1152]{1,0:T(8,128)(2,1)} %pad_maximum_fusion.24), channel_id=1, source_target_pairs={{0,4},{2,6},{4,0},{6,2},{8,12},{10,14},{12,8},{14,10},{16,20},{18,... | collective-permute-start | bytes 1327112 | tf_op jit(solution)/shard_map/ppermute | solution.py:289
  409.3 48.2 %collective-permute-start.19 = (bf16[192,1152]{1,0:T(8,128)(2,1)}, bf16[192,1152]{1,0:T(8,128)(2,1)}, u32[]{:S(2)}, u32[]{:S(2)}) collective-permute-start(bf16[192,1152]{1,0:T(8,128)(2,1)} %pad_maximum_fusion.24), channel_id=1, source_target_pairs={{0,2},{2,0},{4,6},{6,4},{8,10},{10,8},{12,14},{14,12},{16,18},{18,... | collective-permute-start | bytes 1327112 | tf_op jit(solution)/shard_map/ppermute | solution.py:289
  413.1 36.8 %collective-permute-start.40 = (bf16[192,1536]{1,0:T(8,128)(2,1)}, bf16[192,1536]{1,0:T(8,128)(2,1)}, u32[]{:S(2)}, u32[]{:S(2)}) collective-permute-start(bf16[192,1536]{1,0:T(8,128)(2,1)} %constant_dynamic-slice_fusion.6), channel_id=1, source_target_pairs={{0,4},{2,6},{4,0},{6,2},{8,12},{10,14},{12,8},{14,10},{16,20},{18,... | collective-permute-start | bytes 1769480 | tf_op jit(solution)/shard_map/ppermute | solution.py:289
  437.8 17.7 %collective-permute-start.52 = (bf16[768,384]{1,0:T(8,128)(2,1)}, bf16[768,384]{1,0:T(8,128)(2,1)}, u32[]{:S(2)}, u32[]{:S(2)}) collective-permute-start(bf16[768,384]{1,0:T(8,128)(2,1)} %constant_dynamic-slice_fusion.2), channel_id=1, source_target_pairs={{0,4},{2,6},{4,0},{6,2},{8,12},{10,14},{12,8},{14,10},{16,20},{18,... | collective-permute-start | bytes 1769480 | tf_op jit(solution)/shard_map/ppermute | solution.py:289
  442.3 15.5 %collective-permute-start.20 = (bf16[192,1152]{1,0:T(8,128)(2,1)}, bf16[192,1152]{1,0:T(8,128)(2,1)S(1)}, u32[]{:S(2)}, u32[]{:S(2)}) collective-permute-start(bf16[192,1152]{1,0:T(8,128)(2,1)} %copy-done.39), channel_id=1, source_target_pairs={{0,2},{2,0},{4,6},{6,4},{8,10},{10,8},{12,14},{14,12},{16,18},{18,... | collective-permute-start | bytes 1327112 | tf_op jit(solution)/shard_map/ppermute | solution.py:289
  451.9 13.3 %collective-permute-start.43 = (bf16[48,1536]{1,0:T(8,128)(2,1)}, bf16[48,1536]{1,0:T(8,128)(2,1)}, u32[]{:S(2)}, u32[]{:S(2)}) collective-permute-start(bf16[48,1536]{1,0:T(8,128)(2,1)} %get-tuple-element.153), channel_id=1, source_target_pairs={{0,24},{2,26},{4,28},{6,30},{8,16},{10,18},{12,20},{14,22},{16,8},... | collective-permute-start | bytes 442376 | tf_op jit(solution)/shard_map/ppermute | solution.py:289
  452.2 19.3 %collective-permute-start.42 = (bf16[48,1536]{1,0:T(8,128)(2,1)}, bf16[48,1536]{1,0:T(8,128)(2,1)}, u32[]{:S(2)}, u32[]{:S(2)}) collective-permute-start(bf16[48,1536]{1,0:T(8,128)(2,1)} %get-tuple-element.154), channel_id=1, source_target_pairs={{0,16},{2,18},{4,20},{6,22},{8,24},{10,26},{12,28},{14,30},{16,0},... | collective-permute-start | bytes 442376 | tf_op jit(solution)/shard_map/ppermute | solution.py:289
  455.5 16.0 %collective-permute-start.41 = (bf16[48,1536]{1,0:T(8,128)(2,1)}, bf16[48,1536]{1,0:T(8,128)(2,1)}, u32[]{:S(2)}, u32[]{:S(2)}) collective-permute-start(bf16[48,1536]{1,0:T(8,128)(2,1)} %get-tuple-element.152), channel_id=1, source_target_pairs={{0,8},{2,10},{4,12},{6,14},{8,0},{10,2},{12,4},{14,6},{16,24},{18,... | collective-permute-start | bytes 442376 | tf_op jit(solution)/shard_map/ppermute | solution.py:289
  457.5 19.2 %collective-permute-start.55 = (bf16[192,384]{1,0:T(8,128)(2,1)}, bf16[192,384]{1,0:T(8,128)(2,1)}, u32[]{:S(2)}, u32[]{:S(2)}) collective-permute-start(bf16[192,384]{1,0:T(8,128)(2,1)} %get-tuple-element.146), channel_id=1, source_target_pairs={{0,24},{2,26},{4,28},{6,30},{8,16},{10,18},{12,20},{14,22},{16,8},... | collective-permute-start | bytes 442376 | tf_op jit(solution)/shard_map/ppermute | solution.py:289
  457.8 20.2 %collective-permute-start.54 = (bf16[192,384]{1,0:T(8,128)(2,1)}, bf16[192,384]{1,0:T(8,128)(2,1)}, u32[]{:S(2)}, u32[]{:S(2)}) collective-permute-start(bf16[192,384]{1,0:T(8,128)(2,1)} %get-tuple-element.147), channel_id=1, source_target_pairs={{0,16},{2,18},{4,20},{6,22},{8,24},{10,26},{12,28},{14,30},{16,0},... | collective-permute-start | bytes 442376 | tf_op jit(solution)/shard_map/ppermute | solution.py:289
  465.2 12.8 %collective-permute-start.53 = (bf16[192,384]{1,0:T(8,128)(2,1)}, bf16[192,384]{1,0:T(8,128)(2,1)S(1)}, u32[]{:S(2)}, u32[]{:S(2)}) collective-permute-start(bf16[192,384]{1,0:T(8,128)(2,1)} %get-tuple-element.145), channel_id=1, source_target_pairs={{0,8},{2,10},{4,12},{6,14},{8,0},{10,2},{12,4},{14,6},{16,24},{18,... | collective-permute-start | bytes 442376 | tf_op jit(solution)/shard_map/ppermute | solution.py:289
  472.7 10.4 %collective-permute-start.44 = (bf16[48,1536]{1,0:T(8,128)(2,1)S(1)}, bf16[48,1536]{1,0:T(8,128)(2,1)S(1)}, u32[]{:S(2)}, u32[]{:S(2)}) collective-permute-start(bf16[48,1536]{1,0:T(8,128)(2,1)S(1)} %add_convert_fusion.20), channel_id=1, source_target_pairs={{0,8},{2,10},{4,12},{6,14},{8,0},{10,2},{12,4},{14,6},{16,24},{18,... | collective-permute-start | bytes 442376 | tf_op jit(solution)/shard_map/ppermute | solution.py:289
  476.0 11.1 %collective-permute-start.45 = (bf16[48,1536]{1,0:T(8,128)(2,1)S(1)}, bf16[48,1536]{1,0:T(8,128)(2,1)S(1)}, u32[]{:S(2)}, u32[]{:S(2)}) collective-permute-start(bf16[48,1536]{1,0:T(8,128)(2,1)S(1)} %add_convert_fusion.20), channel_id=1, source_target_pairs={{0,16},{2,18},{4,20},{6,22},{8,24},{10,26},{12,28},{14,30},{16,0},... | collective-permute-start | bytes 442376 | tf_op jit(solution)/shard_map/ppermute | solution.py:289
  476.7 22.1 %collective-permute-start.46 = (bf16[48,1536]{1,0:T(8,128)(2,1)S(1)}, bf16[48,1536]{1,0:T(8,128)(2,1)S(1)}, u32[]{:S(2)}, u32[]{:S(2)}) collective-permute-start(bf16[48,1536]{1,0:T(8,128)(2,1)S(1)} %add_convert_fusion.20), channel_id=1, source_target_pairs={{0,24},{2,26},{4,28},{6,30},{8,16},{10,18},{12,20},{14,22},{16,8},... | collective-permute-start | bytes 442376 | tf_op jit(solution)/shard_map/ppermute | solution.py:289
  479.1 20.8 %collective-permute-start.56 = (bf16[192,384]{1,0:T(8,128)(2,1)S(1)}, bf16[192,384]{1,0:T(8,128)(2,1)S(1)}, u32[]{:S(2)}, u32[]{:S(2)}) collective-permute-start(bf16[192,384]{1,0:T(8,128)(2,1)S(1)} %add_convert_fusion.19), channel_id=1, source_target_pairs={{0,8},{2,10},{4,12},{6,14},{8,0},{10,2},{12,4},{14,6},{16,24},{18,... | collective-permute-start | bytes 442376 | tf_op jit(solution)/shard_map/ppermute | solution.py:289
  482.4 17.6 %collective-permute-start.57 = (bf16[192,384]{1,0:T(8,128)(2,1)S(1)}, bf16[192,384]{1,0:T(8,128)(2,1)S(1)}, u32[]{:S(2)}, u32[]{:S(2)}) collective-permute-start(bf16[192,384]{1,0:T(8,128)(2,1)S(1)} %add_convert_fusion.19), channel_id=1, source_target_pairs={{0,16},{2,18},{4,20},{6,22},{8,24},{10,26},{12,28},{14,30},{16,0},... | collective-permute-start | bytes 442376 | tf_op jit(solution)/shard_map/ppermute | solution.py:289
  483.1 22.2 %collective-permute-start.58 = (bf16[192,384]{1,0:T(8,128)(2,1)S(1)}, bf16[192,384]{1,0:T(8,128)(2,1)S(1)}, u32[]{:S(2)}, u32[]{:S(2)}) collective-permute-start(bf16[192,384]{1,0:T(8,128)(2,1)S(1)} %add_convert_fusion.19), channel_id=1, source_target_pairs={{0,24},{2,26},{4,28},{6,30},{8,16},{10,18},{12,20},{14,22},{16,8},... | collective-permute-start | bytes 442376 | tf_op jit(solution)/shard_map/ppermute | solution.py:289
  499.9 19.4 %collective-permute-start.47 = (bf16[192,1536]{1,0:T(8,128)(2,1)}, bf16[192,1536]{1,0:T(8,128)(2,1)}, u32[]{:S(2)}, u32[]{:S(2)}) collective-permute-start(bf16[192,1536]{1,0:T(8,128)(2,1)} %pad_maximum_fusion.22), channel_id=1, source_target_pairs={{0,4},{2,6},{4,0},{6,2},{8,12},{10,14},{12,8},{14,10},{16,20},{18,... | collective-permute-start | bytes 1769480 | tf_op jit(solution)/shard_map/ppermute | solution.py:289
  506.4 20.1 %collective-permute-start.59 = (bf16[768,384]{1,0:T(8,128)(2,1)}, bf16[768,384]{1,0:T(8,128)(2,1)}, u32[]{:S(2)}, u32[]{:S(2)}) collective-permute-start(bf16[768,384]{1,0:T(8,128)(2,1)} %pad_maximum_fusion.23), channel_id=1, source_target_pairs={{0,4},{2,6},{4,0},{6,2},{8,12},{10,14},{12,8},{14,10},{16,20},{18,... | collective-permute-start | bytes 1769480 | tf_op jit(solution)/shard_map/ppermute | solution.py:289
  518.5 13.0 %collective-permute-start.48 = (bf16[192,1536]{1,0:T(8,128)(2,1)}, bf16[192,1536]{1,0:T(8,128)(2,1)S(1)}, u32[]{:S(2)}, u32[]{:S(2)}) collective-permute-start(bf16[192,1536]{1,0:T(8,128)(2,1)} %pad_maximum_fusion.22), channel_id=1, source_target_pairs={{0,2},{2,0},{4,6},{6,4},{8,10},{10,8},{12,14},{14,12},{16,18},{18,... | collective-permute-start | bytes 1769480 | tf_op jit(solution)/shard_map/ppermute | solution.py:289
  519.3 15.5 %collective-permute-start.60 = (bf16[768,384]{1,0:T(8,128)(2,1)}, bf16[768,384]{1,0:T(8,128)(2,1)S(1)}, u32[]{:S(2)}, u32[]{:S(2)}) collective-permute-start(bf16[768,384]{1,0:T(8,128)(2,1)} %pad_maximum_fusion.23), channel_id=1, source_target_pairs={{0,2},{2,0},{4,6},{6,4},{8,10},{10,8},{12,14},{14,12},{16,18},{18,... | collective-permute-start | bytes 1769480 | tf_op jit(solution)/shard_map/ppermute | solution.py:289
  519.4 12.2 %collective-permute-start.49 = (bf16[192,1536]{1,0:T(8,128)(2,1)}, bf16[192,1536]{1,0:T(8,128)(2,1)S(1)}, u32[]{:S(2)}, u32[]{:S(2)}) collective-permute-start(bf16[192,1536]{1,0:T(8,128)(2,1)} %collective-permute-done.47), channel_id=1, source_target_pairs={{0,2},{2,0},{4,6},{6,4},{8,10},{10,8},{12,14},{14,12},{16,18},{18,... | collective-permute-start | bytes 1769480 | tf_op jit(solution)/shard_map/ppermute | solution.py:289
  526.5 8.3 %collective-permute-start.61 = (bf16[768,384]{1,0:T(8,128)(2,1)}, bf16[768,384]{1,0:T(8,128)(2,1)S(1)}, u32[]{:S(2)}, u32[]{:S(2)}) collective-permute-start(bf16[768,384]{1,0:T(8,128)(2,1)} %collective-permute-done.59), channel_id=1, source_target_pairs={{0,2},{2,0},{4,6},{6,4},{8,10},{10,8},{12,14},{14,12},{16,18},{18,... | collective-permute-start | bytes 1769480 | tf_op jit(solution)/shard_map/ppermute | solution.py:289
  (62 other events, 519.1 us)

commit v2 on v1

v2 whole, which is shorter than its diff:
```python
import functools

import jax
import jax.numpy as jnp
from jax import lax
from jax.experimental import pallas as pl
from jax.experimental.pallas import tpu as pltpu
from jax.sharding import PartitionSpec as P

D = 768
FF = 3072
HEADS = 12
HEAD_DIM = 64
LEN = 1024
PAIRS = HEADS // 2
HALF_PAIRS = PAIRS // 2
WIDE = 2 * HEAD_DIM
TRIPLE = 3 * WIDE
KEY_TILE = 128
FORWARD_ROWS = 128
BACKWARD_ROWS = 256
TOKEN_ROWS = 256
CHUNK = 384
BIG = float(2**30)
EPSILON = 1e-12
F32 = jnp.float32
LOW = jnp.bfloat16
B_QV, B_OUT, ATTN_GAIN, ATTN_SHIFT = 0, 2 * D, 3 * D, 4 * D
B_UP, B_DOWN, FFN_GAIN, FFN_SHIFT = 5 * D, 5 * D + FF, 6 * D + FF, 7 * D + FF
VECTORS = 8 * D + FF
CORE, X, Z, Y = 0, 1, 2, 3


def matmul(left, right):
    return jnp.dot(left, right, preferred_element_type=F32)


def matmul_right_t(left, right):
    return lax.dot_general(left, right, (((1,), (1,)), ((), ())), preferred_element_type=F32)


def matmul_left_t(left, right):
    return lax.dot_general(left, right, (((0,), (0,)), ((), ())), preferred_element_type=F32)


def as_float(value):
    return value.astype(F32)


def rounded(value):
    return value.astype(LOW)


def shape(dims, kind=LOW):
    return jax.ShapeDtypeStruct(dims, kind)


def constant(dims):
    return pl.BlockSpec(dims, lambda *at: (0,) * len(dims))


def tokens(width):
    return pl.BlockSpec((TOKEN_ROWS, width), lambda i, *place: (i, 0))


ANYWHERE = pl.BlockSpec(memory_space=pl.ANY)


def call(body, name, out_shape, grid, in_specs, out_specs, scratch=(), flops=0, exps=0):
    return pl.pallas_call(
        body,
        out_shape=out_shape,
        grid_spec=pltpu.PrefetchScalarGridSpec(
            num_scalar_prefetch=1,
            grid=grid,
            in_specs=in_specs,
            out_specs=out_specs,
            scratch_shapes=list(scratch),
        ),
        cost_estimate=pl.CostEstimate(flops=flops, transcendentals=exps, bytes_accessed=1 << 20),
        name=name,
    )


def piece_rows(place, count, own_rows):
    half = own_rows // 2
    core, y = place[CORE], place[Y]
    found = [pl.multiple_of(y * own_rows, half)]
    for d in range(1, (count + 1) // 2):
        base = jnp.bitwise_xor(y, d) * own_rows
        found.append(pl.multiple_of(base + core * half, half))
        found.append(pl.multiple_of(base + (1 - core) * half, half))
    return found


def assemble(place, pieces, buffer, semaphores):
    starts = piece_rows(place, len(pieces), pieces[0].shape[0])
    return [
        pltpu.make_async_copy(
            piece, buffer.at[pl.ds(start, piece.shape[0]), :], semaphores.at[at]
        )
        for at, (piece, start) in enumerate(zip(pieces, starts))
    ]


def start_all(copies):
    for copy in copies:
        copy.start()


def wait_all(copies):
    for copy in copies:
        copy.wait()


def project_body(place, inputs, vectors, *refs):
    pieces, (projected, weight) = refs[:-2], refs[-2:]
    count = len(pieces) // 3
    starts = piece_rows(place, count, pieces[0].shape[0])
    for part in range(3):
        for at in range(count):
            block = pieces[part * count + at]
            rows = pl.ds(starts[at], block.shape[0])
            for j in range(2):
                lanes = slice(j * TRIPLE + part * WIDE, j * TRIPLE + (part + 1) * WIDE)
                weight[rows, lanes] = block[:, j * WIDE : (j + 1) * WIDE]
    first = pl.program_id(0) * 2 * WIDE
    bias = []
    for j in range(2):
        at = pl.multiple_of(first + j * WIDE, WIDE)
        bias.append(vectors[:, pl.ds(B_QV + at, WIDE)])
        bias.append(jnp.zeros((1, WIDE), F32))
        bias.append(vectors[:, pl.ds(B_QV + D + at, WIDE)])
    bias = jnp.concatenate(bias, axis=1)
    projected[...] = rounded(matmul(inputs[...], weight[...]) + bias)


def project(place, inputs, vectors, pieces):
    steps = PAIRS // 2
    column = pl.BlockSpec((LEN, 2 * TRIPLE), lambda i, p: (0, i))
    specs, operands = [], []
    for part in range(3):
        for piece in pieces:
            specs.append(
                pl.BlockSpec(
                    (piece.shape[0], 2 * WIDE), lambda i, p, part=part: (0, part * steps + i)
                )
            )
            operands.append(piece)
    return call(
        project_body,
        "project",
        (shape((LEN, 3 * D)), shape((D, 3 * D))),
        (steps,),
        [constant((LEN, D)), constant((1, VECTORS))] + specs,
        [column, pl.BlockSpec((D, 2 * TRIPLE), lambda i, p: (0, i))],
        flops=2 * LEN * D * 3 * D,
    )(place, inputs, vectors, *operands)


def key_ranges(segments, rows):
    tiles = segments.reshape(LEN // rows, rows)
    below = jnp.sum(segments[None, :] < tiles[:, :1], axis=1, dtype=jnp.int32)
    upto = jnp.sum(segments[None, :] <= tiles[:, -1:], axis=1, dtype=jnp.int32)
    start = below // KEY_TILE
    count = (upto + KEY_TILE - 1) // KEY_TILE - start
    return jnp.concatenate([start, count])
def document_features(segments):
    lane = jnp.arange(WIDE, dtype=jnp.int32) % HEAD_DIM
    hot = segments[:, None] == lane[None, :]
    q = jnp.where((lane < 16) & hot, 1.0, 0.0).astype(LOW)
    k = jnp.where(lane < 16, jnp.where(hot, 0.0, -BIG), jnp.where(lane < 19, 1.0, 0.0)).astype(LOW)
    return q,k
def stack_heads(pair, side_a, side_b, left):
    zero=jnp.zeros_like(pair)
    a=jnp.concatenate([jnp.where(left,pair,zero),side_a],axis=1)
    b=jnp.concatenate([jnp.where(left,zero,pair),side_b],axis=1)
    return jnp.concatenate([a,b],axis=0)


def fwd_body(ranges, packed, feature_q, feature_k, context, log_total, key_side, value_t, *, group):
    tiles=LEN//FORWARD_ROWS
    for g in range(group):
        at=3*WIDE*g
        key_side[g,:,:WIDE]=packed[:,at+WIDE:at+2*WIDE]
        key_side[g,:,WIDE:]=feature_k[...]
        value_t[g,:WIDE,:]=packed[:,at+2*WIDE:at+3*WIDE].T
        value_t[g,WIDE:,:]=jnp.ones((16,LEN),LOW)
    left=lax.broadcasted_iota(jnp.int32,(FORWARD_ROWS,WIDE),1)<HEAD_DIM
    def tile(index,carry):
        here=pl.ds(pl.multiple_of(index*FORWARD_ROWS,FORWARD_ROWS),FORWARD_ROWS)
        side=feature_q[here,:]
        zero=jnp.zeros_like(side)
        sa=jnp.where(left,side,zero); sb=jnp.where(left,zero,side)
        stats=[stack_heads(packed[here,3*WIDE*g:3*WIDE*g+WIDE]*jnp.asarray(HEAD_DIM**-0.5,LOW),sa,sb,left) for g in range(group)]
        start=pl.multiple_of(ranges[index]*KEY_TILE,KEY_TILE)
        def over(width):
            def run():
                span=pl.ds(start,width)
                ss=[matmul_right_t(key_side[g,span,:],stats[g]) for g in range(group)]
                for g in range(group):
                    s=ss[g]
                    m=jnp.max(s,axis=0,keepdims=True)
                    p=jnp.exp(s-m).astype(LOW)
                    o=matmul(value_t[g,:,span],p)
                    total=o[WIDE:WIDE+1,:]
                    inv=1.0/total
                    lse=m+jnp.log(total)
                    log_total[g,0:1,here]=lse[:,:FORWARD_ROWS]
                    log_total[g,1:2,here]=lse[:,FORWARD_ROWS:]
                    both=jnp.concatenate([o[:HEAD_DIM,:FORWARD_ROWS]*inv[:,:FORWARD_ROWS],o[HEAD_DIM:WIDE,FORWARD_ROWS:]*inv[:,FORWARD_ROWS:]],axis=0)
                    context[here,g*WIDE:(g+1)*WIDE]=both.T.astype(LOW)
            return run
        lax.switch(ranges[tiles+index]-1,[over(KEY_TILE*(n+1)) for n in range(LEN//KEY_TILE)])
        return carry
    lax.fori_loop(0,tiles,tile,0)

def attn_fwd(r,packed,fq,fk,group=2):
    whole=pl.BlockSpec((LEN,WIDE),lambda h,r:(0,0))
    return pl.pallas_call(lambda *a: fwd_body(*a,group=group),
        out_shape=(jax.ShapeDtypeStruct((LEN,D),LOW),jax.ShapeDtypeStruct((PAIRS,2,LEN),F32)),
        grid_spec=pltpu.PrefetchScalarGridSpec(num_scalar_prefetch=1,grid=(PAIRS//group,),
          in_specs=[pl.BlockSpec((LEN,3*WIDE*group),lambda h,r:(0,h)),whole,whole],
          out_specs=[pl.BlockSpec((LEN,WIDE*group),lambda h,r:(0,h)),pl.BlockSpec((group,2,LEN),lambda h,r:(h,0,0))],
          scratch_shapes=[pltpu.VMEM((group,LEN,2*WIDE),LOW),pltpu.VMEM((group,WIDE+16,LEN),LOW)]),
        name="attention_forward")(r,packed,fq,fk)

def bwd_body(ranges,packed,context,d_context,log_total,feature_q,feature_k,d_packed,bias_sums,key_side,value_side,key_t,d_key,d_value,*,group):
    tiles=LEN//BACKWARD_ROWS
    lane=lax.broadcasted_iota(jnp.int32,(LEN,WIDE),1)
    ones=jnp.where(lane%HEAD_DIM<3,1.0,0.0).astype(LOW)
    for g in range(group):
        at=3*WIDE*g
        keys=packed[:,at+WIDE:at+2*WIDE]
        key_side[g,:,:WIDE]=keys
        key_side[g,:,WIDE:]=feature_k[...]
        value_side[g,:,:WIDE]=packed[:,at+2*WIDE:at+3*WIDE]
        value_side[g,:,WIDE:]=ones
        key_t[g]=keys.T
    d_key[...]=jnp.zeros_like(d_key); d_value[...]=jnp.zeros_like(d_value)
    lane_q=lax.broadcasted_iota(jnp.int32,(BACKWARD_ROWS,WIDE),1)
    left=lane_q<HEAD_DIM; inner=lane_q%HEAD_DIM
    zero=jnp.zeros((BACKWARD_ROWS,WIDE),LOW)
    def spread(value,base):
        high=as_float(value.astype(LOW)); rest=value-high
        middle=as_float(rest.astype(LOW)); tail=rest-middle
        return jnp.where(inner==base,high,jnp.where(inner==base+1,middle,jnp.where(inner==base+2,tail,0.0))).astype(LOW)
    def tile(index,sums):
        here=pl.ds(pl.multiple_of(index*BACKWARD_ROWS,BACKWARD_ROWS),BACKWARD_ROWS)
        hot=feature_q[here,:]
        qs=[];gs=[]
        for g in range(group):
            queries=packed[here,3*WIDE*g:3*WIDE*g+WIDE]*jnp.asarray(HEAD_DIM**-0.5,LOW)
            logs=log_total[g,:,here]
            cols=jnp.concatenate([logs,jnp.zeros((6,BACKWARD_ROWS),F32)],axis=0).T
            lse=jnp.where(left,cols[:,0:1],cols[:,1:2])
            side=hot+spread(-lse,16)
            qs.append(stack_heads(queries,jnp.where(left,side,zero),jnp.where(left,zero,side),left))
            grad=d_context[here,g*WIDE:(g+1)*WIDE]
            product=as_float(grad)*as_float(context[here,g*WIDE:(g+1)*WIDE])
            dot_a=jnp.sum(jnp.where(left,product,0.0),axis=1,keepdims=True)
            dot_b=jnp.sum(jnp.where(left,0.0,product),axis=1,keepdims=True)
            side_g=spread(-jnp.where(left,dot_a,dot_b),0)
            gs.append(stack_heads(grad,jnp.where(left,side_g,zero),jnp.where(left,zero,side_g),left))
        start=pl.multiple_of(ranges[index]*KEY_TILE,KEY_TILE)
        def over(width):
            def run():
                span=pl.ds(start,width)
                for g in range(group):
                    p=jnp.exp(matmul_right_t(key_side[g,span,:],qs[g]))
                    dp=matmul_right_t(value_side[g,span,:],gs[g])
                    pb=p.astype(LOW); ds=(p*dp).astype(LOW)
                    d_value[g,span,:]+=matmul(pb,gs[g][:,:WIDE])
                    d_key[g,span,:]+=matmul(ds,qs[g][:,:WIDE])
                    dq=matmul(key_t[g,:,span],ds)
                    dq=jnp.concatenate([dq[:HEAD_DIM,:BACKWARD_ROWS],dq[HEAD_DIM:,BACKWARD_ROWS:]],axis=0)
                    d_packed[here,3*WIDE*g:3*WIDE*g+WIDE]=(dq.T*HEAD_DIM**-0.5).astype(LOW)
            return run
        lax.switch(ranges[tiles+index]-1,[over(KEY_TILE*(n+1)) for n in range(LEN//KEY_TILE)])
        return tuple(sums[g]+jnp.sum(as_float(d_packed[here,3*WIDE*g:3*WIDE*g+WIDE]),axis=0,keepdims=True) for g in range(group))
    sums=lax.fori_loop(0,tiles,tile,(jnp.zeros((1,WIDE),F32),)*group)
    for g in range(group):
        at=3*WIDE*g
        low=d_value[g].astype(LOW)
        d_packed[:,at+WIDE:at+2*WIDE]=d_key[g].astype(LOW)
        d_packed[:,at+2*WIDE:at+3*WIDE]=low
        bias_sums[0:1,g*WIDE:(g+1)*WIDE]=sums[g]
        bias_sums[1:2,g*WIDE:(g+1)*WIDE]=jnp.sum(as_float(low),axis=0,keepdims=True)

def attn_bwd(r,packed,ctx,dctx,lse,fq,fk,pairs,group=2):
    whole=pl.BlockSpec((LEN,WIDE),lambda h,r:(0,0))
    last=r.shape[0]-1
    col=lambda w: pl.BlockSpec((LEN,w*group),lambda h,r:(0,r[last]+h))
    return pl.pallas_call(lambda *a: bwd_body(*a,group=group),
        out_shape=(jax.ShapeDtypeStruct((LEN,pairs*3*WIDE),LOW),jax.ShapeDtypeStruct((2,pairs*WIDE),F32)),
        grid_spec=pltpu.PrefetchScalarGridSpec(num_scalar_prefetch=1,grid=(pairs//group,),
          in_specs=[col(3*WIDE),col(WIDE),col(WIDE),pl.BlockSpec((group,2,LEN),lambda h,r:(r[last]+h,0,0)),whole,whole],
          out_specs=[pl.BlockSpec((LEN,3*WIDE*group),lambda h,r:(0,h)),pl.BlockSpec((2,WIDE*group),lambda h,r:(0,h))],
          scratch_shapes=[pltpu.VMEM((group,LEN,2*WIDE),LOW)]*2+[pltpu.VMEM((group,WIDE,LEN),LOW)]+[pltpu.VMEM((group,LEN,WIDE),F32)]*2),
        name="attention_backward")(r,packed,ctx,dctx,lse,fq,fk)


def normalize(hidden):
    average = jnp.mean(hidden, axis=-1, keepdims=True)
    centered = hidden - average
    variance = jnp.mean(centered * centered, axis=-1, keepdims=True)
    inverse = lax.rsqrt(variance + EPSILON)
    return centered * inverse, inverse


def normalize_back(grad, normal, inverse):
    first = jnp.mean(grad, axis=-1, keepdims=True)
    second = jnp.mean(grad * normal, axis=-1, keepdims=True)
    return (grad - first - normal * second) * inverse


def column_sum(value):
    return jnp.sum(value, axis=0, keepdims=True)


def up_body(place, context, inputs, vectors, *refs):
    count = (len(refs) - 9) // 2
    out_pieces, up_pieces = refs[:count], refs[count : 2 * count]
    normal, inverse, low, activated, slope, w_out, w_up, out_sem, up_sem = refs[2 * count :]
    out_copies = assemble(place, out_pieces, w_out, out_sem)
    up_copies = assemble(place, up_pieces, w_up, up_sem)
    step = pl.program_id(0)

    @pl.when(step == 0)
    def _():
        start_all(out_copies)
        start_all(up_copies)
        wait_all(out_copies)

    attended = matmul(context[...], w_out[...]) + vectors[:, B_OUT : B_OUT + D]
    value, scale = normalize(as_float(inputs[...]) + attended)
    normal[...] = value
    inverse[...] = jnp.broadcast_to(scale, inverse.shape)
    normed = rounded(
        value * vectors[:, ATTN_GAIN : ATTN_GAIN + D] + vectors[:, ATTN_SHIFT : ATTN_SHIFT + D]
    )
    low[...] = normed

    @pl.when(step == 0)
    def _():
        wait_all(up_copies)

    for at in range(0, FF, D):
        up = matmul(normed, w_up[:, at : at + D]) + vectors[:, B_UP + at : B_UP + at + D]
        below = 0.5 + 0.5 * lax.erf(up * (0.5**0.5))
        density = jnp.exp(-0.5 * up * up) * 0.3989422804014327
        activated[:, at : at + D] = rounded(up * below)
        slope[:, at : at + D] = rounded(below + up * density)


def up_block(place, context, inputs, vectors, out_pieces, up_pieces):
    count = len(out_pieces)
    return call(
        up_body,
        "out_norm_up",
        (
            shape((LEN, D), F32),
            shape((LEN, WIDE), F32),
            shape((LEN, D)),
            shape((LEN, FF)),
            shape((LEN, FF)),
        ),
        (LEN // TOKEN_ROWS,),
        [tokens(D), tokens(D), constant((1, VECTORS))] + [ANYWHERE] * (2 * count),
        [tokens(D), tokens(WIDE), tokens(D), tokens(FF), tokens(FF)],
        [
            pltpu.VMEM((D, D), LOW),
            pltpu.VMEM((D, FF), LOW),
            pltpu.SemaphoreType.DMA((count,)),
            pltpu.SemaphoreType.DMA((count,)),
        ],
        flops=2 * LEN * D * (D + FF),
        exps=2 * LEN * FF,
    )(place, context, inputs, vectors, *out_pieces, *up_pieces)


def down_body(place, activated, slope, normal, cotangent, vectors, *refs):
    count = len(refs) - 7
    pieces = refs[:count]
    output, d_sum, d_down, d_up, sums, w_down, sem = refs[count:]
    copies = assemble(place, pieces, w_down, sem)
    step = pl.program_id(0)

    @pl.when(step == 0)
    def _():
        start_all(copies)
        sums[...] = jnp.zeros_like(sums)
        wait_all(copies)

    down = matmul(activated[...], w_down[...]) + vectors[:, B_DOWN : B_DOWN + D]
    gain = vectors[:, ATTN_GAIN : ATTN_GAIN + D]
    normed = normal[...] * gain + vectors[:, ATTN_SHIFT : ATTN_SHIFT + D]
    value, scale = normalize(normed + down)
    gain = vectors[:, FFN_GAIN : FFN_GAIN + D]
    output[...] = rounded(value * gain + vectors[:, FFN_SHIFT : FFN_SHIFT + D])
    grad = as_float(cotangent[...])
    sums[:, :D] += column_sum(grad * value)
    sums[:, D : 2 * D] += column_sum(grad)
    d_two = normalize_back(grad * gain, value, scale)
    d_sum[...] = d_two
    d_low = rounded(d_two)
    d_down[...] = d_low
    sums[:, 2 * D : 3 * D] += column_sum(as_float(d_low))
    for at in range(0, FF, D):
        d_activated = matmul_right_t(d_low, w_down[at : at + D, :])
        part = rounded(d_activated * as_float(slope[:, at : at + D]))
        d_up[:, at : at + D] = part
        sums[:, 3 * D + at : 4 * D + at] += column_sum(as_float(part))


def down_block(place, activated, slope, normal, cotangent, vectors, pieces):
    count = len(pieces)
    return call(
        down_body,
        "down_norm_back",
        (
            shape((LEN, D)),
            shape((LEN, D), F32),
            shape((LEN, D)),
            shape((LEN, FF)),
            shape((1, 3 * D + FF), F32),
        ),
        (LEN // TOKEN_ROWS,),
        [tokens(FF), tokens(FF), tokens(D), tokens(D), constant((1, VECTORS))]
        + [ANYWHERE] * count,
        [tokens(D), tokens(D), tokens(D), tokens(FF), constant((1, 3 * D + FF))],
        [pltpu.VMEM((FF, D), LOW), pltpu.SemaphoreType.DMA((count,))],
        flops=4 * LEN * D * FF,
    )(place, activated, slope, normal, cotangent, vectors, *pieces)


def back_body(place, d_up, d_sum_two, normal, inverse, vectors, *refs):
    count = (len(refs) - 8) // 2
    up_pieces, out_pieces = refs[:count], refs[count : 2 * count]
    d_sum, d_attended, d_context, sums, w_up, w_out, up_sem, out_sem = refs[2 * count :]
    up_copies = assemble(place, up_pieces, w_up, up_sem)
    out_copies = assemble(place, out_pieces, w_out, out_sem)
    step = pl.program_id(0)

    @pl.when(step == 0)
    def _():
        start_all(up_copies)
        start_all(out_copies)
        sums[...] = jnp.zeros_like(sums)
        wait_all(up_copies)
        wait_all(out_copies)

    d_normed = d_sum_two[...] + matmul_right_t(d_up[...], w_up[...])
    value = normal[...]
    sums[:, :D] += column_sum(d_normed * value)
    sums[:, D : 2 * D] += column_sum(d_normed)
    d_one = normalize_back(
        d_normed * vectors[:, ATTN_GAIN : ATTN_GAIN + D], value, inverse[:, :1]
    )
    d_sum[...] = d_one
    low = rounded(d_one)
    d_attended[...] = low
    sums[:, 2 * D :] += column_sum(as_float(low))
    d_context[...] = rounded(matmul_right_t(low, w_out[...]))


def back_block(place, d_up, d_sum_two, normal, inverse, vectors, up_pieces, out_pieces):
    count = len(up_pieces)
    return call(
        back_body,
        "norm_back",
        (shape((LEN, D), F32), shape((LEN, D)), shape((LEN, D)), shape((1, 3 * D), F32)),
        (LEN // TOKEN_ROWS,),
        [tokens(FF), tokens(D), tokens(D), tokens(WIDE), constant((1, VECTORS))]
        + [ANYWHERE] * (2 * count),
        [tokens(D), tokens(D), tokens(D), constant((1, 3 * D))],
        [
            pltpu.VMEM((D, FF), LOW),
            pltpu.VMEM((D, D), LOW),
            pltpu.SemaphoreType.DMA((count,)),
            pltpu.SemaphoreType.DMA((count,)),
        ],
        flops=2 * LEN * D * (FF + D),
    )(place, d_up, d_sum_two, normal, inverse, vectors, *up_pieces, *out_pieces)


def input_body(place, weight, d_sum, *refs, spans):
    output, pieces = refs[-1], refs[:-1]
    total = d_sum[...]
    for piece, (partner, first, count) in zip(pieces, spans):
        block = 1 - place[CORE] if partner else place[CORE]
        at = pl.multiple_of((block * HALF_PAIRS + first) * TRIPLE, WIDE)
        total += matmul_right_t(piece[...], weight[:, pl.ds(at, count * TRIPLE)])
    output[...] = rounded(total)


def input_gradient(place, weight, d_sum, pieces, spans):
    return call(
        functools.partial(input_body, spans=spans),
        "input_gradient",
        shape((LEN, D)),
        (LEN // TOKEN_ROWS,),
        [constant((D, 3 * D)), tokens(D)] + [tokens(piece.shape[1]) for piece in pieces],
        tokens(D),
        flops=6 * LEN * D * D,
    )(place, weight, d_sum, *pieces)


def shard_row(place, d, rows):
    return pl.multiple_of(jnp.bitwise_xor(place[Y], d) * rows, rows)


def gradient_specs(shards, rows, block, got, index):
    if got is None:
        return shape((shards, rows, CHUNK)), pl.BlockSpec((shards, block, CHUNK), index), []
    one = pl.BlockSpec((block, CHUNK), lambda *at: index(*at)[1:])
    return (
        (shape((rows, CHUNK)),) * shards,
        [one] * shards,
        [pl.BlockSpec((shards, block, CHUNK), index)],
    )


def down_gradient_body(place, left, right, *refs, shards, adds):
    value = matmul_left_t(left[...], right[...])
    if not adds:
        refs[0][0] = rounded(value)
        return
    got, outs = refs[0], refs[1:]
    value = rounded(value + as_float(got[0]))
    for at in range(shards):

        @pl.when(pl.program_id(0) == shards - 1 - at)
        def _(at=at):
            outs[at][...] = value


def down_gradient(place, activated, d_down, partner, shards, got=None):
    rows = FF // shards
    order = lambda i: shards - 1 - i
    pick_column = lambda i, p: (0, 1 - p[CORE] if partner else p[CORE])
    one = pl.BlockSpec((1, rows, CHUNK), lambda i, p: (order(i), 0, 0))
    operands, specs = [activated, d_down], []
    if got is None:
        outs, out_specs = shape((shards, rows, CHUNK)), one
    else:
        operands.append(got)
        specs.append(one)
        outs, out_specs = (shape((rows, CHUNK)),) * shards, [constant((rows, CHUNK))] * shards
    return call(
        functools.partial(down_gradient_body, shards=shards, adds=got is not None),
        "down_gradient",
        outs,
        (shards,),
        [
            pl.BlockSpec((LEN, rows), lambda i, p: (0, jnp.bitwise_xor(p[Y], order(i)))),
            pl.BlockSpec((LEN, CHUNK), pick_column),
        ]
        + specs,
        out_specs,
        flops=LEN * D * FF,
    )(place, *operands)


def row_gradient_body(place, *refs, terms, shards, adds):
    rows = D // shards
    operands, rest = refs[: 2 * terms], refs[2 * terms :]
    got, outs, total = (rest[0], rest[1:-1], rest[-1]) if adds else (None, rest[:-1], rest[-1])
    block = 0
    for term in range(terms):
        left, right = operands[2 * term : 2 * term + 2]
        width = right.shape[1]
        total[:, :width] = matmul_left_t(left[...], right[...])
        for j in range(width // CHUNK):
            here = slice(block * rows, (block + 1) * rows)
            block += 1
            for d in range(shards):
                value = total[pl.ds(shard_row(place, d, rows), rows), j * CHUNK : (j + 1) * CHUNK]
                if adds:
                    outs[d][here, :] = rounded(value + as_float(got[d, here, :]))
                else:
                    outs[0][d, here, :] = rounded(value)


def row_gradient(place, terms, shards, steps=1, got=None):
    rows = D // shards
    widths = [right_width for _, _, right_width, _ in terms]
    count = sum(widths) // CHUNK
    block = count * rows
    specs, operands = [], []
    for left, right, width, first in terms:
        specs.append(constant((LEN, D)))
        specs.append(pl.BlockSpec((LEN, width), lambda i, p, first=first: (0, first(p) + i)))
        operands += [left, right]
    all_rows = pl.BlockSpec((shards, block, CHUNK), lambda i, p: (0, i, 0))
    one = pl.BlockSpec((block, CHUNK), lambda i, p: (i, 0))
    if got is None:
        outs, out_specs = shape((shards, steps * block, CHUNK)), all_rows
    else:
        specs.append(all_rows)
        operands.append(got)
        outs, out_specs = (shape((steps * block, CHUNK)),) * shards, [one] * shards
    return call(
        functools.partial(
            row_gradient_body, terms=len(terms), shards=shards, adds=got is not None
        ),
        "row_gradient",
        outs,
        (steps,),
        specs,
        out_specs,
        [pltpu.VMEM((D, max(widths)), F32)],
        flops=2 * LEN * D * sum(widths) * steps,
    )(place, *operands)


class Place:
    def __init__(self, replicas, shards):
        self.replicas, self.shards, self.depth = replicas, shards, replicas // 4
        replica = lax.axis_index("replica")
        self.index = [replica % 2, replica // 2 % 2, replica // 4, lax.axis_index("shard")]
        self.core, self.x, self.z, self.y = self.index
        self.vector = jnp.stack(self.index).astype(jnp.int32)

    def shard(self, value, mask):
        return lax.ppermute(value, "shard", [(i, i ^ mask) for i in range(self.shards)])

    def replica(self, value, mask):
        return lax.ppermute(value, "replica", [(i, i ^ mask) for i in range(self.replicas)])


def tie(value, *first):
    return lax.optimization_barrier((value,) + first)[0]


def pick(options, index):
    chosen = options[-1]
    for at in range(len(options) - 2, -1, -1):
        chosen = jnp.where(index == at, options[at], chosen)
    return chosen


def gather_shards(value, at):
    found = {0: value}
    mask = 1
    while mask < at.shards:
        for d in range(mask):
            found[d | mask] = at.shard(found[d], mask)
        mask *= 2
    return [found[d] for d in range(at.shards)]


def half_rows(weight, at):
    half = weight.shape[0] // 2
    return lax.dynamic_slice_in_dim(weight, at.core * half, half, 0)


def weight_pieces(weight, near, at):
    pieces = [weight]
    for block in near[1:]:
        pieces += [block, at.replica(block, 1)]
    return pieces


def exchange_shards(parts, at):
    mask = at.shards // 2
    while mask > 1:
        parts = [
            rounded(as_float(parts[d]) + as_float(at.shard(parts[d | mask], mask)))
            for d in range(mask)
        ]
        mask //= 2
    return parts[0], at.shard(parts[1], 1)


def split_body(place, *refs, count, parts):
    outs = refs[2 * count * parts :]
    for d in range(parts):
        row = 0
        for at in range(count):
            keep, got = refs[2 * (d * count + at) : 2 * (d * count + at) + 2]
            height = keep.shape[0]
            outs[d][row : row + height, :] = rounded(as_float(keep[...]) + as_float(got[...]))
            row += height


def split_add(at, which, groups, parts):
    heights = [keep.shape[0] // parts for keep, _ in groups]
    index = at.index[which]
    if any(height % 16 for height in heights):
        found = []
        for d in range(parts):
            blocks = []
            for (keep, got), height in zip(groups, heights):
                cut = lambda v: lax.dynamic_slice_in_dim(v, (index ^ d) * height, height, 0)
                blocks.append(rounded(as_float(cut(keep)) + as_float(cut(got))))
            found.append(jnp.concatenate(blocks) if len(blocks) > 1 else blocks[0])
        return found
    specs, operands = [], []
    for d in range(parts):
        for (keep, got), height in zip(groups, heights):
            spec = pl.BlockSpec(
                (height, CHUNK), lambda i, p, d=d: (jnp.bitwise_xor(p[which], d), 0)
            )
            specs += [spec, spec]
            operands += [keep, got]
    total = sum(heights)
    return call(
        functools.partial(split_body, count=len(groups), parts=parts),
        "split_add",
        (shape((total, CHUNK)),) * parts,
        (1,),
        specs,
        [constant((total, CHUNK))] * parts,
    )(at.vector, *operands)


def join_body(place, *refs, which):
    output = refs[-1]
    for d, piece in enumerate(refs[:-1]):
        height = piece.shape[0]
        start = pl.multiple_of(jnp.bitwise_xor(place[which], d) * height, 16)
        output[pl.ds(start, height), :] = piece[...]


def join_rows(at, which, pieces):
    height, parts = pieces[0].shape[0], len(pieces)
    index = at.index[which]
    if height % 16:
        return jnp.concatenate([pick(pieces, index ^ j) for j in range(parts)])
    return call(
        functools.partial(join_body, which=which),
        "join_rows",
        shape((parts * height, CHUNK)),
        (1,),
        [constant((height, CHUNK))] * parts,
        constant((parts * height, CHUNK)),
    )(at.vector, *pieces)


def sum_replicas(groups, at):
    keep, send = split_add(at, X, groups, 2)
    return finish_sum(keep, at.replica(send, 2), at)


def finish_sum(keep, got, at):
    blocks = split_add(at, Z, [(keep, got)], at.depth)
    total = as_float(blocks[0])
    for d in range(1, at.depth):
        total += as_float(at.replica(blocks[d], 4 * d))
    total = rounded(total)
    found = [total] + [at.replica(total, 4 * d) for d in range(1, at.depth)]
    mine = join_rows(at, Z, found)
    other = at.replica(mine, 2)
    return [mine, other, at.replica(mine, 1), at.replica(other, 1)]


def finish_feed_body(place, *refs, rows, blocks):
    sources, (down, up) = refs[:4], refs[4:]
    at = pl.program_id(0)
    half = blocks * rows
    for index in range(4):

        @pl.when(at == index)
        def _(index=index):
            source = sources[index]
            down[...] = as_float(source[: down.shape[0], :])
            for j in range(blocks):
                start = down.shape[0] + j * rows
                up[:, j * CHUNK : (j + 1) * CHUNK] = as_float(source[start : start + rows, :])


def finish_feed(at, sources):
    rows, down_rows = D // at.shards, FF // at.shards
    blocks = FF // (4 * CHUNK)
    half = lambda i, p: jnp.bitwise_xor(p[X], i % 2)
    core = lambda i, p: jnp.bitwise_xor(p[CORE], i // 2)
    return call(
        functools.partial(finish_feed_body, rows=rows, blocks=blocks),
        "finish_feed",
        (shape((down_rows, D), F32), shape((rows, FF), F32)),
        (4,),
        [constant(source.shape) for source in sources],
        [
            pl.BlockSpec((down_rows // 2, CHUNK), lambda i, p: (half(i, p), core(i, p))),
            pl.BlockSpec((rows, blocks * CHUNK), lambda i, p: (0, core(i, p) * 2 + half(i, p))),
        ],
    )(at.vector, *sources)


def finish_attention_body(place, *refs, layouts, rows):
    groups = len(layouts)
    sources, (qkv, out), holds = refs[: 4 * groups], refs[4 * groups : 4 * groups + 2], refs[4 * groups + 2 :]
    for group, layout in enumerate(layouts):
        hold = holds[group]
        for index in range(4):
            source = sources[4 * group + index]
            height = source.shape[0]
            start = pl.multiple_of(jnp.bitwise_xor(place[X], index % 2) * height, 16)
            hold[index // 2, pl.ds(start, height), :] = source[...]
        for side in range(2):
            core = jnp.bitwise_xor(place[CORE], side)
            for block, name in enumerate(layout):
                value = as_float(hold[side, block * rows : (block + 1) * rows, :])
                if name is None:
                    out[:, pl.ds(pl.multiple_of(core * CHUNK, WIDE), CHUNK)] = value
                    continue
                for part in range(3):
                    lane = part * D + (core * HALF_PAIRS + name) * WIDE
                    qkv[:, pl.ds(pl.multiple_of(lane, WIDE), WIDE)] = value[
                        :, part * WIDE : (part + 1) * WIDE
                    ]


def finish_attention(at, groups, layouts):
    rows = D // at.shards
    operands = [source for group in groups for source in group]
    return call(
        functools.partial(finish_attention_body, layouts=layouts, rows=rows),
        "finish_attention",
        (shape((rows, 3 * D), F32), shape((rows, D), F32)),
        (1,),
        [constant(source.shape) for source in operands],
        [constant((rows, 3 * D)), constant((rows, D))],
        [pltpu.VMEM((2, len(layout) * rows, CHUNK), LOW) for layout in layouts],
    )(at.vector, *operands)


def sum_small(values, at):
    parts = [lax.dynamic_index_in_dim(values, at.y ^ d, 0, False) for d in range(at.shards)]
    mask = at.shards // 2
    while mask:
        parts = [parts[d] + at.shard(parts[d | mask], mask) for d in range(mask)]
        mask //= 2
    total = parts[0]
    mask = 1
    while mask < at.replicas:
        total = total + at.replica(total, mask)
        mask *= 2
    return total


ATTENTION_GROUPS = ((0, 3),)


def local(
    replicas,
    shards,
    inputs,
    segments,
    w_qkv,
    b_qv,
    w_out,
    b_out,
    attn_gain,
    attn_shift,
    w_up,
    b_up,
    w_down,
    b_down,
    ffn_gain,
    ffn_shift,
    cotangent,
):
    at = Place(replicas, shards)
    place = at.vector
    segments = segments.reshape(LEN)

    near_qkv = gather_shards(half_rows(w_qkv, at), at)
    vectors = (b_qv, b_out, attn_gain, attn_shift, b_up, b_down, ffn_gain, ffn_shift)
    sizes = [vector.shape[0] for vector in vectors]
    small = gather_shards(jnp.concatenate(vectors), at)
    small = as_float(jnp.stack([pick(small, at.y ^ j) for j in range(shards)]))
    full, offset = [], 0
    for size in sizes:
        full.append(small[:, offset : offset + size].reshape(-1))
        offset += size
    full = jnp.concatenate(full).reshape(1, VECTORS)
    feature_q, feature_k = document_features(segments)
    forward_ranges = key_ranges(segments, FORWARD_ROWS)
    backward_ranges = key_ranges(segments, BACKWARD_ROWS)

    pieces_qkv = weight_pieces(w_qkv, near_qkv, at)
    half_out, half_up = (half_rows(w, at) for w in (w_out, w_up))
    half_out, half_up, *_ = lax.optimization_barrier((half_out, half_up, near_qkv[-1]))
    near_out, near_up = gather_shards(half_out, at), gather_shards(half_up, at)
    projected, weight_qkv = project(place, inputs, full, pieces_qkv)
    context, log_total = attn_fwd(
        forward_ranges, projected, feature_q, feature_k, 6
    )
    near_out, near_up, context = lax.optimization_barrier((near_out, near_up, context))
    half_down = tie(half_rows(w_down, at), near_up[-1])
    near_down = gather_shards(half_down, at)
    pieces_out = weight_pieces(w_out, near_out, at)
    pieces_up = weight_pieces(w_up, near_up, at)
    normal, inverse, low, activated, slope = up_block(
        place, context, inputs, full, pieces_out, pieces_up
    )
    near_down, activated = lax.optimization_barrier((near_down, activated))
    pieces_down = weight_pieces(w_down, near_down, at)
    layer_output, d_sum_two, d_down, d_up, sums_two = down_block(
        place, activated, slope, normal, cotangent, full, pieces_down
    )

    down_send = down_gradient(place, activated, d_down, True, shards)
    down_got = at.replica(down_send, 1)
    up_width = FF // 4
    other_half, own_half = (lambda p: 2 * (1 - p[CORE])), (lambda p: 2 * p[CORE])
    up_send = row_gradient(place, [(low, d_up, up_width, other_half)], shards, 2)
    up_got = at.replica(up_send, 1)
    down_parts = down_gradient(place, activated, d_down, False, shards, down_got)
    down_pair = exchange_shards(down_parts, at)
    up_parts = row_gradient(place, [(low, d_up, up_width, own_half)], shards, 2, up_got)
    up_parts, d_up = lax.optimization_barrier((up_parts, d_up))
    d_sum_one, d_attended, d_context, sums_one = back_block(
        place, d_up, d_sum_two, normal, inverse, full, pieces_up, pieces_out
    )

    def attention_back(block, first, count, d_context):
        start = (block * HALF_PAIRS + first) // count
        return attn_bwd(
            jnp.concatenate([backward_ranges, start.reshape(1)]),
            projected,
            context,
            d_context,
            log_total,
            feature_q,
            feature_k,
            count,
            count,
        )

    d_other, bias_other = attention_back(1 - at.core, 0, 3, d_context)
    down_pair, d_other = lax.optimization_barrier((down_pair, d_other))
    up_parts = tie(up_parts, down_pair[1])
    up_pair = exchange_shards(up_parts, at)
    other_out, own_out = (lambda p: 1 - p[CORE]), (lambda p: p[CORE])
    zero = lambda p: 0
    send = row_gradient(
        place,
        [(inputs, d_other, 3 * TRIPLE, zero), (context, d_attended, CHUNK, other_out)],
        shards,
    )
    got = at.replica(send, 1)
    d_context, got = lax.optimization_barrier((d_context, got))
    d_own, bias_own = attention_back(at.core, 0, 3, d_context)
    up_pair, d_own = lax.optimization_barrier((up_pair, d_own))
    parts = row_gradient(
        place,
        [(inputs, d_own, 3 * TRIPLE, zero), (context, d_attended, CHUNK, own_out)],
        shards,
        1,
        got,
    )
    attention_pair = exchange_shards(parts, at)
    feed = sum_replicas([down_pair, up_pair], at)
    attention_sum = sum_replicas([attention_pair], at)
    input_grad = input_gradient(
        place, weight_qkv, d_sum_one, [d_other, d_own], ((True, 0, 3), (False, 0, 3))
    )
    grad_w_down, grad_w_up = finish_feed(at, feed)
    grad_w_qkv, grad_w_out = finish_attention(at, [attention_sum], ((0, 1, 2, None),))

    bias = jnp.concatenate(
        [pick([bias_own, bias_other], at.core), pick([bias_other, bias_own], at.core)], axis=1
    )
    sums_one, sums_two = sums_one[0], sums_two[0]
    grads = (
        bias.reshape(-1),
        sums_one[2 * D :],
        sums_one[:D],
        sums_one[D : 2 * D],
        sums_two[3 * D :],
        sums_two[2 * D : 3 * D],
        sums_two[:D],
        sums_two[D : 2 * D],
    )
    packed = jnp.concatenate([grad.reshape(shards, -1) for grad in grads], axis=1)
    packed = sum_small(packed.reshape(shards, -1, 128), at).reshape(-1)
    owned, offset = [], 0
    for size in sizes:
        owned.append(packed[offset : offset + size])
        offset += size
    return (
        layer_output,
        input_grad,
        grad_w_qkv,
        owned[0],
        grad_w_out,
        owned[1],
        owned[2],
        owned[3],
        grad_w_up,
        owned[4],
        grad_w_down,
        owned[5],
        owned[6],
        owned[7],
    )


def solution(mesh):
    token, matrix, vector = P(("replica", "shard"), None), P("shard", None), P("shard")
    weights = (matrix, vector, matrix, vector, vector, vector)
    weights += (matrix, vector, matrix, vector, vector, vector)
    return jax.shard_map(
        functools.partial(local, mesh.shape["replica"], mesh.shape["shard"]),
        mesh=mesh,
        in_specs=(token, token) + weights + (token,),
        out_specs=(token, token) + weights,
        check_vma=False,
    )
```

time: 547 us -> 417 us (0.76)
  the two profiles are of different devices: /device:TPU:11 before, /device:TPU:0 now
where the time goes in v2:
time: 417 us; the launch traced here: 410 us
  Pallas kernels  211 us (51%)
  waiting for transfers between devices  120 us (29%)
  starting transfers between devices  48.3 us (12%)
  local copies, waits for them, and re-layouts  20.1 us (5%)
  other arithmetic  9.52 us (2%)
    ppermute x31, waiting for transfers between devices, replica(): lax.ppermute(value, 'replica', [(i, i ^ mask) for i in range(self.replica...  92 us
    ppermute x31, starting transfers between devices, replica(): lax.ppermute(value, 'replica', [(i, i ^ mask) for i in range(self.replica...  36.1 us
    pallas_call x2, Pallas kernels, attn_bwd(): pl.pallas_call(lambda *a: bwd_body(*a, group=group), out_shape=(jax.Shape...  35.2 us
    pallas_call x4, Pallas kernels, row_gradient(): call(functools.partial(row_gradient_body, terms=len(terms), shards=shards...  31.4 us
    ppermute x9, waiting for transfers between devices, shard(): lax.ppermute(value, 'shard', [(i, i ^ mask) for i in range(self.shards)])  28 us
    pallas_call x1, Pallas kernels, down_block(): call(down_body, 'down_norm_back', (shape((LEN, D)), shape((LEN, D), F32),...  24.1 us
    pallas_call x1, Pallas kernels, up_block(): call(up_body, 'out_norm_up', (shape((LEN, D), F32), shape((LEN, WIDE), F3...  19.7 us
    pallas_call x1, Pallas kernels, back_block(): call(back_body, 'norm_back', (shape((LEN, D), F32), shape((LEN, D)), shap...  17.2 us
  transfers between devices with their start and end apart: 40, of which 20 were waited for; matrix products, arithmetic and copies ran while one was open for 4% of the time, Pallas kernels for 39%

profile of v2, /device:TPU:0, one launch (start us, length us, event | category | flops | bytes accessed | tf_op | source)
XLA Modules:
  0.0 410.0 jit_solution(14777629477490978725)
XLA Ops:
  0.8 1.3 constant_dynamic-slice_fusion
  2.0 3.0 collective-permute-start
  9.1 1.3 constant_dynamic-slice_fusion.1
  12.7 12.3 %collective-permute-done.3 = bf16[4608]{0:T(1024)(128)(2,1)S(1)} collective-permute-done((bf16[4608]{0:T(1024)(128)(2,1)S(1)}, bf16[4608]{0:T(1024)(128)(2,1)S(1)}, u32[]{:S(2)}, u32[]{:S(2)}) %collective-permute-start.3) | collective-permute-done | bytes 9248 | tf_op jit(solution)/shard_map/ppermute | solution.py:626
  25.1 1.8 collective-permute-start.2
  27.5 2.1 collective-permute-done.4.refs_2_.refs_5_.refs_8_
  30.5 9.1 %project.1 = (bf16[1024,2304]{1,0:T(8,128)(2,1)}, bf16[768,2304]{1,0:T(8,128)(2,1)}) custom-call(s32[4]{0:T(128)} %pad_add_fusion.place, bf16[1024,768]{1,0:T(8,128)(2,1)} %refs_0_.11, f32[1,9216]{1,0:T(1,128)} %bitcast.42, bf16[384,2304]{1,0:T(8,128)(2,1)} %refs_6_.1, bf16[192,2304]{1,0:T(8,128)(2,1)} %collective-permute-done.refs_1_.refs_4_.refs_7_, ...), custom_call_target="tpu_custom_call" | custom-call | flops 3623878656 | bytes 1048576 | tf_op jit(solution)/shard_map/project/pallas_call | solution.py:150
  39.6 15.9 %attention_forward.1 = (bf16[1024,768]{1,0:T(8,128)(2,1)}, f32[6,2,1024]{2,1,0:T(2,128)}) custom-call(s32[16]{0:T(128)} %pad_add_fusion.1.a_0_, bf16[1024,2304]{1,0:T(8,128)(2,1)} %get-tuple-element.81.a_1_, bf16[1024,128]{1,0:T(8,128)(2,1)} %select_convert_fusion.a_2_.a_5_, bf16[1024,128]{1,0:T(8,128)(2,1)} %fusion.1.a_3_.a_6_), custom_call_target="tpu_custom_call" | custom-call | tf_op jit(solution)/shard_map/attention_forward/pallas_call | solution.py:220
  55.4 3.4 collective-permute-done.1.refs_1_.refs_4_
  59.0 1.5 collective-permute-start.5
  60.7 1.7 collective-permute-done.6.refs_2_.refs_5_
  63.0 19.7 %out_norm_up.1 = (f32[1024,768]{1,0:T(8,128)}, f32[1024,128]{1,0:T(8,128)}, bf16[1024,768]{1,0:T(8,128)(2,1)}, bf16[1024,3072]{1,0:T(8,128)(2,1)}, bf16[1024,3072]{1,0:T(8,128)(2,1)}) custom-call(s32[4]{0:T(128)} %pad_add_fusion.place, bf16[1024,768]{1,0:T(8,128)(2,1)} %get-tuple-element.85.context.a_2_.refs_2_, bf16[1024,768]{1,0:T(8,128)(2,1)} %refs_0_.11, ...), custom_call_target="tpu_custom_call" | custom-call | flops 6039797760 | bytes 1048576 | tf_op jit(solution)/shard_map/out_norm_up/pallas_call | solution.py:358
  82.8 4.6 %collective-permute-done.5.refs_1_ = bf16[768,768]{1,0:T(8,128)(2,1)S(1)} collective-permute-done((bf16[768,768]{1,0:T(8,128)(2,1)S(1)}, bf16[768,768]{1,0:T(8,128)(2,1)S(1)}, u32[]{:S(2)}, u32[]{:S(2)}) %collective-permute-start.5) | collective-permute-done | bytes 1179680 | tf_op jit(solution)/shard_map/ppermute | solution.py:626
  87.4 2.8 collective-permute-done.8.refs_2_
  90.2 1.0 copy-done.36
  91.3 24.1 %down_norm_back.1 = (bf16[1024,768]{1,0:T(8,128)(2,1)}, f32[1024,768]{1,0:T(8,128)}, bf16[1024,768]{1,0:T(8,128)(2,1)}, bf16[1024,3072]{1,0:T(8,128)(2,1)}, f32[1,5376]{1,0:T(1,128)}) custom-call(s32[4]{0:T(128)} %pad_add_fusion.place, bf16[1024,3072]{1,0:T(8,128)(2,1)} %get-tuple-element.88.activated.left, bf16[1024,3072]{1,0:T(8,128)(2,1)} %get-tuple-element.89.slope, ...), custom_call_target="tpu_custom_call" | custom-call | flops 9663676416 | bytes 1048576 | tf_op jit(solution)/shard_map/down_norm_back/pallas_call | solution.py:418
  115.4 7.5 %down_gradient.2 = bf16[2,1536,384]{2,1,0:T(8,128)(2,1)} custom-call(s32[4]{0:T(128)} %pad_add_fusion.place, bf16[1024,3072]{1,0:T(8,128)(2,1)} %get-tuple-element.88.activated.left, bf16[1024,768]{1,0:T(8,128)(2,1)} %get-tuple-element.102.right), custom_call_target="tpu_custom_call" | custom-call | flops 2415919104 | bytes 1048576 | tf_op jit(solution)/shard_map/down_gradient/pallas_call | solution.py:550
  123.1 6.7 %row_gradient.4 = bf16[2,1536,384]{2,1,0:T(8,128)(2,1)} custom-call(s32[4]{0:T(128)} %pad_add_fusion.place, bf16[1024,768]{1,0:T(8,128)(2,1)} %get-tuple-element.94.refs_0_, bf16[1024,3072]{1,0:T(8,128)(2,1)} %get-tuple-element.98.refs_1_.d_up), custom_call_target="tpu_custom_call" | custom-call | flops 2415919104 | bytes 1048576 | tf_op jit(solution)/shard_map/row_gradient/pallas_call | solution.py:603
  131.7 8.5 %down_gradient.3 = (bf16[1536,384]{1,0:T(8,128)(2,1)}, bf16[1536,384]{1,0:T(8,128)(2,1)}) custom-call(s32[4]{0:T(128)} %pad_add_fusion.place, bf16[1024,3072]{1,0:T(8,128)(2,1)} %get-tuple-element.88.activated.left, bf16[1024,768]{1,0:T(8,128)(2,1)} %get-tuple-element.102.right, bf16[2,1536,384]{2,1,0:T(8,128)(2,1)} %collective-permute-done.10.refs_0_), custom_call_target="tpu_custom_call" | custom-call | flops 2415919104 | bytes 1048576 | tf_op jit(solution)/shard_map/down_gradient/pallas_call | solution.py:550
  140.2 1.4 collective-permute-start.11
  143.6 1.5 copy-done.6
  145.1 7.5 %row_gradient.5 = (bf16[1536,384]{1,0:T(8,128)(2,1)}, bf16[1536,384]{1,0:T(8,128)(2,1)}) custom-call(s32[4]{0:T(128)} %pad_add_fusion.place, bf16[1024,768]{1,0:T(8,128)(2,1)} %get-tuple-element.94.refs_0_, bf16[1024,3072]{1,0:T(8,128)(2,1)} %get-tuple-element.98.refs_1_.d_up, bf16[2,1536,384]{2,1,0:T(8,128)(2,1)} %copy-done.6), custom_call_target="tpu_custom_call" | custom-call | flops 2415919104 | bytes 1048576 | tf_op jit(solution)/shard_map/row_gradient/pallas_call | solution.py:603
  152.6 17.2 %norm_back.1 = (f32[1024,768]{1,0:T(8,128)}, bf16[1024,768]{1,0:T(8,128)(2,1)}, bf16[1024,768]{1,0:T(8,128)(2,1)}, f32[1,2304]{1,0:T(1,128)}) custom-call(s32[4]{0:T(128)} %pad_add_fusion.place, bf16[1024,3072]{1,0:T(8,128)(2,1)} %get-tuple-element.98.refs_1_.d_up, f32[1024,768]{1,0:T(8,128)} %get-tuple-element.99.d_sum_two, ...), custom_call_target="tpu_custom_call" | custom-call | flops 6039797760 | bytes 1048576 | tf_op jit(solution)/shard_map/norm_back/pallas_call | solution.py:469
  169.9 17.7 %attention_backward.2 = (bf16[1024,1152]{1,0:T(8,128)(2,1)}, f32[2,384]{1,0:T(2,128)}) custom-call(s32[9]{0:T(128)} %get-tuple-element.177.a_0_, bf16[1024,2304]{1,0:T(8,128)(2,1)} %get-tuple-element.81.a_1_, bf16[1024,768]{1,0:T(8,128)(2,1)} %get-tuple-element.85.context.a_2_.refs_2_, bf16[1024,768]{1,0:T(8,128)(2,1)} %get-tuple-element.115.a_3_, ...), custom_call_target="tpu_custom_call" | custom-call | tf_op jit(solution)/shard_map/attention_backward/pallas_call | solution.py:294
  187.6 8.1 %row_gradient.6 = bf16[2,1536,384]{2,1,0:T(8,128)(2,1)} custom-call(s32[4]{0:T(128)} %pad_add_fusion.place, bf16[1024,768]{1,0:T(8,128)(2,1)} %refs_0_.11, bf16[1024,1152]{1,0:T(8,128)(2,1)} %get-tuple-element.108.refs_1_.refs_0_, bf16[1024,768]{1,0:T(8,128)(2,1)} %get-tuple-element.85.context.a_2_.refs_2_, bf16[1024,768]{1,0:T(8,128)(2,1)} %get-tuple-element.114.refs_3_), custom_call_target="tpu_custom_call" | custom-call | flops 2415919104 | bytes 1048576 | tf_op jit(solution)/shard_map/row_gradient/pallas_call | solution.py:603
  195.7 3.5 collective-permute-start.12
  199.2 1.4 collective-permute-done.13.refs_4_
  200.6 17.5 %attention_backward.3 = (bf16[1024,1152]{1,0:T(8,128)(2,1)}, f32[2,384]{1,0:T(2,128)}) custom-call(s32[9]{0:T(128)} %get-tuple-element.176.a_0_, bf16[1024,2304]{1,0:T(8,128)(2,1)} %get-tuple-element.81.a_1_, bf16[1024,768]{1,0:T(8,128)(2,1)} %get-tuple-element.85.context.a_2_.refs_2_, bf16[1024,768]{1,0:T(8,128)(2,1)} %get-tuple-element.115.a_3_, ...), custom_call_target="tpu_custom_call" | custom-call | tf_op jit(solution)/shard_map/attention_backward/pallas_call | solution.py:294
  218.0 7.7 %collective-permute-done.12.refs_3_.refs_7_ = bf16[1536,384]{1,0:T(8,128)(2,1)S(1)} collective-permute-done((bf16[1536,384]{1,0:T(8,128)(2,1)S(1)}, bf16[1536,384]{1,0:T(8,128)(2,1)S(1)}, u32[]{:S(2)}, u32[]{:S(2)}) %collective-permute-start.12) | collective-permute-done | bytes 1179680 | tf_op jit(solution)/shard_map/ppermute | solution.py:626
  225.8 1.0 copy-done.3
  226.8 4.7 %split_add.6 = (bf16[1536,384]{1,0:T(8,128)(2,1)}, bf16[1536,384]{1,0:T(8,128)(2,1)}) custom-call(s32[4]{0:T(128)} %pad_add_fusion.place, bf16[1536,384]{1,0:T(8,128)(2,1)} %get-tuple-element.133.refs_0_.refs_4_, bf16[1536,384]{1,0:T(8,128)(2,1)} %copy-done.2, bf16[1536,384]{1,0:T(8,128)(2,1)} %get-tuple-element.134.refs_2_.refs_6_, ...), custom_call_target="tpu_custom_call" | custom-call | bytes 1048576 | tf_op jit(solution)/shard_map/split_add/pallas_call | solution.py:708
  231.5 3.1 collective-permute-start.30
  234.6 9.0 %row_gradient.7 = (bf16[1536,384]{1,0:T(8,128)(2,1)}, bf16[1536,384]{1,0:T(8,128)(2,1)}) custom-call(s32[4]{0:T(128)} %pad_add_fusion.place, bf16[1024,768]{1,0:T(8,128)(2,1)} %refs_0_.11, bf16[1024,1152]{1,0:T(8,128)(2,1)} %get-tuple-element.117.refs_1_, bf16[1024,768]{1,0:T(8,128)(2,1)} %get-tuple-element.85.context.a_2_.refs_2_, ...), custom_call_target="tpu_custom_call" | custom-call | flops 2415919104 | bytes 1048576 | tf_op jit(solution)/shard_map/row_gradient/pallas_call | solution.py:603
  243.9 16.7 %collective-permute-done.30.refs_1_.refs_3_.refs_5_.refs_7_ = bf16[1536,384]{1,0:T(8,128)(2,1)S(1)} collective-permute-done((bf16[1536,384]{1,0:T(8,128)(2,1)}, bf16[1536,384]{1,0:T(8,128)(2,1)S(1)}, u32[]{:S(2)}, u32[]{:S(2)}) %collective-permute-start.30) | collective-permute-done | bytes 1179680 | tf_op jit(solution)/shard_map/ppermute | solution.py:629
  261.6 3.5 split_add.7
  265.1 1.5 collective-permute-start.31
  266.6 2.6 collective-permute-start.32
  269.8 8.5 %collective-permute-done.31 = bf16[384,384]{1,0:T(8,128)(2,1)S(1)} collective-permute-done((bf16[384,384]{1,0:T(8,128)(2,1)}, bf16[384,384]{1,0:T(8,128)(2,1)S(1)}, u32[]{:S(2)}, u32[]{:S(2)}) %collective-permute-start.31) | collective-permute-done | bytes 294944 | tf_op jit(solution)/shard_map/ppermute | solution.py:629
  278.3 12.0 %collective-permute-done.32 = bf16[384,384]{1,0:T(8,128)(2,1)S(1)} collective-permute-done((bf16[384,384]{1,0:T(8,128)(2,1)}, bf16[384,384]{1,0:T(8,128)(2,1)S(1)}, u32[]{:S(2)}, u32[]{:S(2)}) %collective-permute-start.32) | collective-permute-done | bytes 294944 | tf_op jit(solution)/shard_map/ppermute | solution.py:629
  290.3 1.1 add_convert_fusion.refs_0_
  291.4 4.4 %collective-permute-start.34 = (bf16[384,384]{1,0:T(8,128)(2,1)S(1)}, bf16[384,384]{1,0:T(8,128)(2,1)S(1)}, u32[]{:S(2)}, u32[]{:S(2)}) collective-permute-start(bf16[384,384]{1,0:T(8,128)(2,1)S(1)} %add_convert_fusion.refs_0_), channel_id=1, source_target_pairs={{0,8},{2,10},{4,12},{6,14},{8,0},{10,2},{12,4},{14,6},{16,24},{18,... | collective-permute-start | bytes 884744 | tf_op jit(solution)/shard_map/ppermute | solution.py:629
  296.9 1.4 collective-permute-start.36
  299.3 3.4 split_add.4
  302.8 1.5 collective-permute-start.15
  304.9 13.9 %collective-permute-done.35.refs_2_ = bf16[384,384]{1,0:T(8,128)(2,1)S(1)} collective-permute-done((bf16[384,384]{1,0:T(8,128)(2,1)S(1)}, bf16[384,384]{1,0:T(8,128)(2,1)S(1)}, u32[]{:S(2)}, u32[]{:S(2)}) %collective-permute-start.35) | collective-permute-done | bytes 294944 | tf_op jit(solution)/shard_map/ppermute | solution.py:629
  320.3 3.0 join_rows.3.refs_0_
  324.6 3.0 split_add.5
  327.6 4.2 %collective-permute-start.16 = (bf16[192,384]{1,0:T(8,128)(2,1)}, bf16[192,384]{1,0:T(8,128)(2,1)S(1)}, u32[]{:S(2)}, u32[]{:S(2)}) collective-permute-start(bf16[192,384]{1,0:T(8,128)(2,1)} %get-tuple-element.124), channel_id=1, source_target_pairs={{0,8},{2,10},{4,12},{6,14},{8,0},{10,2},{12,4},{14,6},{16,24},{18,... | collective-permute-start | bytes 442376 | tf_op jit(solution)/shard_map/ppermute | solution.py:629
  331.8 2.4 collective-permute-start.18
  334.2 4.0 collective-permute-done.16
  338.2 5.2 %collective-permute-done.17 = bf16[192,384]{1,0:T(8,128)(2,1)S(1)} collective-permute-done((bf16[192,384]{1,0:T(8,128)(2,1)}, bf16[192,384]{1,0:T(8,128)(2,1)S(1)}, u32[]{:S(2)}, u32[]{:S(2)}) %collective-permute-start.17) | collective-permute-done | bytes 147488 | tf_op jit(solution)/shard_map/ppermute | solution.py:629
  344.5 2.7 collective-permute-start.19
  347.2 2.4 collective-permute-start.21
  349.9 1.6 collective-permute-done.19.refs_1_
  351.5 8.1 %collective-permute-done.20.refs_2_ = bf16[192,384]{1,0:T(8,128)(2,1)S(1)} collective-permute-done((bf16[192,384]{1,0:T(8,128)(2,1)S(1)}, bf16[192,384]{1,0:T(8,128)(2,1)S(1)}, u32[]{:S(2)}, u32[]{:S(2)}) %collective-permute-start.20) | collective-permute-done | bytes 147488 | tf_op jit(solution)/shard_map/ppermute | solution.py:629
  360.9 2.7 join_rows.2.refs_0_
  364.5 1.9 collective-permute-done.26
  366.4 1.7 collective-permute-start.27
  368.1 9.6 %collective-permute-done.27 = f32[36,128]{1,0:T(8,128)S(1)} collective-permute-done((f32[36,128]{1,0:T(8,128)S(1)}, f32[36,128]{1,0:T(8,128)S(1)}, u32[]{:S(2)}, u32[]{:S(2)}) %collective-permute-start.27) | collective-permute-done | bytes 18464 | tf_op jit(solution)/shard_map/ppermute | solution.py:629
  377.8 3.1 collective-permute-start.28
  380.8 1.8 collective-permute-done.28
  384.2 9.7 %input_gradient.1 = bf16[1024,768]{1,0:T(8,128)(2,1)} custom-call(s32[4]{0:T(128)} %pad_add_fusion.place, bf16[768,2304]{1,0:T(8,128)(2,1)} %get-tuple-element.93.weight, f32[1024,768]{1,0:T(8,128)} %get-tuple-element.101.d_sum, bf16[1024,1152]{1,0:T(8,128)(2,1)} %get-tuple-element.108.refs_1_.refs_0_, bf16[1024,1152]{1,0:T(8,128)(2,1)} %get-tuple-element.117.refs_1_), custom_call_target="tpu_custom_call" | custom-call | flops 3623878656 | bytes 1048576 | tf_op jit(solution)/shard_map/input_gradient/pallas_call | solution.py:498
  397.8 5.0 %finish_attention.1 = (f32[384,2304]{1,0:T(8,128)}, f32[384,768]{1,0:T(8,128)}) custom-call(s32[4]{0:T(128)} %pad_add_fusion.place, bf16[768,384]{1,0:T(8,128)(2,1)} %join_rows.2.refs_0_, bf16[768,384]{1,0:T(8,128)(2,1)} %copy-done.10, bf16[768,384]{1,0:T(8,128)(2,1)} %copy-done.11, bf16[768,384]{1,0:T(8,128)(2,1)} %collective-permute-done.24.refs_3_), custom_call_target="tpu_custom_call" | custom-call | bytes 1048576 | tf_op jit(solution)/shard_map/finish_attention/pallas_call | solution.py:818
  402.9 7.0 %finish_feed.1 = (f32[1536,768]{1,0:T(8,128)}, f32[384,3072]{1,0:T(8,128)}) custom-call(s32[4]{0:T(128)} %pad_add_fusion.place, bf16[1536,384]{1,0:T(8,128)(2,1)} %join_rows.3.refs_0_, bf16[1536,384]{1,0:T(8,128)(2,1)} %copy-done.8, bf16[1536,384]{1,0:T(8,128)(2,1)} %collective-permute-done.38.refs_2_, bf16[1536,384]{1,0:T(8,128)(2,1)} %collective-permute-done.39.refs_3_), custom_call_target="tpu_custom_call" | custom-call | bytes 1048576 | tf_op jit(solution)/shard_map/finish_feed/pallas_call | solution.py:778
  (207 shorter events, 29.1 us)
Async XLA Ops:
  0.6 4.4 %copy-start.27 = (bf16[768]{0:T(1024)(128)(2,1)S(1)}, bf16[768]{0:T(1024)(128)(2,1)}, u32[]{:S(2)}) copy-start(bf16[768]{0:T(1024)(128)(2,1)} %param.18) | copy-start | bytes 4612
  0.7 4.6 %copy-start.28 = (bf16[384]{0:T(512)(128)(2,1)S(1)}, bf16[384]{0:T(512)(128)(2,1)}, u32[]{:S(2)}) copy-start(bf16[384]{0:T(512)(128)(2,1)} %param.20) | copy-start | bytes 2308
  0.7 4.8 %copy-start.29 = (bf16[384]{0:T(512)(128)(2,1)S(1)}, bf16[384]{0:T(512)(128)(2,1)}, u32[]{:S(2)}) copy-start(bf16[384]{0:T(512)(128)(2,1)} %param.21) | copy-start | bytes 2308
  0.7 5.0 %copy-start.30 = (bf16[384]{0:T(512)(128)(2,1)S(1)}, bf16[384]{0:T(512)(128)(2,1)}, u32[]{:S(2)}) copy-start(bf16[384]{0:T(512)(128)(2,1)} %param.22) | copy-start | bytes 2308
  0.7 5.2 %copy-start.26 = (bf16[1536]{0:T(1024)(128)(2,1)S(1)}, bf16[1536]{0:T(1024)(128)(2,1)}, u32[]{:S(2)}) copy-start(bf16[1536]{0:T(1024)(128)(2,1)} %param.24) | copy-start | bytes 9220
  0.7 5.5 %copy-start.31 = (bf16[384]{0:T(512)(128)(2,1)S(1)}, bf16[384]{0:T(512)(128)(2,1)}, u32[]{:S(2)}) copy-start(bf16[384]{0:T(512)(128)(2,1)} %param.26) | copy-start | bytes 2308
  0.7 5.7 %copy-start.32 = (bf16[384]{0:T(512)(128)(2,1)S(1)}, bf16[384]{0:T(512)(128)(2,1)}, u32[]{:S(2)}) copy-start(bf16[384]{0:T(512)(128)(2,1)} %param.27) | copy-start | bytes 2308
  0.7 5.9 %copy-start.33 = (bf16[384]{0:T(512)(128)(2,1)S(1)}, bf16[384]{0:T(512)(128)(2,1)}, u32[]{:S(2)}) copy-start(bf16[384]{0:T(512)(128)(2,1)} %param.28) | copy-start | bytes 2308
  0.7 6.3 %copy-start.17 = (s32[1,1024]{1,0:T(1,128)S(1)}, s32[1,1024]{1,0:T(1,128)}, u32[]{:S(2)}) copy-start(s32[1,1024]{1,0:T(1,128)} %param.16) | copy-start | bytes 12292
  2.0 8.4 %copy-start.18 = (bf16[384,768]{1,0:T(8,128)(2,1)S(1)}, bf16[384,768]{1,0:T(8,128)(2,1)}, u32[]{:S(2)}) copy-start(bf16[384,768]{1,0:T(8,128)(2,1)} %refs_3_.5) | copy-start | bytes 1769476
  2.0 23.1 %collective-permute-start = (bf16[192,2304]{1,0:T(8,128)(2,1)S(1)}, bf16[192,2304]{1,0:T(8,128)(2,1)}, u32[]{:S(2)}, u32[]{:S(2)}) collective-permute-start(bf16[192,2304]{1,0:T(8,128)(2,1)S(1)} %constant_dynamic-slice_fusion), channel_id=1, source_target_pairs={{0,1},{1,0},{2,3},{3,2},{4,5},{5,4},{6,7},{7,6},{8,9},{9,8},{10,11... | collective-permute-start | bytes 2654216 | tf_op jit(solution)/shard_map/ppermute | solution.py:626
  6.8 18.1 %collective-permute-start.3 = (bf16[4608]{0:T(1024)(128)(2,1)S(1)}, bf16[4608]{0:T(1024)(128)(2,1)S(1)}, u32[]{:S(2)}, u32[]{:S(2)}) collective-permute-start(bf16[4608]{0:T(1024)(128)(2,1)S(1)} %dynamic-update-slice.24), channel_id=1, source_target_pairs={{0,1},{1,0},{2,3},{3,2},{4,5},{5,4},{6,7},{7,6},{8,9},{9,8},{10,11... | collective-permute-start | bytes 27656 | tf_op jit(solution)/shard_map/ppermute | solution.py:626
  25.1 33.8 %collective-permute-start.2 = (bf16[192,3072]{1,0:T(8,128)(2,1)S(1)}, bf16[192,3072]{1,0:T(8,128)(2,1)}, u32[]{:S(2)}, u32[]{:S(2)}) collective-permute-start(bf16[192,3072]{1,0:T(8,128)(2,1)S(1)} %constant_dynamic-slice_fusion.1), channel_id=1, source_target_pairs={{0,1},{1,0},{2,3},{3,2},{4,5},{5,4},{6,7},{7,6},{8,9},{9,8},{10,11... | collective-permute-start | bytes 3538952 | tf_op jit(solution)/shard_map/ppermute | solution.py:626
  26.9 2.6 collective-permute-start.4
  27.1 31.7 %collective-permute-start.1 = (bf16[192,768]{1,0:T(8,128)(2,1)}, bf16[192,768]{1,0:T(8,128)(2,1)}, u32[]{:S(2)}, u32[]{:S(2)}) collective-permute-start(bf16[192,768]{1,0:T(8,128)(2,1)} %constant_dynamic-slice_fusion.2), channel_id=1, source_target_pairs={{0,1},{1,0},{2,3},{3,2},{4,5},{5,4},{6,7},{7,6},{8,9},{9,8},{10,11... | collective-permute-start | bytes 884744 | tf_op jit(solution)/shard_map/ppermute | solution.py:626
  39.5 19.3 %copy-start.12 = (bf16[1536,768]{1,0:T(8,128)(2,1)S(1)}, bf16[1536,768]{1,0:T(8,128)(2,1)}, u32[]{:S(2)}) copy-start(bf16[1536,768]{1,0:T(8,128)(2,1)} %refs_0_.8) | copy-start | bytes 7077892
  58.9 3.5 collective-permute-start.7
  59.0 28.4 %collective-permute-start.5 = (bf16[768,768]{1,0:T(8,128)(2,1)S(1)}, bf16[768,768]{1,0:T(8,128)(2,1)S(1)}, u32[]{:S(2)}, u32[]{:S(2)}) collective-permute-start(bf16[768,768]{1,0:T(8,128)(2,1)S(1)} %constant_dynamic-slice_fusion.3), channel_id=1, source_target_pairs={{0,1},{1,0},{2,3},{3,2},{4,5},{5,4},{6,7},{7,6},{8,9},{9,8},{10,11... | collective-permute-start | bytes 3538952 | tf_op jit(solution)/shard_map/ppermute | solution.py:626
  60.4 1.9 collective-permute-start.6
  87.4 2.8 collective-permute-start.8
  122.9 8.8 %collective-permute-start.10 = (bf16[2,1536,384]{2,1,0:T(8,128)(2,1)}, bf16[2,1536,384]{2,1,0:T(8,128)(2,1)}, u32[]{:S(2)}, u32[]{:S(2)}) collective-permute-start(bf16[2,1536,384]{2,1,0:T(8,128)(2,1)} %down_gradient.2), channel_id=1, source_target_pairs={{0,2},{2,0},{4,6},{6,4},{8,10},{10,8},{12,14},{14,12},{16,18},{18,... | collective-permute-start | bytes 7077896 | tf_op jit(solution)/shard_map/ppermute | solution.py:629
  129.8 13.8 %collective-permute-start.9 = (bf16[2,1536,384]{2,1,0:T(8,128)(2,1)}, bf16[2,1536,384]{2,1,0:T(8,128)(2,1)S(1)}, u32[]{:S(2)}, u32[]{:S(2)}) collective-permute-start(bf16[2,1536,384]{2,1,0:T(8,128)(2,1)} %row_gradient.4), channel_id=1, source_target_pairs={{0,2},{2,0},{4,6},{6,4},{8,10},{10,8},{12,14},{14,12},{16,18},{18,... | collective-permute-start | bytes 7077896 | tf_op jit(solution)/shard_map/ppermute | solution.py:629
  140.2 47.3 %collective-permute-start.11 = (bf16[1536,384]{1,0:T(8,128)(2,1)}, bf16[1536,384]{1,0:T(8,128)(2,1)S(1)}, u32[]{:S(2)}, u32[]{:S(2)}) collective-permute-start(bf16[1536,384]{1,0:T(8,128)(2,1)} %get-tuple-element.104), channel_id=1, source_target_pairs={{0,1},{1,0},{2,3},{3,2},{4,5},{5,4},{6,7},{7,6},{8,9},{9,8},{10,11... | collective-permute-start | bytes 3538952 | tf_op jit(solution)/shard_map/ppermute | solution.py:626
  187.6 8.1 %copy-start.2 = (bf16[1536,384]{1,0:T(8,128)(2,1)}, bf16[1536,384]{1,0:T(8,128)(2,1)S(1)}, u32[]{:S(2)}) copy-start(bf16[1536,384]{1,0:T(8,128)(2,1)S(1)} %collective-permute-done.11.refs_1_.refs_5_) | copy-start | bytes 3538948
  187.6 8.1 %copy-start.34 = (bf16[1536,384]{1,0:T(8,128)(2,1)S(1)}, bf16[1536,384]{1,0:T(8,128)(2,1)}, u32[]{:S(2)}) copy-start(bf16[1536,384]{1,0:T(8,128)(2,1)} %get-tuple-element.113) | copy-start | bytes 3538948
  195.7 4.9 %collective-permute-start.13 = (bf16[2,1536,384]{2,1,0:T(8,128)(2,1)}, bf16[2,1536,384]{2,1,0:T(8,128)(2,1)}, u32[]{:S(2)}, u32[]{:S(2)}) collective-permute-start(bf16[2,1536,384]{2,1,0:T(8,128)(2,1)} %row_gradient.6), channel_id=1, source_target_pairs={{0,2},{2,0},{4,6},{6,4},{8,10},{10,8},{12,14},{14,12},{16,18},{18,... | collective-permute-start | bytes 7077896 | tf_op jit(solution)/shard_map/ppermute | solution.py:629
  195.7 30.1 %collective-permute-start.12 = (bf16[1536,384]{1,0:T(8,128)(2,1)S(1)}, bf16[1536,384]{1,0:T(8,128)(2,1)S(1)}, u32[]{:S(2)}, u32[]{:S(2)}) collective-permute-start(bf16[1536,384]{1,0:T(8,128)(2,1)S(1)} %copy-done.34), channel_id=1, source_target_pairs={{0,1},{1,0},{2,3},{3,2},{4,5},{5,4},{6,7},{7,6},{8,9},{9,8},{10,11... | collective-permute-start | bytes 3538952 | tf_op jit(solution)/shard_map/ppermute | solution.py:626
  231.5 29.1 %collective-permute-start.30 = (bf16[1536,384]{1,0:T(8,128)(2,1)}, bf16[1536,384]{1,0:T(8,128)(2,1)S(1)}, u32[]{:S(2)}, u32[]{:S(2)}) collective-permute-start(bf16[1536,384]{1,0:T(8,128)(2,1)} %get-tuple-element.137), channel_id=1, source_target_pairs={{0,4},{2,6},{4,0},{6,2},{8,12},{10,14},{12,8},{14,10},{16,20},{18,... | collective-permute-start | bytes 3538952 | tf_op jit(solution)/shard_map/ppermute | solution.py:629
  243.6 54.7 %collective-permute-start.14 = (bf16[1536,384]{1,0:T(8,128)(2,1)}, bf16[1536,384]{1,0:T(8,128)(2,1)S(1)}, u32[]{:S(2)}, u32[]{:S(2)}) collective-permute-start(bf16[1536,384]{1,0:T(8,128)(2,1)} %get-tuple-element.120), channel_id=1, source_target_pairs={{0,1},{1,0},{2,3},{3,2},{4,5},{5,4},{6,7},{7,6},{8,9},{9,8},{10,11... | collective-permute-start | bytes 3538952 | tf_op jit(solution)/shard_map/ppermute | solution.py:626
  261.6 8.0 %copy-start.22 = (f32[1,5376]{1,0:T(1,128)S(1)}, f32[1,5376]{1,0:T(1,128)}, u32[]{:S(2)}) copy-start(f32[1,5376]{1,0:T(1,128)} %get-tuple-element.131) | copy-start | bytes 64516
  261.6 8.1 %copy-start.25 = (f32[1,2304]{1,0:T(1,128)S(1)}, f32[1,2304]{1,0:T(1,128)}, u32[]{:S(2)}) copy-start(f32[1,2304]{1,0:T(1,128)} %get-tuple-element.130) | copy-start | bytes 27652
  265.1 33.2 %copy-start.23 = (f32[2,384]{1,0:T(2,128)S(1)}, f32[2,384]{1,0:T(2,128)}, u32[]{:S(2)}) copy-start(f32[2,384]{1,0:T(2,128)} %get-tuple-element.129) | copy-start | bytes 9220
  265.1 33.2 %copy-start.24 = (f32[2,384]{1,0:T(2,128)S(1)}, f32[2,384]{1,0:T(2,128)}, u32[]{:S(2)}) copy-start(f32[2,384]{1,0:T(2,128)} %get-tuple-element.128) | copy-start | bytes 9220
  265.1 13.2 %collective-permute-start.31 = (bf16[384,384]{1,0:T(8,128)(2,1)}, bf16[384,384]{1,0:T(8,128)(2,1)S(1)}, u32[]{:S(2)}, u32[]{:S(2)}) collective-permute-start(bf16[384,384]{1,0:T(8,128)(2,1)} %get-tuple-element.139), channel_id=1, source_target_pairs={{0,8},{2,10},{4,12},{6,14},{8,0},{10,2},{12,4},{14,6},{16,24},{18,... | collective-permute-start | bytes 884744 | tf_op jit(solution)/shard_map/ppermute | solution.py:629
  266.6 23.7 %collective-permute-start.32 = (bf16[384,384]{1,0:T(8,128)(2,1)}, bf16[384,384]{1,0:T(8,128)(2,1)S(1)}, u32[]{:S(2)}, u32[]{:S(2)}) collective-permute-start(bf16[384,384]{1,0:T(8,128)(2,1)} %get-tuple-element.140), channel_id=1, source_target_pairs={{0,16},{2,18},{4,20},{6,22},{8,24},{10,26},{12,28},{14,30},{16,0},... | collective-permute-start | bytes 884744 | tf_op jit(solution)/shard_map/ppermute | solution.py:629
  269.2 21.1 %collective-permute-start.33 = (bf16[384,384]{1,0:T(8,128)(2,1)}, bf16[384,384]{1,0:T(8,128)(2,1)S(1)}, u32[]{:S(2)}, u32[]{:S(2)}) collective-permute-start(bf16[384,384]{1,0:T(8,128)(2,1)} %get-tuple-element.141), channel_id=1, source_target_pairs={{0,24},{2,26},{4,28},{6,30},{8,16},{10,18},{12,20},{14,22},{16,8},... | collective-permute-start | bytes 884744 | tf_op jit(solution)/shard_map/ppermute | solution.py:629
  291.4 27.4 %copy-start.9 = (bf16[384,384]{1,0:T(8,128)(2,1)}, bf16[384,384]{1,0:T(8,128)(2,1)S(1)}, u32[]{:S(2)}) copy-start(bf16[384,384]{1,0:T(8,128)(2,1)S(1)} %add_convert_fusion.refs_0_) | copy-start | bytes 884740
  291.4 13.5 %collective-permute-start.34 = (bf16[384,384]{1,0:T(8,128)(2,1)S(1)}, bf16[384,384]{1,0:T(8,128)(2,1)S(1)}, u32[]{:S(2)}, u32[]{:S(2)}) collective-permute-start(bf16[384,384]{1,0:T(8,128)(2,1)S(1)} %add_convert_fusion.refs_0_), channel_id=1, source_target_pairs={{0,8},{2,10},{4,12},{6,14},{8,0},{10,2},{12,4},{14,6},{16,24},{18,... | collective-permute-start | bytes 884744 | tf_op jit(solution)/shard_map/ppermute | solution.py:629
  295.9 23.0 %collective-permute-start.35 = (bf16[384,384]{1,0:T(8,128)(2,1)S(1)}, bf16[384,384]{1,0:T(8,128)(2,1)S(1)}, u32[]{:S(2)}, u32[]{:S(2)}) collective-permute-start(bf16[384,384]{1,0:T(8,128)(2,1)S(1)} %add_convert_fusion.refs_0_), channel_id=1, source_target_pairs={{0,16},{2,18},{4,20},{6,22},{8,24},{10,26},{12,28},{14,30},{16,0},... | collective-permute-start | bytes 884744 | tf_op jit(solution)/shard_map/ppermute | solution.py:629
  296.9 22.0 %collective-permute-start.36 = (bf16[384,384]{1,0:T(8,128)(2,1)S(1)}, bf16[384,384]{1,0:T(8,128)(2,1)S(1)}, u32[]{:S(2)}, u32[]{:S(2)}) collective-permute-start(bf16[384,384]{1,0:T(8,128)(2,1)S(1)} %add_convert_fusion.refs_0_), channel_id=1, source_target_pairs={{0,24},{2,26},{4,28},{6,30},{8,16},{10,18},{12,20},{14,22},{16,8},... | collective-permute-start | bytes 884744 | tf_op jit(solution)/shard_map/ppermute | solution.py:629
  302.8 21.0 %collective-permute-start.15 = (bf16[768,384]{1,0:T(8,128)(2,1)}, bf16[768,384]{1,0:T(8,128)(2,1)S(1)}, u32[]{:S(2)}, u32[]{:S(2)}) collective-permute-start(bf16[768,384]{1,0:T(8,128)(2,1)} %get-tuple-element.122), channel_id=1, source_target_pairs={{0,4},{2,6},{4,0},{6,2},{8,12},{10,14},{12,8},{14,10},{16,20},{18,... | collective-permute-start | bytes 1769480 | tf_op jit(solution)/shard_map/ppermute | solution.py:629
  304.9 13.9 %copy-start.14 = (bf16[384,384]{1,0:T(8,128)(2,1)}, bf16[384,384]{1,0:T(8,128)(2,1)S(1)}, u32[]{:S(2)}) copy-start(bf16[384,384]{1,0:T(8,128)(2,1)S(1)} %collective-permute-done.34.refs_1_) | copy-start | bytes 884740
  323.3 40.6 %collective-permute-start.37 = (bf16[1536,384]{1,0:T(8,128)(2,1)}, bf16[1536,384]{1,0:T(8,128)(2,1)S(1)}, u32[]{:S(2)}, u32[]{:S(2)}) collective-permute-start(bf16[1536,384]{1,0:T(8,128)(2,1)} %join_rows.3.refs_0_), channel_id=1, source_target_pairs={{0,4},{2,6},{4,0},{6,2},{8,12},{10,14},{12,8},{14,10},{16,20},{18,... | collective-permute-start | bytes 3538952 | tf_op jit(solution)/shard_map/ppermute | solution.py:629
  324.6 26.8 %copy-start.5 = (bf16[1536,384]{1,0:T(8,128)(2,1)S(1)}, bf16[1536,384]{1,0:T(8,128)(2,1)}, u32[]{:S(2)}) copy-start(bf16[1536,384]{1,0:T(8,128)(2,1)} %join_rows.3.refs_0_) | copy-start | bytes 3538948
  327.6 10.6 %collective-permute-start.16 = (bf16[192,384]{1,0:T(8,128)(2,1)}, bf16[192,384]{1,0:T(8,128)(2,1)S(1)}, u32[]{:S(2)}, u32[]{:S(2)}) collective-permute-start(bf16[192,384]{1,0:T(8,128)(2,1)} %get-tuple-element.124), channel_id=1, source_target_pairs={{0,8},{2,10},{4,12},{6,14},{8,0},{10,2},{12,4},{14,6},{16,24},{18,... | collective-permute-start | bytes 442376 | tf_op jit(solution)/shard_map/ppermute | solution.py:629
  331.8 11.7 %collective-permute-start.17 = (bf16[192,384]{1,0:T(8,128)(2,1)}, bf16[192,384]{1,0:T(8,128)(2,1)S(1)}, u32[]{:S(2)}, u32[]{:S(2)}) collective-permute-start(bf16[192,384]{1,0:T(8,128)(2,1)} %get-tuple-element.125), channel_id=1, source_target_pairs={{0,16},{2,18},{4,20},{6,22},{8,24},{10,26},{12,28},{14,30},{16,0},... | collective-permute-start | bytes 442376 | tf_op jit(solution)/shard_map/ppermute | solution.py:629
  331.8 11.7 %collective-permute-start.18 = (bf16[192,384]{1,0:T(8,128)(2,1)}, bf16[192,384]{1,0:T(8,128)(2,1)S(1)}, u32[]{:S(2)}, u32[]{:S(2)}) collective-permute-start(bf16[192,384]{1,0:T(8,128)(2,1)} %get-tuple-element.126), channel_id=1, source_target_pairs={{0,24},{2,26},{4,28},{6,30},{8,16},{10,18},{12,20},{14,22},{16,8},... | collective-permute-start | bytes 442376 | tf_op jit(solution)/shard_map/ppermute | solution.py:629
  344.4 15.1 %copy-start.13 = (bf16[192,384]{1,0:T(8,128)(2,1)}, bf16[192,384]{1,0:T(8,128)(2,1)S(1)}, u32[]{:S(2)}) copy-start(bf16[192,384]{1,0:T(8,128)(2,1)S(1)} %add_convert_fusion.1.refs_0_) | copy-start | bytes 442372
  344.5 7.0 %collective-permute-start.19 = (bf16[192,384]{1,0:T(8,128)(2,1)S(1)}, bf16[192,384]{1,0:T(8,128)(2,1)S(1)}, u32[]{:S(2)}, u32[]{:S(2)}) collective-permute-start(bf16[192,384]{1,0:T(8,128)(2,1)S(1)} %add_convert_fusion.1.refs_0_), channel_id=1, source_target_pairs={{0,8},{2,10},{4,12},{6,14},{8,0},{10,2},{12,4},{14,6},{16,24},{18,... | collective-permute-start | bytes 442376 | tf_op jit(solution)/shard_map/ppermute | solution.py:629
  347.2 12.4 %collective-permute-start.20 = (bf16[192,384]{1,0:T(8,128)(2,1)S(1)}, bf16[192,384]{1,0:T(8,128)(2,1)S(1)}, u32[]{:S(2)}, u32[]{:S(2)}) collective-permute-start(bf16[192,384]{1,0:T(8,128)(2,1)S(1)} %add_convert_fusion.1.refs_0_), channel_id=1, source_target_pairs={{0,16},{2,18},{4,20},{6,22},{8,24},{10,26},{12,28},{14,30},{16,0},... | collective-permute-start | bytes 442376 | tf_op jit(solution)/shard_map/ppermute | solution.py:629
  347.2 12.4 %collective-permute-start.21 = (bf16[192,384]{1,0:T(8,128)(2,1)S(1)}, bf16[192,384]{1,0:T(8,128)(2,1)S(1)}, u32[]{:S(2)}, u32[]{:S(2)}) collective-permute-start(bf16[192,384]{1,0:T(8,128)(2,1)S(1)} %add_convert_fusion.1.refs_0_), channel_id=1, source_target_pairs={{0,24},{2,26},{4,28},{6,30},{8,16},{10,18},{12,20},{14,22},{16,8},... | collective-permute-start | bytes 442376 | tf_op jit(solution)/shard_map/ppermute | solution.py:629
  349.7 14.3 %collective-permute-start.25 = (f32[36,128]{1,0:T(8,128)S(1)}, f32[36,128]{1,0:T(8,128)S(1)}, u32[]{:S(2)}, u32[]{:S(2)}) collective-permute-start(f32[36,128]{1,0:T(8,128)S(1)} %dynamic-slice_bitcast_fusion), channel_id=1, source_target_pairs={{0,1},{1,0},{2,3},{3,2},{4,5},{5,4},{6,7},{7,6},{8,9},{9,8},{10,11... | collective-permute-start | bytes 55304 | tf_op jit(solution)/shard_map/ppermute | solution.py:626
  351.5 8.1 %copy-start.19 = (bf16[192,384]{1,0:T(8,128)(2,1)}, bf16[192,384]{1,0:T(8,128)(2,1)S(1)}, u32[]{:S(2)}) copy-start(bf16[192,384]{1,0:T(8,128)(2,1)S(1)} %collective-permute-done.19.refs_1_) | copy-start | bytes 442372
  351.5 51.4 %collective-permute-start.38 = (bf16[1536,384]{1,0:T(8,128)(2,1)S(1)}, bf16[1536,384]{1,0:T(8,128)(2,1)}, u32[]{:S(2)}, u32[]{:S(2)}) collective-permute-start(bf16[1536,384]{1,0:T(8,128)(2,1)S(1)} %copy-done.5), channel_id=1, source_target_pairs={{0,2},{2,0},{4,6},{6,4},{8,10},{10,8},{12,14},{14,12},{16,18},{18,... | collective-permute-start | bytes 3538952 | tf_op jit(solution)/shard_map/ppermute | solution.py:629
  363.6 31.1 %collective-permute-start.22 = (bf16[768,384]{1,0:T(8,128)(2,1)}, bf16[768,384]{1,0:T(8,128)(2,1)S(1)}, u32[]{:S(2)}, u32[]{:S(2)}) collective-permute-start(bf16[768,384]{1,0:T(8,128)(2,1)} %join_rows.2.refs_0_), channel_id=1, source_target_pairs={{0,4},{2,6},{4,0},{6,2},{8,12},{10,14},{12,8},{14,10},{16,20},{18,... | collective-permute-start | bytes 1769480 | tf_op jit(solution)/shard_map/ppermute | solution.py:629
  363.9 30.0 %copy-start.8 = (bf16[1536,384]{1,0:T(8,128)(2,1)}, bf16[1536,384]{1,0:T(8,128)(2,1)S(1)}, u32[]{:S(2)}) copy-start(bf16[1536,384]{1,0:T(8,128)(2,1)S(1)} %collective-permute-done.37.refs_1_) | copy-start | bytes 3538948
  363.9 39.0 %collective-permute-start.39 = (bf16[1536,384]{1,0:T(8,128)(2,1)S(1)}, bf16[1536,384]{1,0:T(8,128)(2,1)}, u32[]{:S(2)}, u32[]{:S(2)}) collective-permute-start(bf16[1536,384]{1,0:T(8,128)(2,1)S(1)} %collective-permute-done.37.refs_1_), channel_id=1, source_target_pairs={{0,2},{2,0},{4,6},{6,4},{8,10},{10,8},{12,14},{14,12},{16,18},{18,... | collective-permute-start | bytes 3538952 | tf_op jit(solution)/shard_map/ppermute | solution.py:629
  363.9 2.5 collective-permute-start.26
  366.4 11.3 %collective-permute-start.27 = (f32[36,128]{1,0:T(8,128)S(1)}, f32[36,128]{1,0:T(8,128)S(1)}, u32[]{:S(2)}, u32[]{:S(2)}) collective-permute-start(f32[36,128]{1,0:T(8,128)S(1)} %add.101), channel_id=1, source_target_pairs={{0,4},{2,6},{4,0},{6,2},{8,12},{10,14},{12,8},{14,10},{16,20},{18,... | collective-permute-start | bytes 55304 | tf_op jit(solution)/shard_map/ppermute | solution.py:629
  377.8 4.8 %collective-permute-start.28 = (f32[36,128]{1,0:T(8,128)S(1)}, f32[36,128]{1,0:T(8,128)S(1)}, u32[]{:S(2)}, u32[]{:S(2)}) collective-permute-start(f32[36,128]{1,0:T(8,128)S(1)} %add.102), channel_id=1, source_target_pairs={{0,8},{2,10},{4,12},{6,14},{8,0},{10,2},{12,4},{14,6},{16,24},{18,... | collective-permute-start | bytes 55304 | tf_op jit(solution)/shard_map/ppermute | solution.py:629
  383.2 10.7 %collective-permute-start.29 = (f32[36,128]{1,0:T(8,128)}, f32[36,128]{1,0:T(8,128)}, u32[]{:S(2)}, u32[]{:S(2)}) collective-permute-start(f32[36,128]{1,0:T(8,128)} %add.103), channel_id=1, source_target_pairs={{0,16},{2,18},{4,20},{6,22},{8,24},{10,26},{12,28},{14,30},{16,0},... | collective-permute-start | bytes 55304 | tf_op jit(solution)/shard_map/ppermute | solution.py:629
  384.2 10.5 %copy-start.7 = (bf16[768,384]{1,0:T(8,128)(2,1)S(1)}, bf16[768,384]{1,0:T(8,128)(2,1)}, u32[]{:S(2)}) copy-start(bf16[768,384]{1,0:T(8,128)(2,1)} %join_rows.2.refs_0_) | copy-start | bytes 1769476
  394.7 2.3 collective-permute-start.23
  394.7 3.1 collective-permute-start.24
  (16 other events, 20.1 us)

commit v3 on v2

--- a/solution.py
+++ b/solution.py
@@ -28,7 +28,7 @@
 B_QV, B_OUT, ATTN_GAIN, ATTN_SHIFT = 0, 2 * D, 3 * D, 4 * D
 B_UP, B_DOWN, FFN_GAIN, FFN_SHIFT = 5 * D, 5 * D + FF, 6 * D + FF, 7 * D + FF
 VECTORS = 8 * D + FF
-CORE, X, Z, Y = 0, 1, 2, 3
+CORE, X, Z, Y, Z_BITS = 0, 1, 2, 3, 4
 
 
 def matmul(left, right):
@@ -66,7 +66,9 @@
 ANYWHERE = pl.BlockSpec(memory_space=pl.ANY)
 
 
-def call(body, name, out_shape, grid, in_specs, out_specs, scratch=(), flops=0, exps=0):
+def call(
+    body, name, out_shape, grid, in_specs, out_specs, scratch=(), flops=0, exps=0, aliases=None
+):
     return pl.pallas_call(
         body,
         out_shape=out_shape,
@@ -78,6 +80,7 @@
             scratch_shapes=list(scratch),
         ),
         cost_estimate=pl.CostEstimate(flops=flops, transcendentals=exps, bytes_accessed=1 << 20),
+        input_output_aliases=aliases or {},
         name=name,
     )
 
@@ -489,7 +492,7 @@
     total = d_sum[...]
     for piece, (partner, first, count) in zip(pieces, spans):
         block = 1 - place[CORE] if partner else place[CORE]
-        at = pl.multiple_of((block * HALF_PAIRS + first) * TRIPLE, WIDE)
+        at = pl.multiple_of((first + block * count) * TRIPLE, WIDE)
         total += matmul_right_t(piece[...], weight[:, pl.ds(at, count * TRIPLE)])
     output[...] = rounded(total)
 
@@ -506,19 +509,12 @@
     )(place, weight, d_sum, *pieces)
 
 
-def shard_row(place, d, rows):
-    return pl.multiple_of(jnp.bitwise_xor(place[Y], d) * rows, rows)
-
-
-def gradient_specs(shards, rows, block, got, index):
-    if got is None:
-        return shape((shards, rows, CHUNK)), pl.BlockSpec((shards, block, CHUNK), index), []
-    one = pl.BlockSpec((block, CHUNK), lambda *at: index(*at)[1:])
-    return (
-        (shape((rows, CHUNK)),) * shards,
-        [one] * shards,
-        [pl.BlockSpec((shards, block, CHUNK), index)],
-    )
+def piece_row(place, piece, rows, cuts):
+    dy, dx = divmod(piece, cuts)
+    start = jnp.bitwise_xor(place[Y], dy) * (cuts * rows)
+    if cuts == 2:
+        start += jnp.bitwise_xor(place[X], dx) * rows
+    return pl.multiple_of(start, 16)
 
 
 def down_gradient_body(place, left, right, *refs, shards, adds):
@@ -526,20 +522,18 @@
     if not adds:
         refs[0][0] = rounded(value)
         return
-    got, outs = refs[0], refs[1:]
-    value = rounded(value + as_float(got[0]))
+    value = rounded(value + as_float(refs[0][0]))
     for at in range(shards):
 
-        @pl.when(pl.program_id(0) == shards - 1 - at)
+        @pl.when(pl.program_id(0) == at)
         def _(at=at):
-            outs[at][...] = value
+            refs[1 + at][...] = value
 
 
 def down_gradient(place, activated, d_down, partner, shards, got=None):
     rows = FF // shards
-    order = lambda i: shards - 1 - i
     pick_column = lambda i, p: (0, 1 - p[CORE] if partner else p[CORE])
-    one = pl.BlockSpec((1, rows, CHUNK), lambda i, p: (order(i), 0, 0))
+    one = pl.BlockSpec((1, rows, CHUNK), lambda i, p: (i, 0, 0))
     operands, specs = [activated, d_down], []
     if got is None:
         outs, out_specs = shape((shards, rows, CHUNK)), one
@@ -553,7 +547,7 @@
         outs,
         (shards,),
         [
-            pl.BlockSpec((LEN, rows), lambda i, p: (0, jnp.bitwise_xor(p[Y], order(i)))),
+            pl.BlockSpec((LEN, rows), lambda i, p: (0, jnp.bitwise_xor(p[Y], i))),
             pl.BlockSpec((LEN, CHUNK), pick_column),
         ]
         + specs,
@@ -562,55 +556,63 @@
     )(place, *operands)
 
 
-def row_gradient_body(place, *refs, terms, shards, adds):
-    rows = D // shards
-    operands, rest = refs[: 2 * terms], refs[2 * terms :]
-    got, outs, total = (rest[0], rest[1:-1], rest[-1]) if adds else (None, rest[:-1], rest[-1])
-    block = 0
-    for term in range(terms):
-        left, right = operands[2 * term : 2 * term + 2]
-        width = right.shape[1]
-        total[:, :width] = matmul_left_t(left[...], right[...])
-        for j in range(width // CHUNK):
-            here = slice(block * rows, (block + 1) * rows)
-            block += 1
-            for d in range(shards):
-                value = total[pl.ds(shard_row(place, d, rows), rows), j * CHUNK : (j + 1) * CHUNK]
-                if adds:
-                    outs[d][here, :] = rounded(value + as_float(got[d, here, :]))
-                else:
-                    outs[0][d, here, :] = rounded(value)
-
-
-def row_gradient(place, terms, shards, steps=1, got=None):
-    rows = D // shards
-    widths = [right_width for _, _, right_width, _ in terms]
-    count = sum(widths) // CHUNK
-    block = count * rows
-    specs, operands = [], []
-    for left, right, width, first in terms:
-        specs.append(constant((LEN, D)))
-        specs.append(pl.BlockSpec((LEN, width), lambda i, p, first=first: (0, first(p) + i)))
-        operands += [left, right]
-    all_rows = pl.BlockSpec((shards, block, CHUNK), lambda i, p: (0, i, 0))
-    one = pl.BlockSpec((block, CHUNK), lambda i, p: (i, 0))
+def row_gradient_body(place, left, right, *refs, pieces, cuts, adds, extends):
+    got, refs = (refs[0], refs[1:]) if adds else (None, refs)
+    outs, total = refs[pieces if extends else 0 : -1], refs[-1]
+    rows = D // pieces
+    total[...] = matmul_left_t(left[...], right[...])
+    for j in range(right.shape[1] // CHUNK):
+        here = slice(j * rows, (j + 1) * rows)
+        for piece in range(pieces):
+            start = piece_row(place, piece, rows, cuts)
+            value = total[pl.ds(start, rows), j * CHUNK : (j + 1) * CHUNK]
+            if adds:
+                outs[piece][here, :] = rounded(value + as_float(got[piece, here, :]))
+            else:
+                outs[0][piece, here, :] = rounded(value)
+
+
+def row_gradient(
+    place, left, right, width, first, steps, pieces, cuts, got=None, spare=0, into=None
+):
+    rows = D // pieces
+    block = width // CHUNK * rows
+    specs = [
+        constant((LEN, D)),
+        pl.BlockSpec((LEN, width), lambda i, p: (0, first(p) + i)),
+    ]
+    operands, aliases, at = [left, right], {}, 0
     if got is None:
-        outs, out_specs = shape((shards, steps * block, CHUNK)), all_rows
+        outs = shape((pieces, steps * block, CHUNK))
+        out_specs = pl.BlockSpec((pieces, block, CHUNK), lambda i, p: (0, i, 0))
     else:
-        specs.append(all_rows)
+        specs.append(pl.BlockSpec((pieces, block, CHUNK), lambda i, p: (0, i, 0)))
         operands.append(got)
-        outs, out_specs = (shape((steps * block, CHUNK)),) * shards, [one] * shards
+        height = steps * block + spare * rows
+        if into is not None:
+            height = into[0].shape[0]
+            at = height // block - steps
+            aliases = {len(operands) + 1 + n: n for n in range(pieces)}
+            operands += into
+            specs += [ANYWHERE] * pieces
+        outs = (shape((height, CHUNK)),) * pieces
+        out_specs = [pl.BlockSpec((block, CHUNK), lambda i, p: (at + i, 0))] * pieces
     return call(
         functools.partial(
-            row_gradient_body, terms=len(terms), shards=shards, adds=got is not None
+            row_gradient_body,
+            pieces=pieces,
+            cuts=cuts,
+            adds=got is not None,
+            extends=into is not None,
         ),
         "row_gradient",
         outs,
         (steps,),
         specs,
         out_specs,
-        [pltpu.VMEM((D, max(widths)), F32)],
-        flops=2 * LEN * D * sum(widths) * steps,
+        [pltpu.VMEM((D, width), F32)],
+        flops=2 * LEN * D * width * steps,
+        aliases=aliases,
     )(place, *operands)
 
 
@@ -620,10 +622,20 @@
         replica = lax.axis_index("replica")
         self.index = [replica % 2, replica // 2 % 2, replica // 4, lax.axis_index("shard")]
         self.core, self.x, self.z, self.y = self.index
+        self.z_bits = self.depth.bit_length() - 1
+        self.index += [self.z >> bit & 1 for bit in range(self.z_bits)]
         self.vector = jnp.stack(self.index).astype(jnp.int32)
 
     def shard(self, value, mask):
         return lax.ppermute(value, "shard", [(i, i ^ mask) for i in range(self.shards)])
+
+    def cross(self, value, dy, dx):
+        def partner(i):
+            replica, shard = divmod(i, self.shards)
+            return (replica ^ (2 * dx)) * self.shards + (shard ^ dy)
+
+        pairs = [(i, partner(i)) for i in range(self.replicas * self.shards)]
+        return lax.ppermute(value, ("replica", "shard"), pairs)
 
     def replica(self, value, mask):
         return lax.ppermute(value, "replica", [(i, i ^ mask) for i in range(self.replicas)])
@@ -660,6 +672,10 @@
     for block in near[1:]:
         pieces += [block, at.replica(block, 1)]
     return pieces
+
+
+def exchange_pieces(parts, at):
+    return [parts[0]] + [at.cross(parts[n], *divmod(n, 2)) for n in range(1, len(parts))]
 
 
 def exchange_shards(parts, at):
@@ -673,174 +689,267 @@
     return parts[0], at.shard(parts[1], 1)
 
 
-def split_body(place, *refs, count, parts):
-    outs = refs[2 * count * parts :]
-    for d in range(parts):
-        row = 0
-        for at in range(count):
-            keep, got = refs[2 * (d * count + at) : 2 * (d * count + at) + 2]
-            height = keep.shape[0]
-            outs[d][row : row + height, :] = rounded(as_float(keep[...]) + as_float(got[...]))
-            row += height
-
-
-def split_add(at, which, groups, parts):
-    heights = [keep.shape[0] // parts for keep, _ in groups]
-    index = at.index[which]
-    if any(height % 16 for height in heights):
+def row_block(rows, block):
+    return pl.BlockSpec((rows, CHUNK), lambda i, p: (block(p), 0))
+
+
+def add_job(at, groups, parts, block, plain_block):
+    heights = [rows // parts for _, rows, _ in groups]
+    if any(h % 16 or first % h for h, (_, _, first) in zip(heights, groups)):
         found = []
-        for d in range(parts):
-            blocks = []
-            for (keep, got), height in zip(groups, heights):
-                cut = lambda v: lax.dynamic_slice_in_dim(v, (index ^ d) * height, height, 0)
-                blocks.append(rounded(as_float(cut(keep)) + as_float(cut(got))))
-            found.append(jnp.concatenate(blocks) if len(blocks) > 1 else blocks[0])
+        for n in range(parts):
+            cuts = []
+            for (terms, _, first), h in zip(groups, heights):
+                start = first + plain_block(n) * h
+                cut = [as_float(lax.dynamic_slice_in_dim(t, start, h, 0)) for t in terms]
+                cuts.append(rounded(sum(cut)))
+            found.append(jnp.concatenate(cuts) if len(cuts) > 1 else cuts[0])
         return found
+    count = sum(len(terms) for terms, _, _ in groups)
+
+    def body(place, ins, outs):
+        for n in range(parts):
+            at_term, row = n * count, 0
+            for (terms, _, _), h in zip(groups, heights):
+                total = as_float(ins[at_term][...])
+                for term in range(1, len(terms)):
+                    total += as_float(ins[at_term + term][...])
+                outs[n][row : row + h, :] = rounded(total)
+                at_term, row = at_term + len(terms), row + h
+
     specs, operands = [], []
-    for d in range(parts):
-        for (keep, got), height in zip(groups, heights):
-            spec = pl.BlockSpec(
-                (height, CHUNK), lambda i, p, d=d: (jnp.bitwise_xor(p[which], d), 0)
-            )
-            specs += [spec, spec]
-            operands += [keep, got]
-    total = sum(heights)
-    return call(
-        functools.partial(split_body, count=len(groups), parts=parts),
-        "split_add",
-        (shape((total, CHUNK)),) * parts,
-        (1,),
-        specs,
-        [constant((total, CHUNK))] * parts,
-    )(at.vector, *operands)
-
-
-def join_body(place, *refs, which):
-    output = refs[-1]
-    for d, piece in enumerate(refs[:-1]):
-        height = piece.shape[0]
-        start = pl.multiple_of(jnp.bitwise_xor(place[which], d) * height, 16)
-        output[pl.ds(start, height), :] = piece[...]
-
-
-def join_rows(at, which, pieces):
-    height, parts = pieces[0].shape[0], len(pieces)
-    index = at.index[which]
-    if height % 16:
-        return jnp.concatenate([pick(pieces, index ^ j) for j in range(parts)])
-    return call(
-        functools.partial(join_body, which=which),
-        "join_rows",
-        shape((parts * height, CHUNK)),
-        (1,),
-        [constant((height, CHUNK))] * parts,
-        constant((parts * height, CHUNK)),
-    )(at.vector, *pieces)
-
-
-def sum_replicas(groups, at):
-    keep, send = split_add(at, X, groups, 2)
-    return finish_sum(keep, at.replica(send, 2), at)
-
-
-def finish_sum(keep, got, at):
-    blocks = split_add(at, Z, [(keep, got)], at.depth)
-    total = as_float(blocks[0])
-    for d in range(1, at.depth):
-        total += as_float(at.replica(blocks[d], 4 * d))
-    total = rounded(total)
-    found = [total] + [at.replica(total, 4 * d) for d in range(1, at.depth)]
-    mine = join_rows(at, Z, found)
-    other = at.replica(mine, 2)
+    for n in range(parts):
+        for (terms, _, first), h in zip(groups, heights):
+            where = lambda p, n=n, base=first // h: base + block(n, p)
+            specs += [row_block(h, where)] * len(terms)
+            operands += terms
+    results = [jax.ShapeDtypeStruct((sum(heights), CHUNK), LOW)] * parts
+    return body, operands, specs, results
+
+
+def all_rows(terms):
+    return terms, terms[0].shape[0], 0
+
+
+def halve(at, which, *groups):
+    return add_job(
+        at,
+        groups,
+        2,
+        lambda n, p: jnp.bitwise_xor(p[which], n),
+        lambda n: at.index[which] ^ n,
+    )
+
+
+def add_small(value, got):
+    def body(place, ins, outs):
+        outs[0][...] = ins[0][...] + ins[1][...]
+
+    spec = constant(value.shape)
+    return body, [value, got], [spec, spec], [jax.ShapeDtypeStruct(value.shape, F32)]
+
+
+def split_z(at, terms):
+    return add_job(
+        at, [all_rows(terms)], at.depth, lambda n, p: jnp.bitwise_xor(p[Z], n), lambda n: at.z ^ n
+    )
+
+
+def total(at, terms):
+    return add_job(at, [all_rows(terms)], 1, lambda n, p: 0, lambda n: 0)
+
+
+def join(at, pieces, block, plain_block):
+    rows = pieces[0].shape[0]
+    count = len(pieces)
+    if rows % 16:
+        where = [plain_block(n) for n in range(count)]
+        joined = []
+        for j in range(count):
+            chosen = pieces[0]
+            for n in range(1, count):
+                chosen = jnp.where(where[n] == j, pieces[n], chosen)
+            joined.append(chosen)
+        return [jnp.concatenate(joined)]
+
+    def body(place, ins, outs):
+        for n in range(count):
+            start = pl.multiple_of(block(n, place) * rows, 16)
+            outs[0][pl.ds(start, rows), :] = ins[n][...]
+
+    result = jax.ShapeDtypeStruct((rows * count, CHUNK), LOW)
+    return body, list(pieces), [constant((rows, CHUNK))] * count, [result]
+
+
+def join_z(at, pieces):
+    return join(at, pieces, lambda n, p: jnp.bitwise_xor(p[Z], n), lambda n: at.z ^ n)
+
+
+def bit_order(at):
+    order = [0]
+    for bit in reversed(range(at.z_bits)):
+        order += [d | 1 << bit for d in order]
+    return order
+
+
+def join_bits(at, pieces):
+    order, top = bit_order(at), at.z_bits - 1
+
+    def place_of(n, bits):
+        return sum((bits[bit] ^ (order[n] >> bit & 1)) << (top - bit) for bit in range(at.z_bits))
+
+    return join(
+        at,
+        pieces,
+        lambda n, p: place_of(n, [p[Z_BITS + bit] for bit in range(at.z_bits)]),
+        lambda n: place_of(n, at.index[Z_BITS:]),
+    )
+
+
+def join_split(at, pieces):
+    order = bit_order(at)
+    return join(
+        at, pieces, lambda n, p: jnp.bitwise_xor(p[Z], order[n]), lambda n: at.z ^ order[n]
+    )
+
+
+def run_jobs(at, *jobs):
+    results = [job if isinstance(job, list) else None for job in jobs]
+    todo = [n for n, job in enumerate(jobs) if not isinstance(job, list)]
+    if todo:
+        operands, specs, outs = [], [], []
+        for n in todo:
+            operands += jobs[n][1]
+            specs += jobs[n][2]
+            outs += jobs[n][3]
+
+        def body(place, *refs):
+            ins, outs = refs[: len(operands)], refs[len(operands) :]
+            for n in todo:
+                job_body, job_ins, _, job_outs = jobs[n]
+                job_body(place, ins[: len(job_ins)], outs[: len(job_outs)])
+                ins, outs = ins[len(job_ins) :], outs[len(job_outs) :]
+
+        found = call(
+            body,
+            "exchange_step",
+            outs,
+            (1,),
+            specs,
+            [constant(out.shape) for out in outs],
+        )(at.vector, *operands)
+        for n in todo:
+            count = len(jobs[n][3])
+            results[n], found = list(found[:count]), found[count:]
+    return results
+
+
+def send_x(halves, at):
+    return halves[0], at.replica(halves[1], 2)
+
+
+def send_bit(halves, bit, at):
+    return halves[0], at.replica(halves[1], 4 << bit)
+
+
+def send_z(blocks, at):
+    return [blocks[0]] + [at.replica(blocks[d], 4 * d) for d in range(1, at.depth)]
+
+
+def spread_z(whole, at):
+    return [whole] + [at.replica(whole, 4 * d) for d in range(1, at.depth)]
+
+
+def spread_bit(found, bit, at):
+    return found + [at.replica(piece, 4 << bit) for piece in found]
+
+
+def spread_x(mine, at):
+    return mine, at.replica(mine, 2)
+
+
+def spread_core(mine, other, at):
     return [mine, other, at.replica(mine, 1), at.replica(other, 1)]
 
 
-def finish_feed_body(place, *refs, rows, blocks):
-    sources, (down, up) = refs[:4], refs[4:]
-    at = pl.program_id(0)
-    half = blocks * rows
+def finish_down_body(place, *refs):
     for index in range(4):
 
-        @pl.when(at == index)
+        @pl.when(pl.program_id(0) == index)
+        def _(index=index):
+            refs[4][...] = as_float(refs[index][...])
+
+
+def finish_up_body(place, *refs, rows, blocks):
+    sources, (up, out) = refs[:4], refs[4:]
+    for index in range(4):
+
+        @pl.when(pl.program_id(0) == index)
         def _(index=index):
             source = sources[index]
-            down[...] = as_float(source[: down.shape[0], :])
             for j in range(blocks):
-                start = down.shape[0] + j * rows
-                up[:, j * CHUNK : (j + 1) * CHUNK] = as_float(source[start : start + rows, :])
-
-
-def finish_feed(at, sources):
-    rows, down_rows = D // at.shards, FF // at.shards
+                up[:, j * CHUNK : (j + 1) * CHUNK] = as_float(source[j * rows : (j + 1) * rows, :])
+            out[...] = as_float(source[blocks * rows :, :])
+
+
+def finish_down(at, sources):
+    rows = FF // at.shards
+    half = lambda i, p: jnp.bitwise_xor(p[X], i % 2)
+    core = lambda i, p: jnp.bitwise_xor(p[CORE], i // 2)
+    return call(
+        finish_down_body,
+        "finish_down",
+        shape((rows, D), F32),
+        (4,),
+        [constant(source.shape) for source in sources],
+        pl.BlockSpec((rows // 2, CHUNK), lambda i, p: (half(i, p), core(i, p))),
+    )(at.vector, *sources)
+
+
+def finish_up(at, sources):
+    rows = D // at.shards
     blocks = FF // (4 * CHUNK)
     half = lambda i, p: jnp.bitwise_xor(p[X], i % 2)
     core = lambda i, p: jnp.bitwise_xor(p[CORE], i // 2)
     return call(
-        functools.partial(finish_feed_body, rows=rows, blocks=blocks),
-        "finish_feed",
-        (shape((down_rows, D), F32), shape((rows, FF), F32)),
+        functools.partial(finish_up_body, rows=rows, blocks=blocks),
+        "finish_up",
+        (shape((rows, FF), F32), shape((rows, D), F32)),
         (4,),
         [constant(source.shape) for source in sources],
         [
-            pl.BlockSpec((down_rows // 2, CHUNK), lambda i, p: (half(i, p), core(i, p))),
             pl.BlockSpec((rows, blocks * CHUNK), lambda i, p: (0, core(i, p) * 2 + half(i, p))),
+            pl.BlockSpec((rows // 2, CHUNK), lambda i, p: (half(i, p), core(i, p))),
         ],
     )(at.vector, *sources)
 
 
-def finish_attention_body(place, *refs, layouts, rows):
-    groups = len(layouts)
-    sources, (qkv, out), holds = refs[: 4 * groups], refs[4 * groups : 4 * groups + 2], refs[4 * groups + 2 :]
-    for group, layout in enumerate(layouts):
-        hold = holds[group]
-        for index in range(4):
-            source = sources[4 * group + index]
-            height = source.shape[0]
-            start = pl.multiple_of(jnp.bitwise_xor(place[X], index % 2) * height, 16)
-            hold[index // 2, pl.ds(start, height), :] = source[...]
-        for side in range(2):
-            core = jnp.bitwise_xor(place[CORE], side)
-            for block, name in enumerate(layout):
-                value = as_float(hold[side, block * rows : (block + 1) * rows, :])
-                if name is None:
-                    out[:, pl.ds(pl.multiple_of(core * CHUNK, WIDE), CHUNK)] = value
-                    continue
-                for part in range(3):
-                    lane = part * D + (core * HALF_PAIRS + name) * WIDE
-                    qkv[:, pl.ds(pl.multiple_of(lane, WIDE), WIDE)] = value[
-                        :, part * WIDE : (part + 1) * WIDE
-                    ]
-
-
-def finish_attention(at, groups, layouts):
+def finish_attention_body(place, *refs, rows):
+    sources, qkv = refs[:4], refs[4]
+    half = rows // 2
+    for index in range(4):
+        source = sources[index]
+        core = jnp.bitwise_xor(place[CORE], index // 2)
+        start = pl.multiple_of(jnp.bitwise_xor(place[X], index % 2) * half, 16)
+        for pair in range(HALF_PAIRS):
+            value = as_float(source[pair * half : (pair + 1) * half, :])
+            for part in range(3):
+                lane = pl.multiple_of(part * D + (core * HALF_PAIRS + pair) * WIDE, WIDE)
+                qkv[pl.ds(start, half), pl.ds(lane, WIDE)] = value[
+                    :, part * WIDE : (part + 1) * WIDE
+                ]
+
+
+def finish_attention(at, sources):
     rows = D // at.shards
-    operands = [source for group in groups for source in group]
     return call(
-        functools.partial(finish_attention_body, layouts=layouts, rows=rows),
+        functools.partial(finish_attention_body, rows=rows),
         "finish_attention",
-        (shape((rows, 3 * D), F32), shape((rows, D), F32)),
+        shape((rows, 3 * D), F32),
         (1,),
-        [constant(source.shape) for source in operands],
-        [constant((rows, 3 * D)), constant((rows, D))],
-        [pltpu.VMEM((2, len(layout) * rows, CHUNK), LOW) for layout in layouts],
-    )(at.vector, *operands)
-
-
-def sum_small(values, at):
-    parts = [lax.dynamic_index_in_dim(values, at.y ^ d, 0, False) for d in range(at.shards)]
-    mask = at.shards // 2
-    while mask:
-        parts = [parts[d] + at.shard(parts[d | mask], mask) for d in range(mask)]
-        mask //= 2
-    total = parts[0]
-    mask = 1
-    while mask < at.replicas:
-        total = total + at.replica(total, mask)
-        mask *= 2
-    return total
-
-
-ATTENTION_GROUPS = ((0, 3),)
+        [constant(source.shape) for source in sources],
+        constant((rows, 3 * D)),
+    )(at.vector, *sources)
 
 
 def local(
@@ -902,64 +1011,81 @@
         place, activated, slope, normal, cotangent, full, pieces_down
     )
 
+    barrier = lax.optimization_barrier
+    zero = lambda p: 0
+    other_core, own_core = (lambda p: 1 - p[CORE]), (lambda p: p[CORE])
+    other_half, own_half = (lambda p: 2 * (1 - p[CORE])), (lambda p: 2 * p[CORE])
+    wide, packed_width = FF // 4, HALF_PAIRS * TRIPLE
+
     down_send = down_gradient(place, activated, d_down, True, shards)
     down_got = at.replica(down_send, 1)
-    up_width = FF // 4
-    other_half, own_half = (lambda p: 2 * (1 - p[CORE])), (lambda p: 2 * p[CORE])
-    up_send = row_gradient(place, [(low, d_up, up_width, other_half)], shards, 2)
+    up_send = row_gradient(place, low, d_up, wide, other_half, 2, shards, 1)
     up_got = at.replica(up_send, 1)
     down_parts = down_gradient(place, activated, d_down, False, shards, down_got)
-    down_pair = exchange_shards(down_parts, at)
-    up_parts = row_gradient(place, [(low, d_up, up_width, own_half)], shards, 2, up_got)
-    up_parts, d_up = lax.optimization_barrier((up_parts, d_up))
+    down = exchange_shards(down_parts, at)
+    up_parts = row_gradient(place, low, d_up, wide, own_half, 2, shards, 1, up_got, 1)
+    up_parts, d_up = barrier((up_parts, d_up))
     d_sum_one, d_attended, d_context, sums_one = back_block(
         place, d_up, d_sum_two, normal, inverse, full, pieces_up, pieces_out
     )
 
-    def attention_back(block, first, count, d_context):
-        start = (block * HALF_PAIRS + first) // count
+    def attention_back(index, d_context):
         return attn_bwd(
-            jnp.concatenate([backward_ranges, start.reshape(1)]),
+            jnp.concatenate([backward_ranges, index.reshape(1)]),
             projected,
             context,
             d_context,
             log_total,
             feature_q,
             feature_k,
-            count,
-            count,
+            HALF_PAIRS,
+            HALF_PAIRS,
         )
 
-    d_other, bias_other = attention_back(1 - at.core, 0, 3, d_context)
-    down_pair, d_other = lax.optimization_barrier((down_pair, d_other))
-    up_parts = tie(up_parts, down_pair[1])
-    up_pair = exchange_shards(up_parts, at)
-    other_out, own_out = (lambda p: 1 - p[CORE]), (lambda p: p[CORE])
-    zero = lambda p: 0
-    send = row_gradient(
+    bits = at.z_bits
+    pieces = 2 * shards
+    out_send = row_gradient(place, context, d_attended, CHUNK, other_core, 1, shards, 1)
+    out_got = at.replica(out_send, 1)
+    down, out_send = barrier((down, out_send))
+    (down,) = run_jobs(at, halve(at, X, all_rows(down)))
+    up_parts = row_gradient(
         place,
-        [(inputs, d_other, 3 * TRIPLE, zero), (context, d_attended, CHUNK, other_out)],
-        shards,
-    )
-    got = at.replica(send, 1)
-    d_context, got = lax.optimization_barrier((d_context, got))
-    d_own, bias_own = attention_back(at.core, 0, 3, d_context)
-    up_pair, d_own = lax.optimization_barrier((up_pair, d_own))
-    parts = row_gradient(
-        place,
-        [(inputs, d_own, 3 * TRIPLE, zero), (context, d_attended, CHUNK, own_out)],
+        context,
+        d_attended,
+        CHUNK,
+        own_core,
+        1,
         shards,
         1,
-        got,
-    )
-    attention_pair = exchange_shards(parts, at)
-    feed = sum_replicas([down_pair, up_pair], at)
-    attention_sum = sum_replicas([attention_pair], at)
-    input_grad = input_gradient(
-        place, weight_qkv, d_sum_one, [d_other, d_own], ((True, 0, 3), (False, 0, 3))
-    )
-    grad_w_down, grad_w_up = finish_feed(at, feed)
-    grad_w_qkv, grad_w_out = finish_attention(at, [attention_sum], ((0, 1, 2, None),))
+        tie(out_got, down[0]),
+        0,
+        up_parts,
+    )
+    down = send_x(down, at)
+    up = exchange_shards(up_parts, at)
+    up_parts, d_context = barrier((up_parts, d_context))
+    d_other, bias_other = attention_back(1 - at.core, d_context)
+    down, d_other, d_context = barrier((down, d_other, d_context))
+    (down,) = run_jobs(at, split_z(at, down))
+    send = row_gradient(
+        place, inputs, tie(d_other, down[0]), packed_width, zero, 1, pieces, 2
+    )
+    down = send_z(down, at)
+    got = at.replica(send, 1)
+    up, send, d_context = barrier((up, send, d_context))
+    up_rows = FF // (2 * CHUNK) * (D // shards)
+    (up,) = run_jobs(
+        at, halve(at, X, (up, up_rows, 0), (up, D // shards, up_rows))
+    )
+    up = send_x(up, at)
+    d_own, bias_own = attention_back(at.core, tie(d_context, up[0]))
+    up, down, d_own, got = barrier((up, down, d_own, got))
+    (up,) = run_jobs(at, halve(at, Z_BITS, all_rows(up)))
+    parts = row_gradient(
+        place, inputs, tie(d_own, up[0]), packed_width, zero, 1, pieces, 2, got
+    )
+    up = send_bit(up, 0, at)
+    mine = exchange_pieces(parts, at)
 
     bias = jnp.concatenate(
         [pick([bias_own, bias_other], at.core), pick([bias_other, bias_own], at.core)], axis=1
@@ -976,7 +1102,68 @@
         sums_two[D : 2 * D],
     )
     packed = jnp.concatenate([grad.reshape(shards, -1) for grad in grads], axis=1)
-    packed = sum_small(packed.reshape(shards, -1, 128), at).reshape(-1)
+    packed = packed.reshape(shards, -1, 128)
+    small = [lax.dynamic_index_in_dim(packed, at.y ^ d, 0, False) for d in range(shards)]
+    mask = shards // 2
+    while mask > 1:
+        small = [small[d] + at.shard(small[d | mask], mask) for d in range(mask)]
+        mask //= 2
+
+    down, up, d_own, small, parts = barrier((down, up, d_own, small, parts))
+    if bits > 1:
+        down, up = run_jobs(at, total(at, down), halve(at, Z_BITS + 1, all_rows(up)))
+        up = send_bit(up, 1, at)
+        for bit in range(2, bits):
+            (up,) = run_jobs(at, halve(at, Z_BITS + bit, all_rows(up)))
+            up = send_bit(up, bit, at)
+    else:
+        (down,) = run_jobs(at, total(at, down))
+    down, d_own = barrier((down, d_own))
+    down = spread_bit(down, bits - 1, at)
+    input_grad = input_gradient(
+        place,
+        weight_qkv,
+        d_sum_one,
+        [d_other, d_own],
+        ((True, 0, HALF_PAIRS), (False, 0, HALF_PAIRS)),
+    )
+    down, up, input_grad = barrier((down, up, input_grad))
+    (up,) = run_jobs(at, total(at, up))
+    mine, up = barrier((mine, up))
+    (mine,) = run_jobs(at, split_z(at, mine))
+    mine = send_z(mine, at)
+    for bit in reversed(range(bits - 1)):
+        down = spread_bit(down, bit, at)
+    up = spread_bit(up, bits - 1, at)
+    small = (small[0], at.shard(small[1], 1))
+    down, up, small, kept = barrier((down, up, small, mine[0]))
+    down, small = run_jobs(at, join_split(at, down), add_small(*small))
+    small = (small[0], at.replica(small[0], 1))
+    mine, small, kept = barrier((mine, small, down))
+    mine, small = run_jobs(at, total(at, mine), add_small(*small))
+    down = spread_x(kept[0], at)
+    mine = spread_z(mine[0], at)
+    for bit in reversed(range(bits - 1)):
+        up = spread_bit(up, bit, at)
+    small = (small[0], at.replica(small[0], 2))
+    up, small, kept = barrier((up, small, mine[0]))
+    up, small = run_jobs(at, join_bits(at, up), add_small(*small))
+    mine, up, small = barrier((mine, up, small))
+    (mine,) = run_jobs(at, join_z(at, mine))
+    mine = spread_x(mine[0], at)
+    up = spread_x(up[0], at)
+    small = (small[0], at.replica(small[0], 4))
+    down, kept, small = barrier((down, mine[0], small))
+    grad_w_down = finish_down(at, spread_core(*down, at))
+    small = small[0] + small[1]
+    for bit in range(1, bits):
+        small = small + at.replica(small, 4 << bit)
+    up, grad_w_down, small = barrier((up, grad_w_down, small))
+    grad_w_up, grad_w_out = finish_up(at, spread_core(*up, at))
+    mine, grad_w_up = barrier((mine, grad_w_up))
+    grad_w_qkv = finish_attention(at, spread_core(*mine, at))
+
+    packed = small.reshape(-1)
     owned, offset = [], 0
     for size in sizes:
         owned.append(packed[offset : offset + size])

time: 417 us -> 375 us (0.90)
  waiting for transfers between devices: 120 us -> 49 us
  Pallas kernels: 211 us -> 238 us
    ppermute x31 -> x40, waiting for transfers between devices: 92 us -> 30.4 us  [replica(): lax.ppermute(value, 'replica', [(i, i ^ mask) for i in range(self.replica...]
    pallas_call x12 -> x20, Pallas kernels: 63.6 us -> 83.1 us  [the longest x6 36.9 us: row_gradient(): call(functools.partial(row_gradient_body, pieces=pieces, cuts=cuts, adds=...]
    ppermute x9 -> x8, waiting for transfers between devices: 28 us -> 18.6 us  [shard(): lax.ppermute(value, 'shard', [(i, i ^ mask) for i in range(self.shards)])]
    pallas_call x2, Pallas kernels: 35.2 us -> 41 us  [attn_bwd(): pl.pallas_call(lambda *a: bwd_body(*a, group=group), out_shape=(jax.Shape...]
    unnamed x105 -> x153, local copies, waits for them, and re-layouts: 14.2 us -> 17.1 us
    ppermute x9 -> x8, starting transfers between devices: 12.2 us -> 10.5 us  [shard(): lax.ppermute(value, 'shard', [(i, i ^ mask) for i in range(self.shards)])]
    ppermute x31 -> x40, starting transfers between devices: 36.1 us -> 36.5 us  [replica(): lax.ppermute(value, 'replica', [(i, i ^ mask) for i in range(self.replica...]
  transfers between devices with their start and end apart: 40 -> 51, of which waited for: 20 -> 16; matrix products, arithmetic and copies ran while one was open for 4% -> 4% of each run, Pallas kernels for 39% -> 53%
where the time goes in v3:
time: 375 us; the launch traced here: 369 us
  Pallas kernels  238 us (63%)
  starting transfers between devices  50.5 us (13%)
  waiting for transfers between devices  49 us (13%)
  local copies, waits for them, and re-layouts  24.2 us (6%)
  other arithmetic  5.64 us (2%)
    pallas_call x2, Pallas kernels, attn_bwd(): pl.pallas_call(lambda *a: bwd_body(*a, group=group), out_shape=(jax.Shape...  41 us
    pallas_call x6, Pallas kernels, row_gradient(): call(functools.partial(row_gradient_body, pieces=pieces, cuts=cuts, adds=...  36.9 us
    ppermute x40, starting transfers between devices, replica(): lax.ppermute(value, 'replica', [(i, i ^ mask) for i in range(self.replica...  36.5 us
    pallas_call x11, Pallas kernels, run_jobs(): call(body, 'exchange_step', outs, (1,), specs, [constant(out.shape) for o...  31.8 us
    ppermute x40, waiting for transfers between devices, replica(): lax.ppermute(value, 'replica', [(i, i ^ mask) for i in range(self.replica...  30.4 us
    pallas_call x1, Pallas kernels, down_block(): call(down_body, 'down_norm_back', (shape((LEN, D)), shape((LEN, D), F32),...  24.2 us
    pallas_call x1, Pallas kernels, up_block(): call(up_body, 'out_norm_up', (shape((LEN, D), F32), shape((LEN, WIDE), F3...  19.5 us
    ppermute x8, waiting for transfers between devices, shard(): lax.ppermute(value, 'shard', [(i, i ^ mask) for i in range(self.shards)])  18.6 us
  transfers between devices with their start and end apart: 51, of which 16 were waited for; matrix products, arithmetic and copies ran while one was open for 4% of the time, Pallas kernels for 53%

profile of v3, /device:TPU:0, one launch (start us, length us, event | category | flops | bytes accessed | tf_op | source)
XLA Modules:
  0.0 368.9 jit_solution(17657578149191731408)
XLA Ops:
  2.0 3.0 collective-permute-start
  12.5 12.4 %collective-permute-done.3 = bf16[4608]{0:T(1024)(128)(2,1)S(1)} collective-permute-done((bf16[4608]{0:T(1024)(128)(2,1)S(1)}, bf16[4608]{0:T(1024)(128)(2,1)S(1)}, u32[]{:S(2)}, u32[]{:S(2)}) %collective-permute-start.3) | collective-permute-done | bytes 9248 | tf_op jit(solution)/shard_map/ppermute | solution.py:630
  25.1 1.8 collective-permute-start.2
  27.5 2.1 collective-permute-done.4.refs_2_.refs_5_.refs_8_
  30.5 9.1 %project.1 = (bf16[1024,2304]{1,0:T(8,128)(2,1)}, bf16[768,2304]{1,0:T(8,128)(2,1)}) custom-call(s32[6]{0:T(128)} %stack.36.place, bf16[1024,768]{1,0:T(8,128)(2,1)} %left.3, f32[1,9216]{1,0:T(1,128)} %bitcast.43, bf16[384,2304]{1,0:T(8,128)(2,1)} %refs_6_.1, bf16[192,2304]{1,0:T(8,128)(2,1)} %collective-permute-done.refs_1_.refs_4_.refs_7_, ...), custom_call_target="tpu_custom_call" | custom-call | flops 3623878656 | bytes 1048576 | tf_op jit(solution)/shard_map/project/pallas_call | solution.py:153
  39.6 17.9 %attention_forward.1 = (bf16[1024,768]{1,0:T(8,128)(2,1)}, f32[6,2,1024]{2,1,0:T(2,128)}) custom-call(s32[16]{0:T(128)} %pad_add_fusion.a_0_, bf16[1024,2304]{1,0:T(8,128)(2,1)} %get-tuple-element.165.a_1_, bf16[1024,128]{1,0:T(8,128)(2,1)} %select_convert_fusion.a_2_.a_5_, bf16[1024,128]{1,0:T(8,128)(2,1)} %fusion.1.a_3_.a_6_), custom_call_target="tpu_custom_call" | custom-call | tf_op jit(solution)/shard_map/attention_forward/pallas_call | solution.py:223
  57.4 1.4 collective-permute-done.1.refs_1_.refs_4_
  59.0 1.5 collective-permute-start.5
  60.7 1.7 collective-permute-done.6.refs_2_.refs_5_
  63.0 19.5 %out_norm_up.1 = (f32[1024,768]{1,0:T(8,128)}, f32[1024,128]{1,0:T(8,128)}, bf16[1024,768]{1,0:T(8,128)(2,1)}, bf16[1024,3072]{1,0:T(8,128)(2,1)}, bf16[1024,3072]{1,0:T(8,128)(2,1)}) custom-call(s32[6]{0:T(128)} %stack.36.place, bf16[1024,768]{1,0:T(8,128)(2,1)} %get-tuple-element.169.context.left.a_2_, bf16[1024,768]{1,0:T(8,128)(2,1)} %left.3, ...), custom_call_target="tpu_custom_call" | custom-call | flops 6039797760 | bytes 1048576 | tf_op jit(solution)/shard_map/out_norm_up/pallas_call | solution.py:361
  82.6 4.8 %collective-permute-done.5.refs_1_ = bf16[768,768]{1,0:T(8,128)(2,1)S(1)} collective-permute-done((bf16[768,768]{1,0:T(8,128)(2,1)S(1)}, bf16[768,768]{1,0:T(8,128)(2,1)S(1)}, u32[]{:S(2)}, u32[]{:S(2)}) %collective-permute-start.5) | collective-permute-done | bytes 1179680 | tf_op jit(solution)/shard_map/ppermute | solution.py:630
  87.4 2.8 collective-permute-done.8.refs_2_
  91.3 24.2 %down_norm_back.1 = (bf16[1024,768]{1,0:T(8,128)(2,1)}, f32[1024,768]{1,0:T(8,128)}, bf16[1024,768]{1,0:T(8,128)(2,1)}, bf16[1024,3072]{1,0:T(8,128)(2,1)}, f32[1,5376]{1,0:T(1,128)}) custom-call(s32[6]{0:T(128)} %stack.36.place, bf16[1024,3072]{1,0:T(8,128)(2,1)} %get-tuple-element.172.activated.left, bf16[1024,3072]{1,0:T(8,128)(2,1)} %get-tuple-element.173.slope, ...), custom_call_target="tpu_custom_call" | custom-call | flops 9663676416 | bytes 1048576 | tf_op jit(solution)/shard_map/down_norm_back/pallas_call | solution.py:421
  115.5 7.6 %down_gradient.2 = bf16[2,1536,384]{2,1,0:T(8,128)(2,1)} custom-call(s32[6]{0:T(128)} %stack.36.place, bf16[1024,3072]{1,0:T(8,128)(2,1)} %get-tuple-element.172.activated.left, bf16[1024,768]{1,0:T(8,128)(2,1)} %get-tuple-element.185.right), custom_call_target="tpu_custom_call" | custom-call | flops 2415919104 | bytes 1048576 | tf_op jit(solution)/shard_map/down_gradient/pallas_call | solution.py:544
  123.2 6.7 %row_gradient.6 = bf16[2,1536,384]{2,1,0:T(8,128)(2,1)} custom-call(s32[6]{0:T(128)} %stack.36.place, bf16[1024,768]{1,0:T(8,128)(2,1)} %get-tuple-element.177.left, bf16[1024,3072]{1,0:T(8,128)(2,1)} %get-tuple-element.181.right.d_up), custom_call_target="tpu_custom_call" | custom-call | flops 2415919104 | bytes 1048576 | tf_op jit(solution)/shard_map/row_gradient/pallas_call | solution.py:600
  130.3 8.5 %down_gradient.3 = (bf16[1536,384]{1,0:T(8,128)(2,1)}, bf16[1536,384]{1,0:T(8,128)(2,1)}) custom-call(s32[6]{0:T(128)} %stack.36.place, bf16[1024,3072]{1,0:T(8,128)(2,1)} %get-tuple-element.172.activated.left, bf16[1024,768]{1,0:T(8,128)(2,1)} %get-tuple-element.185.right, bf16[2,1536,384]{2,1,0:T(8,128)(2,1)} %collective-permute-done.11.refs_0_), custom_call_target="tpu_custom_call" | custom-call | flops 2415919104 | bytes 1048576 | tf_op jit(solution)/shard_map/down_gradient/pallas_call | solution.py:544
  138.8 1.4 collective-permute-start.12
  140.2 1.5 copy-done.7
  141.7 8.0 %row_gradient.7 = (bf16[1920,384]{1,0:T(8,128)(2,1)}, bf16[1920,384]{1,0:T(8,128)(2,1)}) custom-call(s32[6]{0:T(128)} %stack.36.place, bf16[1024,768]{1,0:T(8,128)(2,1)} %get-tuple-element.177.left, bf16[1024,3072]{1,0:T(8,128)(2,1)} %get-tuple-element.181.right.d_up, bf16[2,1536,384]{2,1,0:T(8,128)(2,1)} %copy-done.7), custom_call_target="tpu_custom_call" | custom-call | flops 2415919104 | bytes 1048576 | tf_op jit(solution)/shard_map/row_gradient/pallas_call | solution.py:600
  149.7 17.3 %norm_back.1 = (f32[1024,768]{1,0:T(8,128)}, bf16[1024,768]{1,0:T(8,128)(2,1)}, bf16[1024,768]{1,0:T(8,128)(2,1)}, f32[1,2304]{1,0:T(1,128)}) custom-call(s32[6]{0:T(128)} %stack.36.place, bf16[1024,3072]{1,0:T(8,128)(2,1)} %get-tuple-element.181.right.d_up, f32[1024,768]{1,0:T(8,128)} %get-tuple-element.182.d_sum_two, ...), custom_call_target="tpu_custom_call" | custom-call | flops 6039797760 | bytes 1048576 | tf_op jit(solution)/shard_map/norm_back/pallas_call | solution.py:472
  167.0 4.2 %row_gradient.8 = bf16[2,384,384]{2,1,0:T(8,128)(2,1)} custom-call(s32[6]{0:T(128)} %stack.36.place, bf16[1024,768]{1,0:T(8,128)(2,1)} %get-tuple-element.169.context.left.a_2_, bf16[1024,768]{1,0:T(8,128)(2,1)} %get-tuple-element.184.right), custom_call_target="tpu_custom_call" | custom-call | flops 603979776 | bytes 1048576 | tf_op jit(solution)/shard_map/row_gradient/pallas_call | solution.py:600
  172.2 3.4 exchange_step.11
  176.4 4.5 %row_gradient.9 = (bf16[1920,384]{1,0:T(8,128)(2,1)}, bf16[1920,384]{1,0:T(8,128)(2,1)}) custom-call(s32[6]{0:T(128)} %stack.36.place, bf16[1024,768]{1,0:T(8,128)(2,1)} %get-tuple-element.169.context.left.a_2_, bf16[1024,768]{1,0:T(8,128)(2,1)} %get-tuple-element.184.right, ...), custom_call_target="tpu_custom_call", output_to_operand_aliasing={{0}: (4, {}), {1}: (5, {})} | custom-call | flops 603979776 | bytes 1048576 | tf_op jit(solution)/shard_map/row_gradient/pallas_call | solution.py:600
  182.7 1.5 collective-permute-start.14
  185.3 20.5 %attention_backward.2 = (bf16[1024,1152]{1,0:T(8,128)(2,1)}, f32[2,384]{1,0:T(2,128)}) custom-call(s32[9]{0:T(128)} %get-tuple-element.347.a_0_, bf16[1024,2304]{1,0:T(8,128)(2,1)} %get-tuple-element.165.a_1_, bf16[1024,768]{1,0:T(8,128)(2,1)} %get-tuple-element.169.context.left.a_2_, bf16[1024,768]{1,0:T(8,128)(2,1)} %get-tuple-element.215.a_3_, ...), custom_call_target="tpu_custom_call" | custom-call | tf_op jit(solution)/shard_map/attention_backward/pallas_call | solution.py:297
  206.7 2.9 exchange_step.12
  209.6 6.6 %row_gradient.10 = bf16[4,576,384]{2,1,0:T(8,128)(2,1)} custom-call(s32[6]{0:T(128)} %stack.36.place, bf16[1024,768]{1,0:T(8,128)(2,1)} %left.3, bf16[1024,1152]{1,0:T(8,128)(2,1)} %get-tuple-element.205.right.refs_0_), custom_call_target="tpu_custom_call" | custom-call | flops 1811939328 | bytes 1048576 | tf_op jit(solution)/shard_map/row_gradient/pallas_call | solution.py:600
  216.4 1.7 collective-permute-start.16
  218.1 2.6 collective-permute-start.17
  222.0 3.8 %exchange_step.13 = (bf16[960,384]{1,0:T(8,128)(2,1)}, bf16[960,384]{1,0:T(8,128)(2,1)}) custom-call(s32[6]{0:T(128)} %stack.36.place, bf16[1920,384]{1,0:T(8,128)(2,1)} %get-tuple-element.207.refs_0_.refs_2_.refs_4_.refs_6_, bf16[1920,384]{1,0:T(8,128)(2,1)} %copy-done, bf16[1920,384]{1,0:T(8,128)(2,1)} %get-tuple-element.207.refs_0_.refs_2_.refs_4_.refs_6_, ...), custom_call_target="tpu_custom_call" | custom-call | bytes 1048576 | tf_op jit(solution)/shard_map/exchange_step/pallas_call | solution.py:833
  226.9 20.4 %attention_backward.3 = (bf16[1024,1152]{1,0:T(8,128)(2,1)}, f32[2,384]{1,0:T(2,128)}) custom-call(s32[9]{0:T(128)} %get-tuple-element.346.a_0_, bf16[1024,2304]{1,0:T(8,128)(2,1)} %get-tuple-element.165.a_1_, bf16[1024,768]{1,0:T(8,128)(2,1)} %get-tuple-element.169.context.left.a_2_, bf16[1024,768]{1,0:T(8,128)(2,1)} %get-tuple-element.215.a_3_, ...), custom_call_target="tpu_custom_call" | custom-call | tf_op jit(solution)/shard_map/attention_backward/pallas_call | solution.py:297
  249.1 2.9 exchange_step.14
  252.1 6.9 %row_gradient.11 = (bf16[576,384]{1,0:T(8,128)(2,1)}, bf16[576,384]{1,0:T(8,128)(2,1)}, bf16[576,384]{1,0:T(8,128)(2,1)}, bf16[576,384]{1,0:T(8,128)(2,1)}) custom-call(s32[6]{0:T(128)} %stack.36.place, bf16[1024,768]{1,0:T(8,128)(2,1)} %left.3, bf16[1024,1152]{1,0:T(8,128)(2,1)} %get-tuple-element.249.right.refs_1_, ...), custom_call_target="tpu_custom_call" | custom-call | flops 1811939328 | bytes 1048576 | tf_op jit(solution)/shard_map/row_gradient/pallas_call | solution.py:600
  259.0 1.7 collective-permute-start.23
  260.7 1.6 collective-permute-start.24
  263.9 2.9 exchange_step.15
  266.8 3.7 %collective-permute-start.22 = (bf16[240,384]{1,0:T(8,128)(2,1)}, bf16[240,384]{1,0:T(8,128)(2,1)S(1)}, u32[]{:S(2)}, u32[]{:S(2)}) collective-permute-start(bf16[240,384]{1,0:T(8,128)(2,1)} %get-tuple-element.246), channel_id=1, source_target_pairs={{0,16},{2,18},{4,20},{6,22},{8,24},{10,26},{12,28},{14,30},{16,0},... | collective-permute-start | bytes 552968 | tf_op jit(solution)/shard_map/ppermute | solution.py:641
  270.5 9.7 %input_gradient.1 = bf16[1024,768]{1,0:T(8,128)(2,1)} custom-call(s32[6]{0:T(128)} %stack.36.place, bf16[768,2304]{1,0:T(8,128)(2,1)} %get-tuple-element.247.weight, f32[1024,768]{1,0:T(8,128)} %get-tuple-element.248.d_sum, bf16[1024,1152]{1,0:T(8,128)(2,1)} %get-tuple-element.205.right.refs_0_, bf16[1024,1152]{1,0:T(8,128)(2,1)} %get-tuple-element.249.right.refs_1_), custom_call_target="tpu_custom_call" | custom-call | flops 3623878656 | bytes 1048576 | tf_op jit(solution)/shard_map/input_gradient/pallas_call | solution.py:501
  280.2 3.7 %collective-permute-done.21.refs_1_ = bf16[192,384]{1,0:T(8,128)(2,1)S(1)} collective-permute-done((bf16[192,384]{1,0:T(8,128)(2,1)}, bf16[192,384]{1,0:T(8,128)(2,1)S(1)}, u32[]{:S(2)}, u32[]{:S(2)}) %collective-permute-start.21) | collective-permute-done | bytes 147488 | tf_op jit(solution)/shard_map/ppermute | solution.py:641
  284.6 2.4 exchange_step.16.refs_0_
  287.1 2.4 collective-permute-start.31
  290.1 1.7 collective-permute-start.32
  291.8 3.0 exchange_step.17
  294.8 1.4 collective-permute-start.26
  296.9 2.4 collective-permute-start.28
  299.9 2.7 exchange_step.18
  302.6 4.0 %collective-permute-done.27.refs_2_ = bf16[144,384]{1,0:T(8,128)(2,1)S(1)} collective-permute-done((bf16[144,384]{1,0:T(8,128)(2,1)}, bf16[144,384]{1,0:T(8,128)(2,1)S(1)}, u32[]{:S(2)}, u32[]{:S(2)}) %collective-permute-start.27) | collective-permute-done | bytes 110624 | tf_op jit(solution)/shard_map/ppermute | solution.py:641
  306.6 1.5 collective-permute-start.42
  308.2 1.7 collective-permute-start.37
  310.2 2.4 exchange_step.19
  313.2 1.7 collective-permute-start.34
  314.9 5.1 %collective-permute-done.39.refs_5_ = f32[36,128]{1,0:T(8,128)S(1)} collective-permute-done((f32[36,128]{1,0:T(8,128)}, f32[36,128]{1,0:T(8,128)S(1)}, u32[]{:S(2)}, u32[]{:S(2)}) %collective-permute-start.39) | collective-permute-done | bytes 18464 | tf_op jit(solution)/shard_map/ppermute | solution.py:641
  320.0 3.2 collective-permute-start.35
  323.2 1.6 collective-permute-start.36
  325.5 2.8 exchange_step.20
  328.3 1.9 collective-permute-done.35.refs_2_
  331.6 1.7 collective-permute-start.43
  333.3 2.5 exchange_step.21.refs_0_
  337.2 1.5 collective-permute-start.46
  338.7 3.4 collective-permute-done.46
  342.9 4.9 %finish_down.1 = f32[1536,768]{1,0:T(8,128)} custom-call(s32[6]{0:T(128)} %stack.36.place, bf16[768,384]{1,0:T(8,128)(2,1)} %get-tuple-element.299.refs_0_, bf16[768,384]{1,0:T(8,128)(2,1)} %copy-done.16, bf16[768,384]{1,0:T(8,128)(2,1)} %copy-done.17, bf16[768,384]{1,0:T(8,128)(2,1)} %collective-permute-done.45.refs_3_), custom_call_target="tpu_custom_call" | custom-call | bytes 1048576 | tf_op jit(solution)/shard_map/finish_down/pallas_call | solution.py:899
  352.1 5.4 %finish_up.1 = (f32[384,3072]{1,0:T(8,128)}, f32[384,768]{1,0:T(8,128)}) custom-call(s32[6]{0:T(128)} %stack.36.place, bf16[960,384]{1,0:T(8,128)(2,1)} %get-tuple-element.303.refs_0_, bf16[960,384]{1,0:T(8,128)(2,1)} %copy-done.12, bf16[960,384]{1,0:T(8,128)(2,1)} %copy-done.13, bf16[960,384]{1,0:T(8,128)(2,1)} %copy-done.14), custom_call_target="tpu_custom_call" | custom-call | bytes 1048576 | tf_op jit(solution)/shard_map/finish_up/pallas_call | solution.py:914
  357.5 3.2 collective-permute-done.40.refs_1_
  364.6 4.1 %finish_attention.1 = f32[384,2304]{1,0:T(8,128)} custom-call(s32[6]{0:T(128)} %stack.36.place, bf16[576,384]{1,0:T(8,128)(2,1)} %exchange_step.21.refs_0_, bf16[576,384]{1,0:T(8,128)(2,1)} %collective-permute-done.40.refs_1_, bf16[576,384]{1,0:T(8,128)(2,1)} %copy-done.20, bf16[576,384]{1,0:T(8,128)(2,1)} %copy-done.21), custom_call_target="tpu_custom_call" | custom-call | bytes 1048576 | tf_op jit(solution)/shard_map/finish_attention/pallas_call | solution.py:945
  (280 shorter events, 40.1 us)
Async XLA Ops:
  2.0 8.4 %copy-start.30 = (bf16[384,768]{1,0:T(8,128)(2,1)S(1)}, bf16[384,768]{1,0:T(8,128)(2,1)}, u32[]{:S(2)}) copy-start(bf16[384,768]{1,0:T(8,128)(2,1)} %refs_3_.5) | copy-start | bytes 1769476
  2.0 23.1 %collective-permute-start = (bf16[192,2304]{1,0:T(8,128)(2,1)S(1)}, bf16[192,2304]{1,0:T(8,128)(2,1)}, u32[]{:S(2)}, u32[]{:S(2)}) collective-permute-start(bf16[192,2304]{1,0:T(8,128)(2,1)S(1)} %constant_dynamic-slice_fusion), channel_id=1, source_target_pairs={{0,1},{1,0},{2,3},{3,2},{4,5},{5,4},{6,7},{7,6},{8,9},{9,8},{10,11... | collective-permute-start | bytes 2654216 | tf_op jit(solution)/shard_map/ppermute | solution.py:630
  6.8 18.1 %collective-permute-start.3 = (bf16[4608]{0:T(1024)(128)(2,1)S(1)}, bf16[4608]{0:T(1024)(128)(2,1)S(1)}, u32[]{:S(2)}, u32[]{:S(2)}) collective-permute-start(bf16[4608]{0:T(1024)(128)(2,1)S(1)} %dynamic-update-slice.24), channel_id=1, source_target_pairs={{0,1},{1,0},{2,3},{3,2},{4,5},{5,4},{6,7},{7,6},{8,9},{9,8},{10,11... | collective-permute-start | bytes 27656 | tf_op jit(solution)/shard_map/ppermute | solution.py:630
  25.1 33.8 %collective-permute-start.2 = (bf16[192,3072]{1,0:T(8,128)(2,1)S(1)}, bf16[192,3072]{1,0:T(8,128)(2,1)}, u32[]{:S(2)}, u32[]{:S(2)}) collective-permute-start(bf16[192,3072]{1,0:T(8,128)(2,1)S(1)} %constant_dynamic-slice_fusion.1), channel_id=1, source_target_pairs={{0,1},{1,0},{2,3},{3,2},{4,5},{5,4},{6,7},{7,6},{8,9},{9,8},{10,11... | collective-permute-start | bytes 3538952 | tf_op jit(solution)/shard_map/ppermute | solution.py:630
  26.9 2.6 collective-permute-start.4
  27.1 31.7 %collective-permute-start.1 = (bf16[192,768]{1,0:T(8,128)(2,1)}, bf16[192,768]{1,0:T(8,128)(2,1)}, u32[]{:S(2)}, u32[]{:S(2)}) collective-permute-start(bf16[192,768]{1,0:T(8,128)(2,1)} %constant_dynamic-slice_fusion.2), channel_id=1, source_target_pairs={{0,1},{1,0},{2,3},{3,2},{4,5},{5,4},{6,7},{7,6},{8,9},{9,8},{10,11... | collective-permute-start | bytes 884744 | tf_op jit(solution)/shard_map/ppermute | solution.py:630
  39.5 19.3 %copy-start.18 = (bf16[1536,768]{1,0:T(8,128)(2,1)S(1)}, bf16[1536,768]{1,0:T(8,128)(2,1)}, u32[]{:S(2)}) copy-start(bf16[1536,768]{1,0:T(8,128)(2,1)} %refs_0_.6) | copy-start | bytes 7077892
  58.9 3.5 collective-permute-start.7
  59.0 28.4 %collective-permute-start.5 = (bf16[768,768]{1,0:T(8,128)(2,1)S(1)}, bf16[768,768]{1,0:T(8,128)(2,1)S(1)}, u32[]{:S(2)}, u32[]{:S(2)}) collective-permute-start(bf16[768,768]{1,0:T(8,128)(2,1)S(1)} %constant_dynamic-slice_fusion.3), channel_id=1, source_target_pairs={{0,1},{1,0},{2,3},{3,2},{4,5},{5,4},{6,7},{7,6},{8,9},{9,8},{10,11... | collective-permute-start | bytes 3538952 | tf_op jit(solution)/shard_map/ppermute | solution.py:630
  60.4 1.9 collective-permute-start.6
  87.4 2.8 collective-permute-start.8
  123.0 7.2 %collective-permute-start.11 = (bf16[2,1536,384]{2,1,0:T(8,128)(2,1)}, bf16[2,1536,384]{2,1,0:T(8,128)(2,1)}, u32[]{:S(2)}, u32[]{:S(2)}) collective-permute-start(bf16[2,1536,384]{2,1,0:T(8,128)(2,1)} %down_gradient.2), channel_id=1, source_target_pairs={{0,2},{2,0},{4,6},{6,4},{8,10},{10,8},{12,14},{14,12},{16,18},{18,... | collective-permute-start | bytes 7077896 | tf_op jit(solution)/shard_map/ppermute | solution.py:641
  129.9 10.3 %collective-permute-start.9 = (bf16[2,1536,384]{2,1,0:T(8,128)(2,1)}, bf16[2,1536,384]{2,1,0:T(8,128)(2,1)S(1)}, u32[]{:S(2)}, u32[]{:S(2)}) collective-permute-start(bf16[2,1536,384]{2,1,0:T(8,128)(2,1)} %row_gradient.6), channel_id=1, source_target_pairs={{0,2},{2,0},{4,6},{6,4},{8,10},{10,8},{12,14},{14,12},{16,18},{18,... | collective-permute-start | bytes 7077896 | tf_op jit(solution)/shard_map/ppermute | solution.py:641
  138.8 32.4 %collective-permute-start.12 = (bf16[1536,384]{1,0:T(8,128)(2,1)}, bf16[1536,384]{1,0:T(8,128)(2,1)S(1)}, u32[]{:S(2)}, u32[]{:S(2)}) collective-permute-start(bf16[1536,384]{1,0:T(8,128)(2,1)} %get-tuple-element.187), channel_id=1, source_target_pairs={{0,1},{1,0},{2,3},{3,2},{4,5},{5,4},{6,7},{7,6},{8,9},{9,8},{10,11... | collective-permute-start | bytes 3538952 | tf_op jit(solution)/shard_map/ppermute | solution.py:630
  171.2 4.4 %collective-permute-start.10 = (bf16[2,384,384]{2,1,0:T(8,128)(2,1)}, bf16[2,384,384]{2,1,0:T(8,128)(2,1)S(1)}, u32[]{:S(2)}, u32[]{:S(2)}) collective-permute-start(bf16[2,384,384]{2,1,0:T(8,128)(2,1)} %row_gradient.8), channel_id=1, source_target_pairs={{0,2},{2,0},{4,6},{6,4},{8,10},{10,8},{12,14},{14,12},{16,18},{18,... | collective-permute-start | bytes 1769480 | tf_op jit(solution)/shard_map/ppermute | solution.py:641
  180.9 39.9 %collective-permute-start.13 = (bf16[1920,384]{1,0:T(8,128)(2,1)}, bf16[1920,384]{1,0:T(8,128)(2,1)S(1)}, u32[]{:S(2)}, u32[]{:S(2)}) collective-permute-start(bf16[1920,384]{1,0:T(8,128)(2,1)} %get-tuple-element.195), channel_id=1, source_target_pairs={{0,1},{1,0},{2,3},{3,2},{4,5},{5,4},{6,7},{7,6},{8,9},{9,8},{10,11... | collective-permute-start | bytes 4423688 | tf_op jit(solution)/shard_map/ppermute | solution.py:630
  182.7 23.1 %collective-permute-start.14 = (bf16[768,384]{1,0:T(8,128)(2,1)S(1)}, bf16[768,384]{1,0:T(8,128)(2,1)S(1)}, u32[]{:S(2)}, u32[]{:S(2)}) collective-permute-start(bf16[768,384]{1,0:T(8,128)(2,1)S(1)} %copy-done.58), channel_id=1, source_target_pairs={{0,4},{2,6},{4,0},{6,2},{8,12},{10,14},{12,8},{14,10},{16,20},{18,... | collective-permute-start | bytes 1769480 | tf_op jit(solution)/shard_map/ppermute | solution.py:641
  209.6 8.5 %copy-start.61 = (bf16[192,384]{1,0:T(8,128)(2,1)S(1)}, bf16[192,384]{1,0:T(8,128)(2,1)}, u32[]{:S(2)}) copy-start(bf16[192,384]{1,0:T(8,128)(2,1)} %get-tuple-element.212) | copy-start | bytes 442372
  209.6 11.2 %copy-start.60 = (bf16[192,384]{1,0:T(8,128)(2,1)S(1)}, bf16[192,384]{1,0:T(8,128)(2,1)}, u32[]{:S(2)}) copy-start(bf16[192,384]{1,0:T(8,128)(2,1)} %get-tuple-element.213) | copy-start | bytes 442372
  216.2 32.0 %collective-permute-start.19 = (bf16[4,576,384]{2,1,0:T(8,128)(2,1)}, bf16[4,576,384]{2,1,0:T(8,128)(2,1)}, u32[]{:S(2)}, u32[]{:S(2)}) collective-permute-start(bf16[4,576,384]{2,1,0:T(8,128)(2,1)} %row_gradient.10), channel_id=1, source_target_pairs={{0,2},{2,0},{4,6},{6,4},{8,10},{10,8},{12,14},{14,12},{16,18},{18,... | collective-permute-start | bytes 5308424 | tf_op jit(solution)/shard_map/ppermute | solution.py:641
  216.4 31.7 %collective-permute-start.16 = (bf16[192,384]{1,0:T(8,128)(2,1)S(1)}, bf16[192,384]{1,0:T(8,128)(2,1)S(1)}, u32[]{:S(2)}, u32[]{:S(2)}) collective-permute-start(bf16[192,384]{1,0:T(8,128)(2,1)S(1)} %copy-done.62), channel_id=1, source_target_pairs={{0,8},{2,10},{4,12},{6,14},{8,0},{10,2},{12,4},{14,6},{16,24},{18,... | collective-permute-start | bytes 442376 | tf_op jit(solution)/shard_map/ppermute | solution.py:641
  218.1 30.0 %collective-permute-start.17 = (bf16[192,384]{1,0:T(8,128)(2,1)S(1)}, bf16[192,384]{1,0:T(8,128)(2,1)S(1)}, u32[]{:S(2)}, u32[]{:S(2)}) collective-permute-start(bf16[192,384]{1,0:T(8,128)(2,1)S(1)} %copy-done.61), channel_id=1, source_target_pairs={{0,16},{2,18},{4,20},{6,22},{8,24},{10,26},{12,28},{14,30},{16,0},... | collective-permute-start | bytes 442376 | tf_op jit(solution)/shard_map/ppermute | solution.py:641
  220.7 27.4 %collective-permute-start.18 = (bf16[192,384]{1,0:T(8,128)(2,1)S(1)}, bf16[192,384]{1,0:T(8,128)(2,1)S(1)}, u32[]{:S(2)}, u32[]{:S(2)}) collective-permute-start(bf16[192,384]{1,0:T(8,128)(2,1)S(1)} %copy-done.60), channel_id=1, source_target_pairs={{0,24},{2,26},{4,28},{6,30},{8,16},{10,18},{12,20},{14,22},{16,8},... | collective-permute-start | bytes 442376 | tf_op jit(solution)/shard_map/ppermute | solution.py:641
  225.8 22.4 %collective-permute-start.15 = (bf16[960,384]{1,0:T(8,128)(2,1)}, bf16[960,384]{1,0:T(8,128)(2,1)S(1)}, u32[]{:S(2)}, u32[]{:S(2)}) collective-permute-start(bf16[960,384]{1,0:T(8,128)(2,1)} %get-tuple-element.210), channel_id=1, source_target_pairs={{0,4},{2,6},{4,0},{6,2},{8,12},{10,14},{12,8},{14,10},{16,20},{18,... | collective-permute-start | bytes 2211848 | tf_op jit(solution)/shard_map/ppermute | solution.py:641
  226.9 20.4 %copy-start.45 = (f32[2,384]{1,0:T(2,128)S(1)}, f32[2,384]{1,0:T(2,128)}, u32[]{:S(2)}) copy-start(f32[2,384]{1,0:T(2,128)} %get-tuple-element.227) | copy-start | bytes 9220
  248.1 10.9 %copy-start.27 = (bf16[192,384]{1,0:T(8,128)(2,1)}, bf16[192,384]{1,0:T(8,128)(2,1)S(1)}, u32[]{:S(2)}) copy-start(bf16[192,384]{1,0:T(8,128)(2,1)S(1)} %collective-permute-done.16.refs_1_) | copy-start | bytes 442372
  248.1 10.9 %copy-start.28 = (bf16[192,384]{1,0:T(8,128)(2,1)}, bf16[192,384]{1,0:T(8,128)(2,1)S(1)}, u32[]{:S(2)}) copy-start(bf16[192,384]{1,0:T(8,128)(2,1)S(1)} %collective-permute-done.17.refs_2_) | copy-start | bytes 442372
  248.1 10.8 %copy-start.29 = (bf16[192,384]{1,0:T(8,128)(2,1)}, bf16[192,384]{1,0:T(8,128)(2,1)S(1)}, u32[]{:S(2)}) copy-start(bf16[192,384]{1,0:T(8,128)(2,1)S(1)} %collective-permute-done.18.refs_3_) | copy-start | bytes 442372
  252.0 11.1 %collective-permute-start.20 = (bf16[480,384]{1,0:T(8,128)(2,1)}, bf16[480,384]{1,0:T(8,128)(2,1)S(1)}, u32[]{:S(2)}, u32[]{:S(2)}) collective-permute-start(bf16[480,384]{1,0:T(8,128)(2,1)} %get-tuple-element.224), channel_id=1, source_target_pairs={{0,8},{2,10},{4,12},{6,14},{8,0},{10,2},{12,4},{14,6},{16,24},{18,... | collective-permute-start | bytes 1105928 | tf_op jit(solution)/shard_map/ppermute | solution.py:641
  259.0 28.1 %collective-permute-start.23 = (bf16[576,384]{1,0:T(8,128)(2,1)}, bf16[576,384]{1,0:T(8,128)(2,1)S(1)}, u32[]{:S(2)}, u32[]{:S(2)}) collective-permute-start(bf16[576,384]{1,0:T(8,128)(2,1)} %get-tuple-element.233), channel_id=1, source_target_pairs={{0,4},{1,5},{2,6},{3,7},{4,0},{5,1},{6,2},{7,3},{8,12},{9,13},{10,... | collective-permute-start | bytes 1327112 | tf_op jit(solution)/shard_map/ppermute | solution.py:638
  260.7 26.3 %collective-permute-start.24 = (bf16[576,384]{1,0:T(8,128)(2,1)}, bf16[576,384]{1,0:T(8,128)(2,1)S(1)}, u32[]{:S(2)}, u32[]{:S(2)}) collective-permute-start(bf16[576,384]{1,0:T(8,128)(2,1)} %get-tuple-element.234), channel_id=1, source_target_pairs={{0,1},{1,0},{2,3},{3,2},{4,5},{5,4},{6,7},{7,6},{8,9},{9,8},{10,11... | collective-permute-start | bytes 1327112 | tf_op jit(solution)/shard_map/ppermute | solution.py:638
  262.3 24.8 %collective-permute-start.25 = (bf16[576,384]{1,0:T(8,128)(2,1)}, bf16[576,384]{1,0:T(8,128)(2,1)S(1)}, u32[]{:S(2)}, u32[]{:S(2)}) collective-permute-start(bf16[576,384]{1,0:T(8,128)(2,1)} %get-tuple-element.235), channel_id=1, source_target_pairs={{0,5},{1,4},{2,7},{3,6},{4,1},{5,0},{6,3},{7,2},{8,13},{9,12},{10,... | collective-permute-start | bytes 1327112 | tf_op jit(solution)/shard_map/ppermute | solution.py:638
  266.8 17.2 %collective-permute-start.22 = (bf16[240,384]{1,0:T(8,128)(2,1)}, bf16[240,384]{1,0:T(8,128)(2,1)S(1)}, u32[]{:S(2)}, u32[]{:S(2)}) collective-permute-start(bf16[240,384]{1,0:T(8,128)(2,1)} %get-tuple-element.246), channel_id=1, source_target_pairs={{0,16},{2,18},{4,20},{6,22},{8,24},{10,26},{12,28},{14,30},{16,0},... | collective-permute-start | bytes 552968 | tf_op jit(solution)/shard_map/ppermute | solution.py:641
  270.5 13.4 %collective-permute-start.21 = (bf16[192,384]{1,0:T(8,128)(2,1)}, bf16[192,384]{1,0:T(8,128)(2,1)S(1)}, u32[]{:S(2)}, u32[]{:S(2)}) collective-permute-start(bf16[192,384]{1,0:T(8,128)(2,1)} %get-tuple-element.266.refs_0_), channel_id=1, source_target_pairs={{0,16},{2,18},{4,20},{6,22},{8,24},{10,26},{12,28},{14,30},{16,0},... | collective-permute-start | bytes 442376 | tf_op jit(solution)/shard_map/ppermute | solution.py:641
  270.5 13.4 %copy-start.31 = (bf16[192,384]{1,0:T(8,128)(2,1)S(1)}, bf16[192,384]{1,0:T(8,128)(2,1)}, u32[]{:S(2)}) copy-start(bf16[192,384]{1,0:T(8,128)(2,1)} %get-tuple-element.266.refs_0_) | copy-start | bytes 442372
  283.9 15.3 %copy-start.32 = (bf16[192,384]{1,0:T(8,128)(2,1)}, bf16[192,384]{1,0:T(8,128)(2,1)S(1)}, u32[]{:S(2)}) copy-start(bf16[192,384]{1,0:T(8,128)(2,1)S(1)} %collective-permute-done.21.refs_1_) | copy-start | bytes 442372
  283.9 12.9 %collective-permute-start.29 = (bf16[192,384]{1,0:T(8,128)(2,1)S(1)}, bf16[192,384]{1,0:T(8,128)(2,1)S(1)}, u32[]{:S(2)}, u32[]{:S(2)}) collective-permute-start(bf16[192,384]{1,0:T(8,128)(2,1)S(1)} %copy-done.31), channel_id=1, source_target_pairs={{0,8},{2,10},{4,12},{6,14},{8,0},{10,2},{12,4},{14,6},{16,24},{18,... | collective-permute-start | bytes 442376 | tf_op jit(solution)/shard_map/ppermute | solution.py:641
  287.0 21.1 %copy-start.10 = (bf16[240,384]{1,0:T(8,128)(2,1)S(1)}, bf16[240,384]{1,0:T(8,128)(2,1)}, u32[]{:S(2)}) copy-start(bf16[240,384]{1,0:T(8,128)(2,1)} %exchange_step.16.refs_0_) | copy-start | bytes 552964
  287.1 12.2 %collective-permute-start.31 = (bf16[240,384]{1,0:T(8,128)(2,1)}, bf16[240,384]{1,0:T(8,128)(2,1)S(1)}, u32[]{:S(2)}, u32[]{:S(2)}) collective-permute-start(bf16[240,384]{1,0:T(8,128)(2,1)} %exchange_step.16.refs_0_), channel_id=1, source_target_pairs={{0,16},{2,18},{4,20},{6,22},{8,24},{10,26},{12,28},{14,30},{16,0},... | collective-permute-start | bytes 552968 | tf_op jit(solution)/shard_map/ppermute | solution.py:641
  289.5 9.8 %collective-permute-start.30 = (bf16[192,384]{1,0:T(8,128)(2,1)S(1)}, bf16[192,384]{1,0:T(8,128)(2,1)S(1)}, u32[]{:S(2)}, u32[]{:S(2)}) collective-permute-start(bf16[192,384]{1,0:T(8,128)(2,1)S(1)} %collective-permute-done.21.refs_1_), channel_id=1, source_target_pairs={{0,8},{2,10},{4,12},{6,14},{8,0},{10,2},{12,4},{14,6},{16,24},{18,... | collective-permute-start | bytes 442376 | tf_op jit(solution)/shard_map/ppermute | solution.py:641
  290.1 6.2 %collective-permute-start.32 = (f32[36,128]{1,0:T(8,128)S(1)}, f32[36,128]{1,0:T(8,128)S(1)}, u32[]{:S(2)}, u32[]{:S(2)}) collective-permute-start(f32[36,128]{1,0:T(8,128)S(1)} %get-tuple-element.265), channel_id=1, source_target_pairs={{0,1},{1,0},{2,3},{3,2},{4,5},{5,4},{6,7},{7,6},{8,9},{9,8},{10,11... | collective-permute-start | bytes 55304 | tf_op jit(solution)/shard_map/ppermute | solution.py:630
  294.8 7.7 %collective-permute-start.26 = (bf16[144,384]{1,0:T(8,128)(2,1)}, bf16[144,384]{1,0:T(8,128)(2,1)S(1)}, u32[]{:S(2)}, u32[]{:S(2)}) collective-permute-start(bf16[144,384]{1,0:T(8,128)(2,1)} %get-tuple-element.258), channel_id=1, source_target_pairs={{0,8},{2,10},{4,12},{6,14},{8,0},{10,2},{12,4},{14,6},{16,24},{18,... | collective-permute-start | bytes 331784 | tf_op jit(solution)/shard_map/ppermute | solution.py:641
  296.2 10.3 %collective-permute-start.27 = (bf16[144,384]{1,0:T(8,128)(2,1)}, bf16[144,384]{1,0:T(8,128)(2,1)S(1)}, u32[]{:S(2)}, u32[]{:S(2)}) collective-permute-start(bf16[144,384]{1,0:T(8,128)(2,1)} %get-tuple-element.259), channel_id=1, source_target_pairs={{0,16},{2,18},{4,20},{6,22},{8,24},{10,26},{12,28},{14,30},{16,0},... | collective-permute-start | bytes 331784 | tf_op jit(solution)/shard_map/ppermute | solution.py:641
  296.9 9.7 %collective-permute-start.28 = (bf16[144,384]{1,0:T(8,128)(2,1)}, bf16[144,384]{1,0:T(8,128)(2,1)S(1)}, u32[]{:S(2)}, u32[]{:S(2)}) collective-permute-start(bf16[144,384]{1,0:T(8,128)(2,1)} %get-tuple-element.260), channel_id=1, source_target_pairs={{0,24},{2,26},{4,28},{6,30},{8,16},{10,18},{12,20},{14,22},{16,8},... | collective-permute-start | bytes 331784 | tf_op jit(solution)/shard_map/ppermute | solution.py:641
  299.2 25.5 %copy-start.24 = (bf16[240,384]{1,0:T(8,128)(2,1)}, bf16[240,384]{1,0:T(8,128)(2,1)S(1)}, u32[]{:S(2)}) copy-start(bf16[240,384]{1,0:T(8,128)(2,1)S(1)} %collective-permute-done.31.refs_1_) | copy-start | bytes 552964
  302.6 33.3 %copy-start.15 = (bf16[768,384]{1,0:T(8,128)(2,1)S(1)}, bf16[768,384]{1,0:T(8,128)(2,1)}, u32[]{:S(2)}) copy-start(bf16[768,384]{1,0:T(8,128)(2,1)} %get-tuple-element.299.refs_0_) | copy-start | bytes 1769476
  302.6 4.0 %collective-permute-start.33 = (f32[36,128]{1,0:T(8,128)}, f32[36,128]{1,0:T(8,128)S(1)}, u32[]{:S(2)}, u32[]{:S(2)}) collective-permute-start(f32[36,128]{1,0:T(8,128)} %get-tuple-element.278.refs_4_), channel_id=1, source_target_pairs={{0,2},{2,0},{4,6},{6,4},{8,10},{10,8},{12,14},{14,12},{16,18},{18,... | collective-permute-start | bytes 55304 | tf_op jit(solution)/shard_map/ppermute | solution.py:641
  306.6 29.2 %collective-permute-start.42 = (bf16[768,384]{1,0:T(8,128)(2,1)}, bf16[768,384]{1,0:T(8,128)(2,1)S(1)}, u32[]{:S(2)}, u32[]{:S(2)}) collective-permute-start(bf16[768,384]{1,0:T(8,128)(2,1)} %get-tuple-element.299.refs_0_), channel_id=1, source_target_pairs={{0,4},{2,6},{4,0},{6,2},{8,12},{10,14},{12,8},{14,10},{16,20},{18,... | collective-permute-start | bytes 1769480 | tf_op jit(solution)/shard_map/ppermute | solution.py:641
  308.2 15.0 %collective-permute-start.37 = (bf16[240,384]{1,0:T(8,128)(2,1)S(1)}, bf16[240,384]{1,0:T(8,128)(2,1)S(1)}, u32[]{:S(2)}, u32[]{:S(2)}) collective-permute-start(bf16[240,384]{1,0:T(8,128)(2,1)S(1)} %copy-done.10), channel_id=1, source_target_pairs={{0,8},{2,10},{4,12},{6,14},{8,0},{10,2},{12,4},{14,6},{16,24},{18,... | collective-permute-start | bytes 552968 | tf_op jit(solution)/shard_map/ppermute | solution.py:641
  309.9 14.9 %collective-permute-start.38 = (bf16[240,384]{1,0:T(8,128)(2,1)S(1)}, bf16[240,384]{1,0:T(8,128)(2,1)S(1)}, u32[]{:S(2)}, u32[]{:S(2)}) collective-permute-start(bf16[240,384]{1,0:T(8,128)(2,1)S(1)} %collective-permute-done.31.refs_1_), channel_id=1, source_target_pairs={{0,8},{2,10},{4,12},{6,14},{8,0},{10,2},{12,4},{14,6},{16,24},{18,... | collective-permute-start | bytes 552968 | tf_op jit(solution)/shard_map/ppermute | solution.py:641
  312.6 7.4 %collective-permute-start.39 = (f32[36,128]{1,0:T(8,128)}, f32[36,128]{1,0:T(8,128)S(1)}, u32[]{:S(2)}, u32[]{:S(2)}) collective-permute-start(f32[36,128]{1,0:T(8,128)} %get-tuple-element.288.refs_4_), channel_id=1, source_target_pairs={{0,4},{2,6},{4,0},{6,2},{8,12},{10,14},{12,8},{14,10},{16,20},{18,... | collective-permute-start | bytes 55304 | tf_op jit(solution)/shard_map/ppermute | solution.py:641
  313.2 15.1 %collective-permute-start.34 = (bf16[144,384]{1,0:T(8,128)(2,1)}, bf16[144,384]{1,0:T(8,128)(2,1)S(1)}, u32[]{:S(2)}, u32[]{:S(2)}) collective-permute-start(bf16[144,384]{1,0:T(8,128)(2,1)} %get-tuple-element.292.refs_0_), channel_id=1, source_target_pairs={{0,8},{2,10},{4,12},{6,14},{8,0},{10,2},{12,4},{14,6},{16,24},{18,... | collective-permute-start | bytes 331784 | tf_op jit(solution)/shard_map/ppermute | solution.py:641
  320.0 10.2 %collective-permute-start.35 = (bf16[144,384]{1,0:T(8,128)(2,1)}, bf16[144,384]{1,0:T(8,128)(2,1)S(1)}, u32[]{:S(2)}, u32[]{:S(2)}) collective-permute-start(bf16[144,384]{1,0:T(8,128)(2,1)} %get-tuple-element.292.refs_0_), channel_id=1, source_target_pairs={{0,16},{2,18},{4,20},{6,22},{8,24},{10,26},{12,28},{14,30},{16,0},... | collective-permute-start | bytes 331784 | tf_op jit(solution)/shard_map/ppermute | solution.py:641
  323.2 7.0 %collective-permute-start.36 = (bf16[144,384]{1,0:T(8,128)(2,1)}, bf16[144,384]{1,0:T(8,128)(2,1)S(1)}, u32[]{:S(2)}, u32[]{:S(2)}) collective-permute-start(bf16[144,384]{1,0:T(8,128)(2,1)} %get-tuple-element.292.refs_0_), channel_id=1, source_target_pairs={{0,24},{2,26},{4,28},{6,30},{8,16},{10,18},{12,20},{14,22},{16,8},... | collective-permute-start | bytes 331784 | tf_op jit(solution)/shard_map/ppermute | solution.py:641
  330.2 17.6 %collective-permute-start.41 = (bf16[960,384]{1,0:T(8,128)(2,1)}, bf16[960,384]{1,0:T(8,128)(2,1)S(1)}, u32[]{:S(2)}, u32[]{:S(2)}) collective-permute-start(bf16[960,384]{1,0:T(8,128)(2,1)} %get-tuple-element.303.refs_0_), channel_id=1, source_target_pairs={{0,4},{2,6},{4,0},{6,2},{8,12},{10,14},{12,8},{14,10},{16,20},{18,... | collective-permute-start | bytes 2211848 | tf_op jit(solution)/shard_map/ppermute | solution.py:641
  331.6 4.2 %collective-permute-start.43 = (f32[36,128]{1,0:T(8,128)}, f32[36,128]{1,0:T(8,128)S(1)}, u32[]{:S(2)}, u32[]{:S(2)}) collective-permute-start(f32[36,128]{1,0:T(8,128)} %get-tuple-element.301), channel_id=1, source_target_pairs={{0,8},{2,10},{4,12},{6,14},{8,0},{10,2},{12,4},{14,6},{16,24},{18,... | collective-permute-start | bytes 55304 | tf_op jit(solution)/shard_map/ppermute | solution.py:641
  335.9 6.2 %collective-permute-start.44 = (bf16[768,384]{1,0:T(8,128)(2,1)S(1)}, bf16[768,384]{1,0:T(8,128)(2,1)S(1)}, u32[]{:S(2)}, u32[]{:S(2)}) collective-permute-start(bf16[768,384]{1,0:T(8,128)(2,1)S(1)} %copy-done.15), channel_id=1, source_target_pairs={{0,2},{2,0},{4,6},{6,4},{8,10},{10,8},{12,14},{14,12},{16,18},{18,... | collective-permute-start | bytes 1769480 | tf_op jit(solution)/shard_map/ppermute | solution.py:641
  335.9 7.0 %collective-permute-start.45 = (bf16[768,384]{1,0:T(8,128)(2,1)S(1)}, bf16[768,384]{1,0:T(8,128)(2,1)}, u32[]{:S(2)}, u32[]{:S(2)}) collective-permute-start(bf16[768,384]{1,0:T(8,128)(2,1)S(1)} %collective-permute-done.42.refs_1_), channel_id=1, source_target_pairs={{0,2},{2,0},{4,6},{6,4},{8,10},{10,8},{12,14},{14,12},{16,18},{18,... | collective-permute-start | bytes 1769480 | tf_op jit(solution)/shard_map/ppermute | solution.py:641
  337.2 4.9 %collective-permute-start.46 = (f32[36,128]{1,0:T(8,128)S(1)}, f32[36,128]{1,0:T(8,128)S(1)}, u32[]{:S(2)}, u32[]{:S(2)}) collective-permute-start(f32[36,128]{1,0:T(8,128)S(1)} %add.68), channel_id=1, source_target_pairs={{0,16},{2,18},{4,20},{6,22},{8,24},{10,26},{12,28},{14,30},{16,0},... | collective-permute-start | bytes 55304 | tf_op jit(solution)/shard_map/ppermute | solution.py:641
  347.8 2.3 collective-permute-start.47
  347.9 3.3 collective-permute-start.48
  348.4 12.3 %collective-permute-start.40 = (bf16[576,384]{1,0:T(8,128)(2,1)S(1)}, bf16[576,384]{1,0:T(8,128)(2,1)}, u32[]{:S(2)}, u32[]{:S(2)}) collective-permute-start(bf16[576,384]{1,0:T(8,128)(2,1)S(1)} %copy-done.8), channel_id=1, source_target_pairs={{0,4},{2,6},{4,0},{6,2},{8,12},{10,14},{12,8},{14,10},{16,20},{18,... | collective-permute-start | bytes 1327112 | tf_op jit(solution)/shard_map/ppermute | solution.py:641
  360.7 2.4 collective-permute-start.49
  360.7 2.6 collective-permute-start.50
  (51 other events, 173.2 us)
